TPU v7x, 128 devices: a whole 4x4x4 slice. The times are simulated.
128 devices in a mesh: pw: 64 (over z, y, x), mm: 2 (over core).
Axes of the slice: x: 4, y: 4, z: 4, core: 2. Of those that a mesh axis runs over, the one named last changes fastest.
Arguments:
- coefficients: float32 [2, 2, 28672, 384], P(None, 'mm', 'pw'), may hold values from -0.0009765625 to 0.0009765625
- col_map: int32 [28672], replicated, may hold values from 0 to 147456, as said below
- charge_cell: int32 [3, 512], replicated, may hold values from 0 to 383
- charge_frac: float32 [3, 512], replicated, may hold values from 0.05 to 0.95
- charge: float32 [512], replicated, may hold values from -1.5 to 1.5
- tile_list: int32 [128, 16], P(('pw', 'mm')), may hold values from 0 to 511, as said below
Outputs:
- field_orbital: float32 [2, 2, 64, 384, 384], P(None, 'mm', 'pw')
- forces: float32 [3, 512], replicated
Inputs may be any that keep to these rules, and one draw needn't show every extreme that they name: Block d of col_map, its 448 entries from d * 448, belongs to pw index d. In each block the live entries, grid columns gb * 384 + gc below 147456, come first and the rest equal 147456; live entries are distinct over all blocks, 14336 in all; blocks d and d plus half the number of blocks together hold exactly 448 live entries; some block is full in every draw. `tile_list`: each row holds 16 distinct charge numbers.
All inputs are finite; a program needn't handle non-finite values.
Results may differ from a plain program's by a relative error of at most 0.0003.
Values sent between devices are 32-bit elements; how exact they have to be, the bound alone decides.
No kernel may reach another device: no remote copies, remote signals or barrier semaphores. Data moves between devices by JAX's collectives and lax.ppermute only.
A program may use at most 192 MiB of HBM per device.

v0:
```python
import math

import jax
import jax.numpy as jnp
from jax import lax
from jax.sharding import PartitionSpec as P

NP = 1


spacing = 0.25
soften_sq = 0.09
damping = 1.0
volume = spacing * spacing * spacing
peak_slope = 2.0 / (math.sqrt(math.pi) * damping)
highest = lax.Precision.HIGHEST


def tile_field(density, start_a, start_b, grid_len, neighbor_row, charge_cell, charge_frac, charge):
    plane_count, row_count, line_count = density.shape
    coord_a = (start_a + jnp.arange(plane_count)).astype(density.dtype)
    coord_b = (start_b + jnp.arange(row_count)).astype(density.dtype)
    coord_c = jnp.arange(line_count).astype(density.dtype)
    half_len = grid_len / 2.0

    def wrap_offset(coord, center):
        return spacing * (jnp.mod(coord - center + half_len, grid_len) - half_len)

    def visit(total, index):
        center = charge_cell[:, index].astype(density.dtype) + charge_frac[:, index]
        off_a = wrap_offset(coord_a, center[0])
        off_b = wrap_offset(coord_b, center[1])
        off_c = wrap_offset(coord_c, center[2])
        dist_sq = (
            off_a[:, None, None] ** 2
            + off_b[None, :, None] ** 2
            + off_c[None, None, :] ** 2
            + soften_sq
        )
        radius = jnp.sqrt(dist_sq)
        ratio = lax.erf(radius / damping)
        kernel = ratio / radius
        slope = (peak_slope * jnp.exp(-dist_sq / (damping * damping)) * radius - ratio) / dist_sq
        weight = density * slope / radius
        push_a = jnp.sum(jnp.sum(weight, axis=(1, 2)) * off_a)
        push_b = jnp.sum(jnp.sum(weight, axis=(0, 2)) * off_b)
        push_c = jnp.sum(jnp.sum(weight, axis=(0, 1)) * off_c)
        strength = charge[index]
        return (total + strength * kernel, strength * volume * jnp.stack([push_a, push_b, push_c]))

    potential, pushes = lax.scan(visit, jnp.zeros(density.shape, density.dtype), neighbor_row)
    return (potential, jnp.transpose(pushes))


def dft_tables(length):
    index = jnp.arange(length, dtype=jnp.int32)
    product = index[:, None] * index[None, :] % length
    angle = 2.0 * math.pi / length * product.astype(jnp.float32)
    return (jnp.cos(angle), jnp.sin(angle))


def local(coefficients, col_map, charge_cell, charge_frac, charge, tile_list):
    grid_len = coefficients.shape[-1]
    empty_mark = grid_len * grid_len
    pw_count = lax.axis_size("pw")
    pw_index = lax.axis_index("pw")
    mm_index = lax.axis_index("mm")
    plane_total = NP * pw_count
    real_cols = coefficients[0, 0]
    imag_cols = coefficients[1, 0]
    cos_table, sin_table = dft_tables(grid_len)
    cos_slab = cos_table[:, :plane_total]
    sin_slab = sin_table[:, :plane_total]

    def along_first(table, columns):
        return jnp.einsum("gz,sg->zs", table, columns, precision=highest)

    column_real = along_first(cos_slab, real_cols) - along_first(sin_slab, imag_cols)
    column_imag = along_first(sin_slab, real_cols) + along_first(cos_slab, imag_cols)
    regrouped = lax.all_to_all(
        jnp.stack([column_real, column_imag]), "pw", split_axis=1, concat_axis=2, tiled=True
    )
    plane_count = regrouped.shape[1]
    planes = (
        jnp.zeros((2, plane_count, empty_mark), jnp.float32)
        .at[:, :, col_map]
        .set(regrouped, mode="drop")
    )
    planes = planes.reshape(2, plane_count, grid_len, grid_len)

    def along_last(table, values):
        return jnp.einsum("pbg,gc->pbc", values, table, precision=highest)

    def along_middle(table, values):
        return jnp.einsum("pgc,gb->pbc", values, table, precision=highest)

    pass_real = along_last(cos_table, planes[0]) - along_last(sin_table, planes[1])
    pass_imag = along_last(sin_table, planes[0]) + along_last(cos_table, planes[1])
    psi_real = along_middle(cos_table, pass_real) - along_middle(sin_table, pass_imag)
    psi_imag = along_middle(sin_table, pass_real) + along_middle(cos_table, pass_imag)
    partial_density = psi_real * psi_real + psi_imag * psi_imag
    density = lax.psum_scatter(partial_density, "mm", scatter_dimension=1, tiled=True)
    row_count = density.shape[1]
    neighbor_row = tile_list[0]
    potential, pushes = tile_field(
        density,
        pw_index * plane_count,
        mm_index * row_count,
        grid_len,
        neighbor_row,
        charge_cell,
        charge_frac,
        charge,
    )
    member = (neighbor_row[:, None] == jnp.arange(charge.shape[0])[None, :]).astype(jnp.float32)
    force_terms = jnp.dot(pushes, member, precision=highest)
    forces = lax.psum(force_terms, ("pw", "mm"))
    piece = lax.all_gather(potential, "mm", axis=1, tiled=True)
    applied = jnp.stack([piece * psi_real, piece * psi_imag])
    return (applied[:, None], forces)


def solution(mesh):
    placed = (P(None, "mm", "pw", None), P(), P(), P(), P(), P(("pw", "mm"), None))
    return jax.shard_map(
        local,
        mesh=mesh,
        in_specs=placed,
        out_specs=(P(None, "mm", "pw", None, None), P()),
        check_vma=False,
    )
```

profile of v0, /device:TPU:0, one launch (start us, length us, event | category | flops | bytes accessed | tf_op | source)
XLA Modules:
  0.0 752.8 jit_solution(7444131278347468729)
XLA Ops:
  7.2 2.2 fusion.41
  9.4 2.2 fusion.42
  11.6 2.0 fusion.27
  13.6 2.0 fusion.29
  15.5 2.0 fusion.23
  17.5 2.0 fusion.24
  20.4 11.5 %all-to-all-start = ((f32[2,64,448]{2,0,1:T(2,128)}), f32[2,64,448]{2,0,1:T(2,128)S(1)}, u32[]{:S(2)}, u32[]{:S(2)}) async-start(f32[2,64,448]{2,0,1:T(2,128)} %copy.14), calls=%async_computation | async-start | bytes 524288 | tf_op jit(solution)/shard_map/all_to_all | solution.py:80
  33.4 10.5 %sort = (s32[28672]{0:T(1024)S(1)}, s32[28672]{0:T(1024)S(1)}) sort(s32[28672]{0:T(1024)S(1)} %compare_select_fusion, s32[28672]{0:T(1024)S(1)} %iota.27), dimensions={0}, to_apply=%compare | sort | flops 430080 | bytes 458752 | tf_op jit(solution)/shard_map/scatter | solution.py:87
  44.2 8.5 %copy.16 = f32[28672,2]{1,0:T(8,128)} copy(f32[28672,2]{0,1:T(2,128)S(1)} %bitcast.74) | data formatting | bytes 458752 | tf_op jit(solution)/shard_map/all_to_all | solution.py:80
  52.7 265.9 %scatter_custom_fusion = f32[2,147456]{0,1:T(8,128)} fusion(s32[28672]{0:T(1024)S(1)} %get-tuple-element.225, f32[]{:T(128)} %constant.139.clone.1, f32[28672,2]{1,0:T(8,128)} %copy.16, s32[28672]{0:T(1024)S(1)} %broadcast_clamp_fusion), kind=kCustom, calls=%fused_computation.33 | custom fusion | bytes 1180160 | tf_op jit(solution)/shard_map/scatter | solution.py:87
  318.7 73.7 %slice_reduce_fusion = (f32[147456]{0:T(1024)S(1)}, f32[147456]{0:T(1024)S(1)}) fusion(f32[2,147456]{0,1:T(8,128)} %scatter_custom_fusion), kind=kLoop, calls=%fused_computation.31 | loop fusion | bytes 2359296 | tf_op jit(solution)/shard_map/slice | solution.py:97
  392.5 3.5 fusion.53
  396.0 3.5 fusion.48
  399.6 3.5 convolution_subtract_fusion.1
  403.2 4.3 fusion.46
  407.4 4.1 fusion.50
  411.5 3.5 convolution_add_fusion.1
  415.0 4.1 convolution_subtract_fusion
  419.2 4.1 convolution_add_fusion
  424.2 11.9 %reduce-scatter.2.cloned.1.call-done = f32[1,192,384]{2,1,0:T(8,128)} async-done(((f32[1,384,384]{2,1,0:T(8,128)}), f32[1,192,384]{2,1,0:T(8,128)}) %reduce-scatter.2.cloned.1.call-update) | async-done | bytes 294928 | tf_op jit(solution)/shard_map/reduce_scatter | solution.py:102
  436.1 238.7 %while.16 = (s32[]{:T(128)}, f32[1,192,384]{2,1,0:T(8,128)S(1)}, f32[16,3]{0,1:T(4,128)S(1)}, s32[16]{0:T(128)S(1)}, f32[512]{0:T(512)}, /*index=5*/s32[3,512]{1...) while((s32[]{:T(128)}, f32[1,192,384]{2,1,0:T(8,128)S(1)}, ...), condition=%wide.region_8.9_spmd.clone, body=%wide.region_2.8_spmd.clone.sunk | while | flops 1194080 | bytes 1484343 | solution.py:51
  443.3 1.9 multiply_divide_fusion.2
  458.1 1.9 multiply_divide_fusion.2
  473.1 1.9 multiply_divide_fusion.2
  488.0 1.9 multiply_divide_fusion.2
  502.9 1.9 multiply_divide_fusion.2
  517.9 1.9 multiply_divide_fusion.2
  547.7 1.9 multiply_divide_fusion.2
  562.6 1.9 multiply_divide_fusion.2
  577.6 1.9 multiply_divide_fusion.2
  674.8 2.2 all_gather.3
  677.4 67.3 %psum.7 = f32[3,512]{1,0:T(4,128)} all-reduce(f32[3,512]{1,0:T(4,128)S(1)} %fusion.60), channel_id=1, replica_groups=mesh['pw'=64,'mm'=2] {'pw','mm'}, use_global_device_ids=true, to_apply=%region_9.10 | all-reduce | flops 1536 | bytes 12288 | tf_op jit(solution)/shard_map/psum | solution.py:117
  (203 shorter events, 163.5 us)
Async XLA Ops:
  20.4 23.5 %all-to-all-start = ((f32[2,64,448]{2,0,1:T(2,128)}), f32[2,64,448]{2,0,1:T(2,128)S(1)}, u32[]{:S(2)}, u32[]{:S(2)}) async-start(f32[2,64,448]{2,0,1:T(2,128)} %copy.14), calls=%async_computation | async-start | bytes 524288 | tf_op jit(solution)/shard_map/all_to_all | solution.py:80
  31.9 404.2 %reduce-scatter.2.cloned.1.call-start = ((), (), s32[]{:S(2)}) async-start(), calls=%async_computation.2 | async-start | bytes 884736 | tf_op jit(solution)/shard_map/reduce_scatter | solution.py:102
  392.4 43.7 %copy-start = (s32[1,16]{1,0:T(1,128)S(1)}, s32[1,16]{1,0:T(1,128)}, u32[]{:S(2)}) copy-start(s32[1,16]{1,0:T(1,128)} %param.13) | copy-start | bytes 196
Sparse Core Ops, SparseCore 0:
  424.3 11.7 reduce-scatter.1
where the time goes:
time: 765 us; the launch traced here: 753 us
  local copies, waits for them, and re-layouts  391 us (51%)
  other arithmetic  152 us (20%)
  blocking collectives  69.5 us (9%)
  loops' own time  63.3 us (8%)
  matrix products  38.5 us (5%)
  between operations  14.4 us (2%)
  starting transfers between devices  12 us (2%)
  waiting for transfers between devices  11.9 us (2%)
    scatter x2, local copies, waits for them, and re-layouts, local(): planes = jnp.zeros((2, plane_count, empty_mark), jnp.float32).at[:, :, co...  266 us
    slice x1, local copies, waits for them, and re-layouts, local(): planes[1]  73.7 us
    psum x1, blocking collectives, local(): forces = lax.psum(force_terms, ('pw', 'mm'))  67.3 us
    another operation x1, loops' own time, tile_field(): lax.scan(visit, jnp.zeros(density.shape, density.dtype), neighbor_row)  63.3 us
    div x16, other arithmetic, visit(): weight = density * slope / radius  30.6 us
    reduce_sum x16, other arithmetic, visit(): push_c = jnp.sum(jnp.sum(weight, axis=(0, 1)) * off_c)  20.9 us
    dynamic_slice x16, local copies, waits for them, and re-layouts, visit(): strength = charge[index]  20.3 us
    reduce_sum x16, other arithmetic, visit(): push_b = jnp.sum(jnp.sum(weight, axis=(0, 2)) * off_b)  19.3 us
  transfers between devices with their start and end apart: 2, of which 1 were waited for; matrix products, arithmetic and copies ran while one was open for 2% of the time, Pallas kernels for 0%

commit v1 on v0

v1 whole, which is shorter than its diff:
```python
import functools
import math

import jax
import jax.numpy as jnp
import ml_dtypes
import numpy as np
from jax import lax
from jax.experimental import pallas as pl
from jax.experimental.pallas import tpu as pltpu
from jax.sharding import PartitionSpec as P

f32, bf16, i32 = jnp.float32, jnp.bfloat16, jnp.int32
N = 384
HALF = 192
LANE = 128
SPACING = 0.25
SOFTEN = 0.09
VOLUME = SPACING**3
PEAK = 2.0 / math.sqrt(math.pi)
EMPTY = N * N
TILE_CHUNKS = 8
NT = (((1,), (1,)), ((), ()))
VMEM_LIMIT = 60 * 1024 * 1024


def split_table(table):
    high = table.astype(np.float32).astype(ml_dtypes.bfloat16)
    low = (table - high.astype(np.float64)).astype(np.float32).astype(ml_dtypes.bfloat16)
    return high, low


def tables(planes):
    index = np.arange(N, dtype=np.int64)
    angle = 2.0 * np.pi / N * ((index[:, None] * index[None, :]) % N).astype(np.float64)
    cos, sin = np.cos(angle), np.sin(angle)
    cz, sz = cos[:planes], sin[:planes]
    first = np.block([[cz, -sz], [sz, cz]])
    first_high, first_low = split_table(first)
    cos_high, cos_low = split_table(cos)
    sin_high, sin_low = split_table(sin)
    return (
        np.concatenate([first_high, first_low], axis=0),
        np.concatenate([cos_high, sin_high, cos_low, sin_low], axis=0),
    )


def mm(a, b, dims=(((1,), (0,)), ((), ()))):
    return lax.dot_general(a, b, dims, preferred_element_type=f32)


def halves(value):
    high = value.astype(bf16)
    low = (value - high.astype(f32)).astype(bf16)
    return high, low


def columns_kernel(coef_ref, table_ref, out_ref, high_ref, low_ref):
    slots = coef_ref.shape[1]
    pad = high_ref.shape[0] - slots
    planes = out_ref.shape[0]
    for part in range(2):
        high, low = halves(coef_ref[part])
        high_ref[:slots, part * N : (part + 1) * N] = high
        low_ref[:slots, part * N : (part + 1) * N] = low
    high_ref[slots:, :] = jnp.zeros((pad, 2 * N), bf16)
    low_ref[slots:, :] = jnp.zeros((pad, 2 * N), bf16)
    rows = 2 * planes
    both = mm(table_ref[...], high_ref[...], NT)
    result = both[:rows] + both[rows:] + mm(table_ref[:rows], low_ref[...], NT)
    for part in range(2):
        for piece in range(4):
            out_ref[:, 4 * part + piece, :] = result[
                part * planes : (part + 1) * planes, piece * LANE : (piece + 1) * LANE
            ]


def wrap(offset):
    shifted = offset + HALF
    shifted = jnp.where(shifted < 0, shifted + N, shifted)
    shifted = jnp.where(shifted >= N, shifted - N, shifted)
    return SPACING * (shifted - HALF)


ERF_NUM = (
    -2.72614225801306e-10,
    2.77068142495902e-08,
    -2.10102402082508e-06,
    -5.69250639462346e-05,
    -7.34990630326855e-04,
    -2.95459980854025e-03,
    -1.60960333262415e-02,
)
ERF_DEN = (
    -1.45660718464996e-05,
    -2.13374055278905e-04,
    -1.68282697438203e-03,
    -7.37332916720468e-03,
    -1.42647390514189e-02,
)


def erf(s):
    s = jnp.minimum(s, 4.0)
    sq = s * s
    num = jnp.full_like(s, ERF_NUM[0])
    for c in ERF_NUM[1:]:
        num = num * sq + c
    den = jnp.full_like(s, ERF_DEN[0])
    for c in ERF_DEN[1:]:
        den = den * sq + c
    return s * num / den


def charges_kernel(
    list_s,
    cell_s,
    frac_s,
    plane_s,
    live_s,
    list_ref,
    cell_ref,
    frac_ref,
    charge_ref,
    gc_ref,
    pot_ref,
    slope_ref,
    offb_ref,
    offc_ref,
    col_ref,
    order_s,
    count_s,
    uab_ref,
    eab_ref,
    uc_ref,
    ec_ref,
):
    chunks = live_s.shape[0]

    def note(i, c):
        order_s[c] = i
        return c + live_s[i]

    count = lax.fori_loop(0, chunks, note, jnp.int32(0))
    for j in range(TILE_CHUNKS):
        order_s[count + j] = jnp.int32(chunks)
    count_s[0] = count
    gc = gc_ref[...]
    for pair in range(3):
        inside = (gc >= pair * LANE) & (gc < (pair + 1) * LANE)
        count_s[1 + pair] = jnp.max(jnp.where(inside, 1.0, 0.0)).astype(i32)

    listed = list_ref[...]
    mask = lax.broadcasted_iota(i32, (LANE, cell_ref.shape[1]), 1) == listed
    center = cell_ref[...].astype(f32) + frac_ref[...]

    def pick(row):
        return jnp.sum(jnp.where(mask, row, 0.0), axis=1, keepdims=True)

    ca, cb, cc = (pick(center[i : i + 1]) for i in range(3))
    strength = pick(charge_ref[...])
    plane = plane_s[0].astype(f32)
    off_a = wrap(plane - ca)
    col_ref[...] = jnp.concatenate(
        [off_a, strength, listed.astype(f32)] + [jnp.zeros((LANE, 5), f32)], axis=1
    )
    off_c = wrap(lax.broadcasted_iota(i32, (32, N), 1).astype(f32) - cc[:32])
    offc_ref[...] = off_c
    sq_c = off_c * off_c
    uc_ref[...] = sq_c
    ec_ref[...] = jnp.exp(-sq_c)

    def across(column):
        return jnp.transpose(jnp.broadcast_to(column, (LANE, LANE)))[:1]

    off_b = wrap(lax.broadcasted_iota(i32, (N, LANE), 0).astype(f32) - across(cb))
    offb_ref[...] = off_b
    row_a = across(off_a)
    uab = off_b * off_b + (row_a * row_a + SOFTEN)
    uab_ref[...] = uab
    eab_ref[...] = PEAK * jnp.exp(-uab)
    pot_ref[...] = jnp.zeros((N, N), f32)

    for q in range(32):
        base = (q // 16) * HALF
        ucq = jnp.broadcast_to(uc_ref[q : q + 1, :], (8, N))
        ecq = jnp.broadcast_to(ec_ref[q : q + 1, :], (8, N))
        own = list_s[q]
        power = jnp.broadcast_to(strength[q : q + 1, :], (8, N))

        def far(i, _, q=q, base=base, ucq=ucq, ecq=ecq, power=power):
            r = pl.multiple_of(base + 8 * i, 8)
            u = uab_ref[pl.ds(r, 8), q : q + 1] + ucq
            k = lax.rsqrt(u)
            e = eab_ref[pl.ds(r, 8), q : q + 1] * ecq
            slope_ref[q, pl.ds(pl.multiple_of(8 * i, 8), 8), :] = k * k * (e - k)
            pot_ref[pl.ds(r, 8), :] += power * k
            return 0

        lax.fori_loop(0, HALF // 8, far, 0, unroll=4)
        da = wrap(plane - (cell_s[0, own].astype(f32) + frac_s[0, own]))
        sb = cell_s[1, own].astype(f32) + frac_s[1, own]

        @pl.when(da * da < 16.0)
        def _(q=q, base=base, ucq=ucq, ecq=ecq, power=power, da=da, sb=sb):
            def near(i, _):
                r = pl.multiple_of(base + 8 * i, 8)
                db = jnp.abs(wrap(r.astype(f32) + 3.5 - sb))
                db = jnp.maximum(db - 3.5 * SPACING, 0.0)

                @pl.when(da * da + db * db < 16.0)
                def _():
                    u = uab_ref[pl.ds(r, 8), q : q + 1] + ucq
                    k = lax.rsqrt(u)
                    e = eab_ref[pl.ds(r, 8), q : q + 1] * ecq
                    full = erf(u * k) * k
                    slope_ref[q, pl.ds(pl.multiple_of(8 * i, 8), 8), :] = k * k * (e - full)
                    pot_ref[pl.ds(r, 8), :] += power * (full - k)

                return 0

            lax.fori_loop(0, HALF // 8, near, 0)


def grid_kernel(
    order_s,
    count_s,
    recv_ref,
    gb_ref,
    gc_ref,
    table_ref,
    pot_ref,
    slope_ref,
    offb_ref,
    offc_ref,
    col_ref,
    field_ref,
    push_ref,
    acc_ref,
    hot_ref,
    val_ref,
    tab_ref,
    flow_ref,
    mid_ref,
    dens_ref,
    sum_ref,
):
    sources = recv_ref.shape[0]
    width = TILE_CHUNKS * LANE
    acc_ref[...] = jnp.zeros(acc_ref.shape, f32)
    iota_b = lax.broadcasted_iota(i32, (N, LANE), 0)
    iota_c = lax.broadcasted_iota(i32, (LANE, LANE), 0)

    def tile(t, _):
        where = []
        for j in range(TILE_CHUNKS):
            index = order_s[t * TILE_CHUNKS + j]
            where.append(index)
            hot = iota_b == gb_ref[pl.ds(index, 1), :]
            hot_ref[:, j * LANE : (j + 1) * LANE] = jnp.where(hot, 1.0, 0.0).astype(bf16)
        for pair in range(3):

            @pl.when(count_s[1 + pair] > 0)
            def _(pair=pair):
                for j, index in enumerate(where):
                    source = jnp.minimum(index >> 2, sources - 1)
                    piece = index & 3
                    hot = (iota_c + pair * LANE) == gc_ref[pl.ds(index, 1), :]
                    cut = slice(j * LANE, (j + 1) * LANE)
                    for part in range(2):
                        value = recv_ref[source, pl.ds(4 * part + piece, 1), :]
                        high = value.astype(bf16).astype(f32)
                        low = value - high
                        for k, v in ((part, high), (2 + part, low)):
                            val_ref[k * LANE : (k + 1) * LANE, cut] = jnp.where(
                                hot, v, 0.0
                            ).astype(bf16)
                acc_ref[pair] += mm(hot_ref[...], val_ref[...], NT)

        return 0

    tiles = (count_s[0] + TILE_CHUNKS - 1) // TILE_CHUNKS
    lax.fori_loop(0, tiles, tile, 0)

    for level in range(2):
        cos = table_ref[2 * level * N : (2 * level + 1) * N, :]
        sin = table_ref[(2 * level + 1) * N : (2 * level + 2) * N, :]
        for pair in range(3):
            cut = slice(pair * LANE, (pair + 1) * LANE)
            top = slice(2 * pair * LANE, (2 * pair + 1) * LANE)
            bottom = slice((2 * pair + 1) * LANE, (2 * pair + 2) * LANE)
            tab_ref[level, top, :N] = cos[cut]
            tab_ref[level, top, N:] = sin[cut]
            tab_ref[level, bottom, :N] = -sin[cut]
            tab_ref[level, bottom, N:] = cos[cut]
    for pair in range(3):
        cut = slice(2 * pair * LANE, 2 * (pair + 1) * LANE)
        flow_ref[:N, cut] = acc_ref[pair, :, : 2 * LANE].astype(bf16)
        flow_ref[N:, cut] = acc_ref[pair, :, 2 * LANE :].astype(bf16)
    both = mm(flow_ref[...], tab_ref[0])
    passed = both[:N] + both[N:] + mm(flow_ref[:N], tab_ref[1])
    high, low = halves(passed)
    mid_ref[...] = mm(table_ref[: 2 * N], high) + (
        mm(table_ref[2 * N :], high) + mm(table_ref[: 2 * N], low)
    )

    def finish(i, _):
        r = pl.ds(pl.multiple_of(8 * i, 8), 8)
        s = pl.ds(pl.multiple_of(N + 8 * i, 8), 8)
        real = mid_ref[r, :N] - mid_ref[s, N:]
        imag = mid_ref[s, :N] + mid_ref[r, N:]
        dens_ref[r, :] = real * real + imag * imag
        pot = pot_ref[r, :]
        field_ref[0, r, :] = pot * real
        field_ref[1, r, :] = pot * imag
        return 0

    lax.fori_loop(0, N // 8, finish, 0, unroll=4)

    for q in range(32):
        base = (q // 16) * HALF

        def gather(i, carry, q=q, base=base):
            plain, scaled = carry
            r = pl.ds(pl.multiple_of(base + 8 * i, 8), 8)
            w = dens_ref[r, :] * slope_ref[q, pl.ds(pl.multiple_of(8 * i, 8), 8), :]
            return plain + w, scaled + w * offb_ref[r, q : q + 1]

        zero = jnp.zeros((8, N), f32)
        plain, scaled = lax.fori_loop(0, HALF // 8, gather, (zero, zero), unroll=4)
        sum_ref[q : q + 1, :] = jnp.sum(plain, axis=0, keepdims=True)
        sum_ref[32 + q : 33 + q, :] = jnp.sum(scaled, axis=0, keepdims=True)
    plain = sum_ref[:32, :]
    off_a = col_ref[:32, 0:1]
    scale = col_ref[:32, 1:2] * VOLUME
    push_a = off_a * jnp.sum(plain, axis=1, keepdims=True) * scale
    push_b = jnp.sum(sum_ref[32:, :], axis=1, keepdims=True) * scale
    push_c = jnp.sum(plain * offc_ref[...], axis=1, keepdims=True) * scale
    packed = jnp.concatenate([push_a, push_b, push_c, 0.5 * col_ref[:32, 2:3]], axis=0)
    turned = jnp.transpose(jnp.broadcast_to(packed, (LANE, LANE)))
    push_ref[...] = turned[:8]


def spread_kernel(terms_ref, out_ref):
    terms = terms_ref[...]
    charges = out_ref.shape[1]
    lane = lax.broadcasted_iota(i32, (terms.shape[0], charges), 1).astype(f32)
    totals = [jnp.zeros((terms.shape[0], charges), f32)] * 3
    for q in range(32):
        hot = terms[:, 96 + q : 97 + q] == lane
        for axis in range(3):
            value = terms[:, 32 * axis + q : 32 * axis + q + 1]
            totals[axis] = totals[axis] + jnp.where(hot, value, 0.0)
    for axis in range(3):
        out_ref[axis : axis + 1, :] = jnp.sum(totals[axis], axis=0, keepdims=True)


def vmem(count):
    return [pl.BlockSpec(memory_space=pltpu.VMEM)] * count


def smem(count):
    return [pl.BlockSpec(memory_space=pltpu.SMEM)] * count


def params():
    return pltpu.CompilerParams(vmem_limit_bytes=VMEM_LIMIT)


def local(coefficients, col_map, charge_cell, charge_frac, charge, tile_list):
    slots = coefficients.shape[2]
    sources = lax.axis_size("pw")
    planes = sources
    plane = lax.axis_index("pw").astype(i32)
    first_table, second_table = tables(planes)
    chunks = 4 * sources

    own = tile_list[0]
    other = lax.ppermute(own, "mm", [(0, 1), (1, 0)])
    first = lax.axis_index("mm") == 0
    listed = jnp.concatenate([jnp.where(first, own, other), jnp.where(first, other, own)])
    listed_col = jnp.pad(listed, (0, LANE - 32), constant_values=-1)[:, None]

    sent = pl.pallas_call(
        columns_kernel,
        out_shape=jax.ShapeDtypeStruct((planes, 8, LANE), f32),
        in_specs=vmem(2),
        out_specs=vmem(1)[0],
        scratch_shapes=[pltpu.VMEM((4 * LANE, 2 * N), bf16)] * 2,
        compiler_params=params(),
        name="columns",
    )(coefficients.reshape(2, slots, N), jnp.asarray(first_table))
    recv = lax.all_to_all(sent, "pw", 0, 0, tiled=True)

    grid = jnp.pad(
        col_map.reshape(sources, slots), ((0, 2), (0, 4 * LANE - slots)), constant_values=EMPTY
    ).reshape(chunks + 8, LANE)
    live = grid < EMPTY
    gb = jnp.where(live, grid // N, -1000)
    gc = jnp.where(live, grid % N, -1000)
    live_chunk = live[:chunks, 0].astype(i32)

    pot, slope, offb, offc, col, order, count = pl.pallas_call(
        charges_kernel,
        out_shape=(
            jax.ShapeDtypeStruct((N, N), f32),
            jax.ShapeDtypeStruct((32, HALF, N), f32),
            jax.ShapeDtypeStruct((N, LANE), f32),
            jax.ShapeDtypeStruct((32, N), f32),
            jax.ShapeDtypeStruct((LANE, 8), f32),
            jax.ShapeDtypeStruct((chunks + TILE_CHUNKS,), i32),
            jax.ShapeDtypeStruct((4,), i32),
        ),
        in_specs=smem(5) + vmem(5),
        out_specs=tuple(vmem(5) + smem(2)),
        scratch_shapes=[
            pltpu.VMEM((N, LANE), f32),
            pltpu.VMEM((N, LANE), f32),
            pltpu.VMEM((32, N), f32),
            pltpu.VMEM((32, N), f32),
        ],
        compiler_params=params(),
        name="charges",
    )(
        listed,
        charge_cell,
        charge_frac,
        plane[None],
        live_chunk,
        listed_col,
        charge_cell,
        charge_frac,
        charge[None],
        gc,
    )

    field, push = pl.pallas_call(
        grid_kernel,
        out_shape=(
            jax.ShapeDtypeStruct((2, N, N), f32),
            jax.ShapeDtypeStruct((8, LANE), f32),
        ),
        in_specs=smem(2) + vmem(9),
        out_specs=tuple(vmem(2)),
        scratch_shapes=[
            pltpu.VMEM((3, N, 4 * LANE), f32),
            pltpu.VMEM((N, TILE_CHUNKS * LANE), bf16),
            pltpu.VMEM((4 * LANE, TILE_CHUNKS * LANE), bf16),
            pltpu.VMEM((2, 2 * N, 2 * N), bf16),
            pltpu.VMEM((2 * N, 2 * N), bf16),
            pltpu.VMEM((2 * N, 2 * N), f32),
            pltpu.VMEM((N, N), f32),
            pltpu.VMEM((64, N), f32),
        ],
        compiler_params=params(),
        name="grid",
    )(order, count, recv, gb, gc, jnp.asarray(second_table), pot, slope, offb, offc, col)

    push = push[:1]
    push = push + lax.ppermute(push, "mm", [(0, 1), (1, 0)])
    terms = lax.all_to_all(
        jnp.broadcast_to(push[None], (sources, 1, LANE)), "pw", 0, 0, tiled=True
    ).reshape(sources, LANE)
    forces = pl.pallas_call(
        spread_kernel,
        out_shape=jax.ShapeDtypeStruct((3, charge.shape[0]), f32),
        in_specs=vmem(1),
        out_specs=vmem(1)[0],
        compiler_params=params(),
        name="spread",
    )(terms)
    return (field[:, None, None], forces)


def solution(mesh):
    placed = (P(None, "mm", "pw", None), P(), P(), P(), P(), P(("pw", "mm"), None))
    return jax.shard_map(
        local,
        mesh=mesh,
        in_specs=placed,
        out_specs=(P(None, "mm", "pw", None, None), P()),
        check_vma=False,
    )
```

time: 765 us -> 127 us (0.17); the launches traced: 753 us -> 126 us
  local copies, waits for them, and re-layouts: 391 us -> 2.39 us
  other arithmetic: 152 us -> 2.37 us
  Pallas kernels: 0 us -> 87.5 us
  loops' own time: 63.3 us -> 0 us
  blocking collectives: 69.5 us -> 20.3 us
  matrix products: 38.5 us -> 0 us
  between operations: 14.4 us -> 0.75 us
  waiting for transfers between devices: 11.9 us -> 0.94 us
    scatter x2 -> x0, local copies, waits for them, and re-layouts: 266 us -> none  [local(): planes = jnp.zeros((2, plane_count, empty_mark), jnp.float32).at[:, :, co...]
    pallas_call x0 -> x4, Pallas kernels: none -> 87.5 us  [the longest x1 54.9 us: local(): pl.pallas_call(grid_kernel, out_shape=(jax.ShapeDtypeStruct((2, N, N), f3...]
    slice x17 -> x1, local copies, waits for them, and re-layouts: 83.3 us -> 0.69 us  [local(): push = push[:1]]
    psum x1 -> x0, blocking collectives: 67.3 us -> none  [local(): forces = lax.psum(force_terms, ('pw', 'mm'))]
    another operation x1 -> x0, loops' own time: 63.3 us -> none  [tile_field(): lax.scan(visit, jnp.zeros(density.shape, density.dtype), neighbor_row)]
    reduce_sum x48 -> x0, other arithmetic: 51.6 us -> none  [the longest x16 20.9 us: visit(): push_c = jnp.sum(jnp.sum(weight, axis=(0, 1)) * off_c)]
    dot_general x13 -> x0, matrix products: 38.5 us -> none  [the longest x4 16.6 us: along_middle(): return jnp.einsum('pgc,gb->pbc', values, table, precision=highest)]
    div x16 -> x1, other arithmetic: 30.6 us -> 0.06 us  [local(): gb = jnp.where(live, grid // N, -1000)]
  transfers between devices with their start and end apart: 2 -> 3, of which waited for: 1 -> 1; matrix products, arithmetic and copies ran while one was open for 2% -> 2% of each run, Pallas kernels for 0% -> 23%
where the time goes in v1:
time: 127 us; the launch traced here: 126 us
  Pallas kernels  87.5 us (69%)
  blocking collectives  20.3 us (16%)
  starting transfers between devices  12 us (9%)
  local copies, waits for them, and re-layouts  2.39 us (2%)
  other arithmetic  2.37 us (2%)
    pallas_call x1, Pallas kernels, local(): pl.pallas_call(grid_kernel, out_shape=(jax.ShapeDtypeStruct((2, N, N), f3...  54.9 us
    pallas_call x1, Pallas kernels, local(): pl.pallas_call(charges_kernel, out_shape=(jax.ShapeDtypeStruct((N, N), f3...  26.8 us
    all_to_all x1, blocking collectives, local(): lax.all_to_all(jnp.broadcast_to(push[None], (sources, 1, LANE)), 'pw', 0,...  20.3 us
    all_to_all x1, starting transfers between devices, local(): recv = lax.all_to_all(sent, 'pw', 0, 0, tiled=True)  11.7 us
    pallas_call x1, Pallas kernels, local(): pl.pallas_call(spread_kernel, out_shape=jax.ShapeDtypeStruct((3, charge.s...  2.99 us
    pallas_call x1, Pallas kernels, local(): pl.pallas_call(columns_kernel, out_shape=jax.ShapeDtypeStruct((planes, 8,...  2.85 us
  transfers between devices with their start and end apart: 3, of which 1 were waited for; matrix products, arithmetic and copies ran while one was open for 2% of the time, Pallas kernels for 23%

profile of v1, /device:TPU:0, one launch (start us, length us, event | category | flops | bytes accessed | tf_op | source)
XLA Modules:
  0.0 126.3 jit_solution(4571174790840989354)
XLA Ops:
  0.6 0.0 copy-start.1
  0.6 0.1 collective-permute-start
  0.7 2.9 %columns.1 = f32[64,8,128]{2,1,0:T(8,128)} custom-call(f32[2,448,384]{2,1,0:T(8,128)} %bitcast.14, bf16[256,768]{1,0:T(8,128)(2,1)} %constant.39.clone.table_ref), custom_call_target="tpu_custom_call" | custom-call | tf_op jit(solution)/shard_map/columns/pallas_call | solution.py:384
  3.6 0.0 copy-start.3
  3.6 11.7 %all-to-all-start = ((f32[64,8,128]{2,1,0:T(8,128)}), f32[64,8,128]{2,1,0:T(8,128)S(1)}, u32[]{:S(2)}, u32[]{:S(2)}) async-start(f32[64,8,128]{2,1,0:T(8,128)} %columns.1), calls=%async_computation | async-start | bytes 524288 | tf_op jit(solution)/shard_map/all_to_all | solution.py:393
  15.3 0.0 copy-done.1
  15.3 0.1 reshape.28
  15.4 0.1 sign_compare_fusion
  15.4 0.1 pad_divide_fusion
  15.5 0.1 ne.26
  15.6 0.1 lt.17
  15.6 0.7 convert_reduce_fusion.live_s
  16.3 0.8 fusion.1
  17.1 0.0 collective-permute-done
  17.1 0.0 copy-done.3
  17.2 0.1 pad_add_fusion.list_s
  17.2 0.0 copy-start.2
  17.2 0.7 copy.14.list_ref
  18.0 0.0 copy-done.2
  18.0 26.8 %charges.1 = (f32[384,384]{1,0:T(8,128)}, f32[32,192,384]{2,1,0:T(8,128)}, f32[384,128]{1,0:T(8,128)}, f32[32,384]{1,0:T(8,128)}, f32[128,8]{1,0:T(8,128)}, /*index=5*/s32[264]{0:T(512)}, s32[4]{0:T(128)}) custom-call(s32[32]{0:T(128)} %copy-done.2, s32[3,512]{1,0:T(4,128)} %cell_ref.1, f32[3,512]{1,0:T(4,128)} %frac_ref.1, s32[1]{0:T(128)} %bitcast.1.plane_s, ...), custom_call_target="tpu_custom_call" | custom-call | tf_op jit(solution)/shard_map/charges/pallas_call | solution.py:403
  44.8 0.0 all-to-all-done.recv_ref
  44.8 0.0 copy-start
  44.8 0.7 copy-done
  45.5 54.9 %grid.1 = (f32[2,384,384]{2,1,0:T(8,128)}, f32[8,128]{1,0:T(8,128)}) custom-call(s32[264]{0:T(512)} %get-tuple-element.11.order_s, s32[4]{0:T(128)} %get-tuple-element.12.count_s, f32[64,8,128]{2,1,0:T(8,128)} %copy-done, s32[264,128]{1,0:T(8,128)} %get-tuple-element.26.gb_ref, s32[264,128]{1,0:T(8,128)} %get-tuple-element.27.gc_ref, ...), custom_call_target="tpu_custom_call" | custom-call | tf_op jit(solution)/shard_map/grid/pallas_call | solution.py:437
  100.4 0.7 slice.7
  101.1 0.2 collective-permute-start.1
  101.3 0.9 collective-permute-done.1
  102.3 0.7 add_bitcast_fusion
  103.0 20.3 %all_to_all.10 = f32[64,1,128]{2,1,0:T(1,128)} all-to-all(f32[64,1,128]{2,1,0:T(1,128)S(1)} %broadcast_in_dim.31), channel_id=1, replica_groups=mesh['pw'=64,'mm'=2] {'pw'}, dimensions={0} | all-to-all | bytes 65536 | tf_op jit(solution)/shard_map/all_to_all | solution.py:461
  123.3 3.0 %spread.1 = f32[3,512]{1,0:T(4,128)} custom-call(f32[64,128]{1,0:T(8,128)} %bitcast.15), custom_call_target="tpu_custom_call" | custom-call | tf_op jit(solution)/shard_map/spread/pallas_call | solution.py:464
  (5 shorter events, 0.1 us)
Async XLA Ops:
  0.6 14.6 %copy-start.1 = (s32[28672]{0:T(1024)S(1)}, s32[28672]{0:T(1024)}, u32[]{:S(2)}) copy-start(s32[28672]{0:T(1024)} %param.9) | copy-start | bytes 344068
  0.6 16.5 %collective-permute-start = (s32[16]{0:T(128)}, s32[16]{0:T(128)S(1)}, u32[]{:S(2)}, u32[]{:S(2)}) collective-permute-start(s32[16]{0:T(128)} %bitcast.17), channel_id=1, source_target_pairs={{0,1},{1,0},{2,3},{3,2},{4,5},{5,4},{6,7},{7,6},{8,9},{9,8},{10,11... | collective-permute-start | bytes 200 | tf_op jit(solution)/shard_map/ppermute | solution.py:379
  3.6 13.6 %copy-start.3 = (s32[1,16]{1,0:T(1,128)S(1)}, s32[1,16]{1,0:T(1,128)}, u32[]{:S(2)}) copy-start(s32[1,16]{1,0:T(1,128)} %param.13) | copy-start | bytes 196
  3.6 41.2 %all-to-all-start = ((f32[64,8,128]{2,1,0:T(8,128)}), f32[64,8,128]{2,1,0:T(8,128)S(1)}, u32[]{:S(2)}, u32[]{:S(2)}) async-start(f32[64,8,128]{2,1,0:T(8,128)} %columns.1), calls=%async_computation | async-start | bytes 524288 | tf_op jit(solution)/shard_map/all_to_all | solution.py:393
  17.2 0.7 copy-start.2
  44.8 0.7 copy-start
  101.1 1.2 collective-permute-start.1

commit v2 on v1

--- a/solution.py
+++ b/solution.py
@@ -19,7 +19,7 @@
 VOLUME = SPACING**3
 PEAK = 2.0 / math.sqrt(math.pi)
 EMPTY = N * N
-TILE_CHUNKS = 8
+TILE_CHUNKS = 4
 NT = (((1,), (1,)), ((), ()))
 VMEM_LIMIT = 60 * 1024 * 1024
 
@@ -122,18 +122,22 @@
     cell_ref,
     frac_ref,
     charge_ref,
-    gc_ref,
+    grid_ref,
     pot_ref,
-    slope_ref,
+    slope_out,
     offb_ref,
     offc_ref,
     col_ref,
+    gb_ref,
+    gc_ref,
     order_s,
-    count_s,
+    plan_s,
     uab_ref,
     eab_ref,
     uc_ref,
     ec_ref,
+    slope_ref,
+    sems,
 ):
     chunks = live_s.shape[0]
 
@@ -141,14 +145,28 @@
         order_s[c] = i
         return c + live_s[i]
 
-    count = lax.fori_loop(0, chunks, note, jnp.int32(0))
-    for j in range(TILE_CHUNKS):
+    count = lax.fori_loop(0, chunks, note, jnp.int32(0), unroll=8)
+    for j in range(4 * TILE_CHUNKS):
         order_s[count + j] = jnp.int32(chunks)
-    count_s[0] = count
-    gc = gc_ref[...]
-    for pair in range(3):
-        inside = (gc >= pair * LANE) & (gc < (pair + 1) * LANE)
-        count_s[1 + pair] = jnp.max(jnp.where(inside, 1.0, 0.0)).astype(i32)
+    plan_s[0] = count
+    cells = grid_ref[...]
+    live = cells < EMPTY
+    row = jnp.floor((cells.astype(f32) + 0.5) * (1.0 / N)).astype(i32)
+    gb = jnp.where(live, row, -1000)
+    gc = jnp.where(live, cells - N * row, -1000)
+    blocks = cells.shape[0]
+    for values, out, start in ((gb, gb_ref, 4), (gc, gc_ref, 8)):
+        for piece in range(4):
+            out[piece, :blocks, :] = values[:, piece * LANE : (piece + 1) * LANE]
+        out[:, blocks:, :] = jnp.full((4, 8, LANE), -1000, i32)
+        found = jnp.int32(0)
+        for band in range(3):
+            inside = (values >= band * LANE) & (values < (band + 1) * LANE)
+            plan_s[start + found] = jnp.int32(band)
+            found = found + jnp.max(jnp.where(inside, 1.0, 0.0)).astype(i32)
+        for slot in range(4):
+            plan_s[start + slot] = jnp.where(slot < found, plan_s[start + slot], 3)
+        plan_s[start // 4] = (found + 1) // 2
 
     listed = list_ref[...]
     mask = lax.broadcasted_iota(i32, (LANE, cell_ref.shape[1]), 1) == listed
@@ -181,23 +199,19 @@
     eab_ref[...] = PEAK * jnp.exp(-uab)
     pot_ref[...] = jnp.zeros((N, N), f32)
 
+    copies = []
     for q in range(32):
         base = (q // 16) * HALF
         ucq = jnp.broadcast_to(uc_ref[q : q + 1, :], (8, N))
         ecq = jnp.broadcast_to(ec_ref[q : q + 1, :], (8, N))
         own = list_s[q]
         power = jnp.broadcast_to(strength[q : q + 1, :], (8, N))
-
-        def far(i, _, q=q, base=base, ucq=ucq, ecq=ecq, power=power):
-            r = pl.multiple_of(base + 8 * i, 8)
-            u = uab_ref[pl.ds(r, 8), q : q + 1] + ucq
-            k = lax.rsqrt(u)
-            e = eab_ref[pl.ds(r, 8), q : q + 1] * ecq
-            slope_ref[q, pl.ds(pl.multiple_of(8 * i, 8), 8), :] = k * k * (e - k)
-            pot_ref[pl.ds(r, 8), :] += power * k
-            return 0
-
-        lax.fori_loop(0, HALF // 8, far, 0, unroll=4)
+        for i in range(HALF // 8):
+            r = slice(base + 8 * i, base + 8 * i + 8)
+            k = lax.rsqrt(uab_ref[r, q : q + 1] + ucq)
+            e = eab_ref[r, q : q + 1] * ecq
+            slope_ref[q, 8 * i : 8 * i + 8, :] = k * k * (e - k)
+            pot_ref[r, :] += power * k
         da = wrap(plane - (cell_s[0, own].astype(f32) + frac_s[0, own]))
         sb = cell_s[1, own].astype(f32) + frac_s[1, own]
 
@@ -221,88 +235,160 @@
 
             lax.fori_loop(0, HALF // 8, near, 0)
 
+        copy = pltpu.make_async_copy(slope_ref.at[q], slope_out.at[q], sems.at[q])
+        copy.start()
+        copies.append(copy)
+    for copy in copies:
+        copy.wait()
+
 
 def grid_kernel(
     order_s,
-    count_s,
+    plan_s,
     recv_ref,
     gb_ref,
     gc_ref,
+    table_in,
+    pot_in,
+    slope_in,
+    offb_ref,
+    offc_ref,
+    col_ref,
+    field_out,
+    push_ref,
+    acc_ref,
+    val_a,
+    val_b,
+    hot_a,
+    hot_b,
+    tab_ref,
+    flow_ref,
+    edge_ref,
+    pass_ref,
+    mid_ref,
+    dens_ref,
+    sum_ref,
+    field_ref,
     table_ref,
     pot_ref,
     slope_ref,
-    offb_ref,
-    offc_ref,
-    col_ref,
-    field_ref,
-    push_ref,
-    acc_ref,
-    hot_ref,
-    val_ref,
-    tab_ref,
-    flow_ref,
-    mid_ref,
-    dens_ref,
-    sum_ref,
+    sems,
 ):
+    table_copy = pltpu.make_async_copy(table_in, table_ref, sems.at[0])
+    pot_copy = pltpu.make_async_copy(pot_in, pot_ref, sems.at[1])
+    slope_copy = pltpu.make_async_copy(slope_in, slope_ref, sems.at[2])
+    table_copy.start()
+    pot_copy.start()
+    slope_copy.start()
     sources = recv_ref.shape[0]
     width = TILE_CHUNKS * LANE
-    acc_ref[...] = jnp.zeros(acc_ref.shape, f32)
-    iota_b = lax.broadcasted_iota(i32, (N, LANE), 0)
-    iota_c = lax.broadcasted_iota(i32, (LANE, LANE), 0)
-
-    def tile(t, _):
-        where = []
+    iota = lax.broadcasted_iota(i32, (LANE, LANE), 0)
+
+    def build(tile, group_b, group_c, val_ref, hot_ref):
         for j in range(TILE_CHUNKS):
-            index = order_s[t * TILE_CHUNKS + j]
-            where.append(index)
-            hot = iota_b == gb_ref[pl.ds(index, 1), :]
-            hot_ref[:, j * LANE : (j + 1) * LANE] = jnp.where(hot, 1.0, 0.0).astype(bf16)
-        for pair in range(3):
-
-            @pl.when(count_s[1 + pair] > 0)
-            def _(pair=pair):
-                for j, index in enumerate(where):
-                    source = jnp.minimum(index >> 2, sources - 1)
-                    piece = index & 3
-                    hot = (iota_c + pair * LANE) == gc_ref[pl.ds(index, 1), :]
-                    cut = slice(j * LANE, (j + 1) * LANE)
-                    for part in range(2):
-                        value = recv_ref[source, pl.ds(4 * part + piece, 1), :]
-                        high = value.astype(bf16).astype(f32)
-                        low = value - high
-                        for k, v in ((part, high), (2 + part, low)):
-                            val_ref[k * LANE : (k + 1) * LANE, cut] = jnp.where(
-                                hot, v, 0.0
-                            ).astype(bf16)
-                acc_ref[pair] += mm(hot_ref[...], val_ref[...], NT)
-
+            index = order_s[tile * TILE_CHUNKS + j]
+            block, piece = index >> 2, index & 3
+            cut = slice(j * LANE, (j + 1) * LANE)
+            gb = gb_ref[piece, pl.ds(block, 1), :]
+            gc = gc_ref[piece, pl.ds(block, 1), :]
+            source = jnp.minimum(block, sources - 1)
+            parts = []
+            for part in range(2):
+                value = recv_ref[source, pl.ds(4 * part + piece, 1), :]
+                high = value.astype(bf16).astype(f32)
+                parts.append((part, high))
+                parts.append((2 + part, value - high))
+            for h in range(2):
+                hot = iota == gc - LANE * plan_s[8 + 2 * group_c + h]
+                hot_ref[h * LANE : (h + 1) * LANE, cut] = jnp.where(hot, 1.0, 0.0).astype(bf16)
+                hit = iota == gb - LANE * plan_s[4 + 2 * group_b + h]
+                for k, v in parts:
+                    top = (4 * h + k) * LANE
+                    val_ref[top : top + LANE, cut] = jnp.where(hit, v, 0.0).astype(bf16)
+
+    acc_ref[0] = jnp.zeros(acc_ref.shape[1:], f32)
+    build(0, 0, 0, val_a, hot_a)
+
+    def step(t, _):
+        build(2 * t + 1, 0, 0, val_b, hot_b)
+        acc_ref[0] += mm(val_a[...], hot_a[...], NT)
+        build(2 * t + 2, 0, 0, val_a, hot_a)
+        acc_ref[0] += mm(val_b[...], hot_b[...], NT)
         return 0
 
-    tiles = (count_s[0] + TILE_CHUNKS - 1) // TILE_CHUNKS
-    lax.fori_loop(0, tiles, tile, 0)
-
-    for level in range(2):
-        cos = table_ref[2 * level * N : (2 * level + 1) * N, :]
-        sin = table_ref[(2 * level + 1) * N : (2 * level + 2) * N, :]
-        for pair in range(3):
-            cut = slice(pair * LANE, (pair + 1) * LANE)
-            top = slice(2 * pair * LANE, (2 * pair + 1) * LANE)
-            bottom = slice((2 * pair + 1) * LANE, (2 * pair + 2) * LANE)
-            tab_ref[level, top, :N] = cos[cut]
-            tab_ref[level, top, N:] = sin[cut]
-            tab_ref[level, bottom, :N] = -sin[cut]
-            tab_ref[level, bottom, N:] = cos[cut]
-    for pair in range(3):
-        cut = slice(2 * pair * LANE, 2 * (pair + 1) * LANE)
-        flow_ref[:N, cut] = acc_ref[pair, :, : 2 * LANE].astype(bf16)
-        flow_ref[N:, cut] = acc_ref[pair, :, 2 * LANE :].astype(bf16)
-    both = mm(flow_ref[...], tab_ref[0])
-    passed = both[:N] + both[N:] + mm(flow_ref[:N], tab_ref[1])
-    high, low = halves(passed)
-    mid_ref[...] = mm(table_ref[: 2 * N], high) + (
-        mm(table_ref[2 * N :], high) + mm(table_ref[: 2 * N], low)
-    )
+    steps = (plan_s[0] + 2 * TILE_CHUNKS - 1) // (2 * TILE_CHUNKS)
+    lax.fori_loop(0, steps, step, 0)
+
+    def rest(combo, _):
+        group_b, group_c = combo >> 1, combo & 1
+
+        @pl.when((group_b < plan_s[1]) & (group_c < plan_s[2]))
+        def _():
+            acc_ref[combo] = jnp.zeros(acc_ref.shape[1:], f32)
+
+            def extra(t, _):
+                build(t, group_b, group_c, val_a, hot_a)
+                acc_ref[combo] += mm(val_a[...], hot_a[...], NT)
+                return 0
+
+            lax.fori_loop(0, 2 * steps, extra, 0)
+
+        return 0
+
+    lax.fori_loop(1, 4, rest, 0)
+
+    table_copy.wait()
+
+    def transform(group_b):
+        def along(group_c, first):
+            for level in range(2):
+                for h in range(2):
+                    band = jnp.minimum(plan_s[8 + 2 * group_c + h], 2) * LANE
+                    base = 2 * level * N
+                    cos = table_ref[pl.ds(pl.multiple_of(base + band, LANE), LANE), :]
+                    sin = table_ref[pl.ds(pl.multiple_of(base + N + band, LANE), LANE), :]
+                    top = slice(h * LANE, (h + 1) * LANE)
+                    bottom = slice((2 + h) * LANE, (3 + h) * LANE)
+                    tab_ref[level, top, :N] = cos
+                    tab_ref[level, top, N:] = sin
+                    tab_ref[level, bottom, :N] = -sin
+                    tab_ref[level, bottom, N:] = cos
+            combo = 2 * group_b + group_c
+            for h in range(2):
+                for k in range(4):
+                    top = ((k // 2) * 2 + h) * LANE
+                    flow_ref[top : top + LANE, (k % 2) * 2 * LANE : (k % 2 + 1) * 2 * LANE] = acc_ref[
+                        combo, (4 * h + k) * LANE : (4 * h + k + 1) * LANE, :
+                    ].astype(bf16)
+            half = 2 * LANE
+            both = mm(flow_ref[...], tab_ref[0])
+            result = both[:half] + both[half:] + mm(flow_ref[:half], tab_ref[1])
+            pass_ref[...] = result if first else pass_ref[...] + result
+
+        along(0, True)
+
+        @pl.when(plan_s[2] > 1)
+        def _():
+            along(1, False)
+
+        for h in range(2):
+            band = jnp.minimum(plan_s[4 + 2 * group_b + h], 2) * LANE
+            edge_ref[:, h * LANE : (h + 1) * LANE] = table_ref[
+                :, pl.ds(pl.multiple_of(band, LANE), LANE)
+            ]
+        high, low = halves(pass_ref[...])
+        result = mm(edge_ref[: 2 * N], high) + (
+            mm(edge_ref[2 * N :], high) + mm(edge_ref[: 2 * N], low)
+        )
+        mid_ref[...] = result if group_b == 0 else mid_ref[...] + result
+
+    transform(0)
+
+    @pl.when(plan_s[1] > 1)
+    def _():
+        transform(1)
+
+    pot_copy.wait()
 
     def finish(i, _):
         r = pl.ds(pl.multiple_of(8 * i, 8), 8)
@@ -315,30 +401,33 @@
         field_ref[1, r, :] = pot * imag
         return 0
 
-    lax.fori_loop(0, N // 8, finish, 0, unroll=4)
+    lax.fori_loop(0, N // 8, finish, 0, unroll=8)
+    field_copy = pltpu.make_async_copy(field_ref, field_out, sems.at[3])
+    field_copy.start()
+    slope_copy.wait()
 
     for q in range(32):
         base = (q // 16) * HALF
-
-        def gather(i, carry, q=q, base=base):
-            plain, scaled = carry
-            r = pl.ds(pl.multiple_of(base + 8 * i, 8), 8)
-            w = dens_ref[r, :] * slope_ref[q, pl.ds(pl.multiple_of(8 * i, 8), 8), :]
-            return plain + w, scaled + w * offb_ref[r, q : q + 1]
-
-        zero = jnp.zeros((8, N), f32)
-        plain, scaled = lax.fori_loop(0, HALF // 8, gather, (zero, zero), unroll=4)
-        sum_ref[q : q + 1, :] = jnp.sum(plain, axis=0, keepdims=True)
-        sum_ref[32 + q : 33 + q, :] = jnp.sum(scaled, axis=0, keepdims=True)
+        plain = [jnp.zeros((8, LANE), f32)] * 3
+        scaled = jnp.zeros((8, LANE), f32)
+        for i in range(HALF // 8):
+            r = slice(base + 8 * i, base + 8 * i + 8)
+            w = dens_ref[r, :] * slope_ref[q, 8 * i : 8 * i + 8, :]
+            w = [w[:, k * LANE : (k + 1) * LANE] for k in range(3)]
+            plain = [p + v for p, v in zip(plain, w)]
+            scaled = scaled + (w[0] + w[1] + w[2]) * offb_ref[r, q : q + 1]
+        for k in range(3):
+            sum_ref[q : q + 1, k * LANE : (k + 1) * LANE] = jnp.sum(plain[k], axis=0, keepdims=True)
+        sum_ref[32 + q : 33 + q, :LANE] = jnp.sum(scaled, axis=0, keepdims=True)
     plain = sum_ref[:32, :]
     off_a = col_ref[:32, 0:1]
     scale = col_ref[:32, 1:2] * VOLUME
     push_a = off_a * jnp.sum(plain, axis=1, keepdims=True) * scale
-    push_b = jnp.sum(sum_ref[32:, :], axis=1, keepdims=True) * scale
+    push_b = jnp.sum(sum_ref[32:, :LANE], axis=1, keepdims=True) * scale
     push_c = jnp.sum(plain * offc_ref[...], axis=1, keepdims=True) * scale
     packed = jnp.concatenate([push_a, push_b, push_c, 0.5 * col_ref[:32, 2:3]], axis=0)
-    turned = jnp.transpose(jnp.broadcast_to(packed, (LANE, LANE)))
-    push_ref[...] = turned[:8]
+    push_ref[...] = jnp.transpose(jnp.broadcast_to(packed, (LANE, LANE)))[:1]
+    field_copy.wait()
 
 
 def spread_kernel(terms_ref, out_ref):
@@ -363,6 +452,10 @@
     return [pl.BlockSpec(memory_space=pltpu.SMEM)] * count
 
 
+def anywhere(count):
+    return [pl.BlockSpec(memory_space=pl.ANY)] * count
+
+
 def params():
     return pltpu.CompilerParams(vmem_limit_bytes=VMEM_LIMIT)
 
@@ -392,15 +485,11 @@
     )(coefficients.reshape(2, slots, N), jnp.asarray(first_table))
     recv = lax.all_to_all(sent, "pw", 0, 0, tiled=True)
 
-    grid = jnp.pad(
-        col_map.reshape(sources, slots), ((0, 2), (0, 4 * LANE - slots)), constant_values=EMPTY
-    ).reshape(chunks + 8, LANE)
-    live = grid < EMPTY
-    gb = jnp.where(live, grid // N, -1000)
-    gc = jnp.where(live, grid % N, -1000)
-    live_chunk = live[:chunks, 0].astype(i32)
-
-    pot, slope, offb, offc, col, order, count = pl.pallas_call(
+    blocks = col_map.reshape(sources, slots)
+    grid = jnp.pad(blocks, ((0, 0), (0, 4 * LANE - slots)), constant_values=EMPTY)
+    live_chunk = (blocks[:, ::LANE] < EMPTY).astype(i32).reshape(chunks)
+
+    pot, slope, offb, offc, col, gb, gc, order, plan = pl.pallas_call(
         charges_kernel,
         out_shape=(
             jax.ShapeDtypeStruct((N, N), f32),
@@ -408,16 +497,20 @@
             jax.ShapeDtypeStruct((N, LANE), f32),
             jax.ShapeDtypeStruct((32, N), f32),
             jax.ShapeDtypeStruct((LANE, 8), f32),
-            jax.ShapeDtypeStruct((chunks + TILE_CHUNKS,), i32),
-            jax.ShapeDtypeStruct((4,), i32),
+            jax.ShapeDtypeStruct((4, sources + 8, LANE), i32),
+            jax.ShapeDtypeStruct((4, sources + 8, LANE), i32),
+            jax.ShapeDtypeStruct((chunks + 4 * TILE_CHUNKS,), i32),
+            jax.ShapeDtypeStruct((16,), i32),
         ),
         in_specs=smem(5) + vmem(5),
-        out_specs=tuple(vmem(5) + smem(2)),
+        out_specs=tuple(vmem(1) + anywhere(1) + vmem(5) + smem(2)),
         scratch_shapes=[
             pltpu.VMEM((N, LANE), f32),
             pltpu.VMEM((N, LANE), f32),
             pltpu.VMEM((32, N), f32),
             pltpu.VMEM((32, N), f32),
+            pltpu.VMEM((32, HALF, N), f32),
+            pltpu.SemaphoreType.DMA((32,)),
         ],
         compiler_params=params(),
         name="charges",
@@ -431,32 +524,40 @@
         charge_cell,
         charge_frac,
         charge[None],
-        gc,
+        grid,
     )
 
     field, push = pl.pallas_call(
         grid_kernel,
         out_shape=(
             jax.ShapeDtypeStruct((2, N, N), f32),
-            jax.ShapeDtypeStruct((8, LANE), f32),
+            jax.ShapeDtypeStruct((1, LANE), f32),
         ),
-        in_specs=smem(2) + vmem(9),
-        out_specs=tuple(vmem(2)),
+        in_specs=smem(2) + vmem(3) + anywhere(3) + vmem(3),
+        out_specs=tuple(anywhere(1) + vmem(1)),
         scratch_shapes=[
-            pltpu.VMEM((3, N, 4 * LANE), f32),
-            pltpu.VMEM((N, TILE_CHUNKS * LANE), bf16),
-            pltpu.VMEM((4 * LANE, TILE_CHUNKS * LANE), bf16),
-            pltpu.VMEM((2, 2 * N, 2 * N), bf16),
-            pltpu.VMEM((2 * N, 2 * N), bf16),
+            pltpu.VMEM((4, 8 * LANE, 2 * LANE), f32),
+            pltpu.VMEM((8 * LANE, TILE_CHUNKS * LANE), bf16),
+            pltpu.VMEM((8 * LANE, TILE_CHUNKS * LANE), bf16),
+            pltpu.VMEM((2 * LANE, TILE_CHUNKS * LANE), bf16),
+            pltpu.VMEM((2 * LANE, TILE_CHUNKS * LANE), bf16),
+            pltpu.VMEM((2, 4 * LANE, 2 * N), bf16),
+            pltpu.VMEM((4 * LANE, 4 * LANE), bf16),
+            pltpu.VMEM((4 * N, 2 * LANE), bf16),
+            pltpu.VMEM((2 * LANE, 2 * N), f32),
             pltpu.VMEM((2 * N, 2 * N), f32),
             pltpu.VMEM((N, N), f32),
             pltpu.VMEM((64, N), f32),
+            pltpu.VMEM((2, N, N), f32),
+            pltpu.VMEM((4 * N, N), bf16),
+            pltpu.VMEM((N, N), f32),
+            pltpu.VMEM((32, HALF, N), f32),
+            pltpu.SemaphoreType.DMA((4,)),
         ],
         compiler_params=params(),
         name="grid",
-    )(order, count, recv, gb, gc, jnp.asarray(second_table), pot, slope, offb, offc, col)
-
-    push = push[:1]
+    )(order, plan, recv, gb, gc, jnp.asarray(second_table), pot, slope, offb, offc, col)
+
     push = push + lax.ppermute(push, "mm", [(0, 1), (1, 0)])
     terms = lax.all_to_all(
         jnp.broadcast_to(push[None], (sources, 1, LANE)), "pw", 0, 0, tiled=True

time: 127 us -> 79.6 us (0.63)
  Pallas kernels: 87.5 us -> 41.2 us
  other arithmetic: 2.37 us -> 0.71 us
    pallas_call x1, Pallas kernels: 54.9 us -> 24.1 us  [local(): pl.pallas_call(grid_kernel, out_shape=(jax.ShapeDtypeStruct((2, N, N), f3...]
    pallas_call x1, Pallas kernels: 26.8 us -> 11.3 us  [local(): pl.pallas_call(charges_kernel, out_shape=(jax.ShapeDtypeStruct((N, N), f3...]
  transfers between devices with their start and end apart: 3 -> 3, of which waited for: 1 -> 1; matrix products, arithmetic and copies ran while one was open for 2% -> 3% of each run, Pallas kernels for 23% -> 18%
where the time goes in v2:
time: 79.6 us; the launch traced here: 79.7 us
  Pallas kernels  41.2 us (52%)
  blocking collectives  21.1 us (27%)
  starting transfers between devices  11.9 us (15%)
  local copies, waits for them, and re-layouts  2.95 us (4%)
  waiting for transfers between devices  1.16 us (1%)
    pallas_call x1, Pallas kernels, local(): pl.pallas_call(grid_kernel, out_shape=(jax.ShapeDtypeStruct((2, N, N), f3...  24.1 us
    all_to_all x1, blocking collectives, local(): lax.all_to_all(jnp.broadcast_to(push[None], (sources, 1, LANE)), 'pw', 0,...  21.1 us
    all_to_all x1, starting transfers between devices, local(): recv = lax.all_to_all(sent, 'pw', 0, 0, tiled=True)  11.5 us
    pallas_call x1, Pallas kernels, local(): pl.pallas_call(charges_kernel, out_shape=(jax.ShapeDtypeStruct((N, N), f3...  11.3 us
    pallas_call x1, Pallas kernels, local(): pl.pallas_call(spread_kernel, out_shape=jax.ShapeDtypeStruct((3, charge.s...  2.99 us
    pallas_call x1, Pallas kernels, local(): pl.pallas_call(columns_kernel, out_shape=jax.ShapeDtypeStruct((planes, 8,...  2.85 us
  transfers between devices with their start and end apart: 3, of which 1 were waited for; matrix products, arithmetic and copies ran while one was open for 3% of the time, Pallas kernels for 18%

profile of v2, /device:TPU:0, one launch (start us, length us, event | category | flops | bytes accessed | tf_op | source)
XLA Modules:
  0.0 79.7 jit_solution(13742097618551262517)
XLA Ops:
  0.6 0.0 copy-start.1
  0.6 0.1 collective-permute-start
  0.7 0.0 copy-start.3
  0.7 2.9 %columns.1 = f32[64,8,128]{2,1,0:T(8,128)} custom-call(f32[2,448,384]{2,1,0:T(8,128)} %bitcast.14, bf16[256,768]{1,0:T(8,128)(2,1)} %constant.19.clone.table_ref), custom_call_target="tpu_custom_call" | custom-call | tf_op jit(solution)/shard_map/columns/pallas_call | solution.py:477
  3.6 11.5 %all-to-all-start = ((f32[64,8,128]{2,1,0:T(8,128)}), f32[64,8,128]{2,1,0:T(8,128)S(1)}, u32[]{:S(2)}, u32[]{:S(2)}) async-start(f32[64,8,128]{2,1,0:T(8,128)} %columns.1), calls=%async_computation | async-start | bytes 524288 | tf_op jit(solution)/shard_map/all_to_all | solution.py:486
  15.1 0.0 copy-done.1
  15.1 0.1 reshape.21
  15.2 0.1 slice.3
  15.3 0.7 pad.9.grid_ref
  16.0 0.6 reshape.27.live_s
  16.6 0.0 collective-permute-done
  16.6 0.0 copy-done.3
  16.6 0.1 pad_add_fusion.list_s
  16.7 0.0 copy-start.2
  16.7 0.7 copy.14.list_ref
  17.5 0.0 copy-done.2
  17.5 11.3 %charges.1 = (f32[384,384]{1,0:T(8,128)}, f32[32,192,384]{2,1,0:T(8,128)}, f32[384,128]{1,0:T(8,128)}, f32[32,384]{1,0:T(8,128)}, f32[128,8]{1,0:T(8,128)}, /*in...) custom-call(s32[32]{0:T(128)} %copy-done.2, s32[3,512]{1,0:T(4,128)} %cell_ref.1, ...), custom_call_target="tpu_custom_call" | custom-call | tf_op jit(solution)/shard_map/charges/pallas_call | solution.py:492
  28.7 0.0 all-to-all-done.recv_ref
  28.7 0.0 copy-start
  28.8 0.7 copy-done
  29.5 24.1 %grid.1 = (f32[2,384,384]{2,1,0:T(8,128)}, f32[1,128]{1,0:T(1,128)}) custom-call(s32[272]{0:T(512)} %get-tuple-element.13.order_s, s32[16]{0:T(128)} %get-tuple-element.14.plan_s, f32[64,8,128]{2,1,0:T(8,128)} %copy-done, s32[4,72,128]{2,1,0:T(8,128)} %get-tuple-element.15.gb_ref, s32[4,72,128]{2,1,0:T(8,128)} %get-tuple-element.16.gc_ref, ...), custom_call_target="tpu_custom_call" | custom-call | tf_op jit(solution)/shard_map/grid/pallas_call | solution.py:530
  53.5 0.3 collective-permute-start.1
  53.8 1.2 %collective-permute-done.1 = f32[1,128]{1,0:T(1,128)S(1)} collective-permute-done((f32[1,128]{1,0:T(1,128)}, f32[1,128]{1,0:T(1,128)S(1)}, u32[]{:S(2)}, u32[]{:S(2)}) %collective-permute-start.1) | collective-permute-done | bytes 544 | tf_op jit(solution)/shard_map/ppermute | solution.py:561
  55.0 0.6 add_bitcast_fusion
  55.6 21.1 %all_to_all.10 = f32[64,1,128]{2,1,0:T(1,128)} all-to-all(f32[64,1,128]{2,1,0:T(1,128)S(1)} %broadcast_in_dim.25), channel_id=1, replica_groups=mesh['pw'=64,'mm'=2] {'pw'}, dimensions={0} | all-to-all | bytes 65536 | tf_op jit(solution)/shard_map/all_to_all | solution.py:562
  76.7 3.0 %spread.1 = f32[3,512]{1,0:T(4,128)} custom-call(f32[64,128]{1,0:T(8,128)} %bitcast.15), custom_call_target="tpu_custom_call" | custom-call | tf_op jit(solution)/shard_map/spread/pallas_call | solution.py:565
  (4 shorter events, 0.0 us)
Async XLA Ops:
  0.6 14.5 %copy-start.1 = (s32[28672]{0:T(1024)S(1)}, s32[28672]{0:T(1024)}, u32[]{:S(2)}) copy-start(s32[28672]{0:T(1024)} %param.9) | copy-start | bytes 344068
  0.6 16.0 %collective-permute-start = (s32[16]{0:T(128)}, s32[16]{0:T(128)S(1)}, u32[]{:S(2)}, u32[]{:S(2)}) collective-permute-start(s32[16]{0:T(128)} %bitcast.17), channel_id=1, source_target_pairs={{0,1},{1,0},{2,3},{3,2},{4,5},{5,4},{6,7},{7,6},{8,9},{9,8},{10,11... | collective-permute-start | bytes 200 | tf_op jit(solution)/shard_map/ppermute | solution.py:472
  0.7 15.9 %copy-start.3 = (s32[1,16]{1,0:T(1,128)S(1)}, s32[1,16]{1,0:T(1,128)}, u32[]{:S(2)}) copy-start(s32[1,16]{1,0:T(1,128)} %param.13) | copy-start | bytes 196
  3.6 25.1 %all-to-all-start = ((f32[64,8,128]{2,1,0:T(8,128)}), f32[64,8,128]{2,1,0:T(8,128)S(1)}, u32[]{:S(2)}, u32[]{:S(2)}) async-start(f32[64,8,128]{2,1,0:T(8,128)} %columns.1), calls=%async_computation | async-start | bytes 524288 | tf_op jit(solution)/shard_map/all_to_all | solution.py:486
  16.7 0.7 copy-start.2
  28.7 0.7 copy-start
  53.5 1.5 %collective-permute-start.1 = (f32[1,128]{1,0:T(1,128)}, f32[1,128]{1,0:T(1,128)S(1)}, u32[]{:S(2)}, u32[]{:S(2)}) collective-permute-start(f32[1,128]{1,0:T(1,128)} %get-tuple-element.23), channel_id=1, source_target_pairs={{0,1},{1,0},{2,3},{3,2},{4,5},{5,4},{6,7},{7,6},{8,9},{9,8},{10,11... | collective-permute-start | bytes 1544 | tf_op jit(solution)/shard_map/ppermute | solution.py:561

commit v3 on v2

--- a/solution.py
+++ b/solution.py
@@ -19,9 +19,8 @@
 VOLUME = SPACING**3
 PEAK = 2.0 / math.sqrt(math.pi)
 EMPTY = N * N
-TILE_CHUNKS = 4
+TILE_CHUNKS = 8
 NT = (((1,), (1,)), ((), ()))
-VMEM_LIMIT = 60 * 1024 * 1024
 
 
 def split_table(table):
@@ -217,13 +216,17 @@
 
         @pl.when(da * da < 16.0)
         def _(q=q, base=base, ucq=ucq, ecq=ecq, power=power, da=da, sb=sb):
-            def near(i, _):
-                r = pl.multiple_of(base + 8 * i, 8)
-                db = jnp.abs(wrap(r.astype(f32) + 3.5 - sb))
-                db = jnp.maximum(db - 3.5 * SPACING, 0.0)
-
-                @pl.when(da * da + db * db < 16.0)
+            first = jnp.floor((sb - 16.0) * 0.125).astype(i32)
+
+            def near(k, _):
+                group = first + k
+                group = jnp.where(group < 0, group + N // 8, group)
+                group = jnp.where(group >= N // 8, group - N // 8, group)
+                i = group - base // 8
+
+                @pl.when((i >= 0) & (i < HALF // 8))
                 def _():
+                    r = pl.multiple_of(8 * group, 8)
                     u = uab_ref[pl.ds(r, 8), q : q + 1] + ucq
                     k = lax.rsqrt(u)
                     e = eab_ref[pl.ds(r, 8), q : q + 1] * ecq
@@ -233,14 +236,13 @@
 
                 return 0
 
-            lax.fori_loop(0, HALF // 8, near, 0)
+            lax.fori_loop(0, 6, near, 0)
 
         copy = pltpu.make_async_copy(slope_ref.at[q], slope_out.at[q], sems.at[q])
         copy.start()
         copies.append(copy)
     for copy in copies:
         copy.wait()
-
 
 def grid_kernel(
     order_s,
@@ -248,8 +250,8 @@
     recv_ref,
     gb_ref,
     gc_ref,
-    table_in,
-    pot_in,
+    table_ref,
+    pot_ref,
     slope_in,
     offb_ref,
     offc_ref,
@@ -269,20 +271,17 @@
     dens_ref,
     sum_ref,
     field_ref,
-    table_ref,
-    pot_ref,
     slope_ref,
     sems,
 ):
-    table_copy = pltpu.make_async_copy(table_in, table_ref, sems.at[0])
-    pot_copy = pltpu.make_async_copy(pot_in, pot_ref, sems.at[1])
-    slope_copy = pltpu.make_async_copy(slope_in, slope_ref, sems.at[2])
-    table_copy.start()
-    pot_copy.start()
+    slope_copy = pltpu.make_async_copy(slope_in, slope_ref, sems.at[1])
     slope_copy.start()
     sources = recv_ref.shape[0]
-    width = TILE_CHUNKS * LANE
-    iota = lax.broadcasted_iota(i32, (LANE, LANE), 0)
+    iota = lax.broadcasted_iota(i32, (LANE, LANE), 0).astype(f32).astype(bf16)
+    one, zero = jnp.ones((LANE, LANE), bf16), jnp.zeros((LANE, LANE), bf16)
+
+    def within(cells, band):
+        return iota == (cells - LANE * band).astype(f32).astype(bf16)
 
     def build(tile, group_b, group_c, val_ref, hot_ref):
         for j in range(TILE_CHUNKS):
@@ -295,25 +294,25 @@
             parts = []
             for part in range(2):
                 value = recv_ref[source, pl.ds(4 * part + piece, 1), :]
-                high = value.astype(bf16).astype(f32)
+                high, low = halves(value)
                 parts.append((part, high))
-                parts.append((2 + part, value - high))
+                parts.append((2 + part, low))
             for h in range(2):
-                hot = iota == gc - LANE * plan_s[8 + 2 * group_c + h]
-                hot_ref[h * LANE : (h + 1) * LANE, cut] = jnp.where(hot, 1.0, 0.0).astype(bf16)
-                hit = iota == gb - LANE * plan_s[4 + 2 * group_b + h]
+                hot = within(gc, plan_s[8 + 2 * group_c + h])
+                hot_ref[h * LANE : (h + 1) * LANE, cut] = jnp.where(hot, one, zero)
+                hit = within(gb, plan_s[4 + 2 * group_b + h])
                 for k, v in parts:
                     top = (4 * h + k) * LANE
-                    val_ref[top : top + LANE, cut] = jnp.where(hit, v, 0.0).astype(bf16)
+                    val_ref[top : top + LANE, cut] = jnp.where(hit, v, zero)
 
     acc_ref[0] = jnp.zeros(acc_ref.shape[1:], f32)
     build(0, 0, 0, val_a, hot_a)
 
     def step(t, _):
+        acc_ref[0] += mm(val_a[...], hot_a[...], NT)
         build(2 * t + 1, 0, 0, val_b, hot_b)
-        acc_ref[0] += mm(val_a[...], hot_a[...], NT)
+        acc_ref[0] += mm(val_b[...], hot_b[...], NT)
         build(2 * t + 2, 0, 0, val_a, hot_a)
-        acc_ref[0] += mm(val_b[...], hot_b[...], NT)
         return 0
 
     steps = (plan_s[0] + 2 * TILE_CHUNKS - 1) // (2 * TILE_CHUNKS)
@@ -336,8 +335,6 @@
         return 0
 
     lax.fori_loop(1, 4, rest, 0)
-
-    table_copy.wait()
 
     def transform(group_b):
         def along(group_c, first):
@@ -388,8 +385,6 @@
     def _():
         transform(1)
 
-    pot_copy.wait()
-
     def finish(i, _):
         r = pl.ds(pl.multiple_of(8 * i, 8), 8)
         s = pl.ds(pl.multiple_of(N + 8 * i, 8), 8)
@@ -402,10 +397,9 @@
         return 0
 
     lax.fori_loop(0, N // 8, finish, 0, unroll=8)
-    field_copy = pltpu.make_async_copy(field_ref, field_out, sems.at[3])
+    field_copy = pltpu.make_async_copy(field_ref, field_out, sems.at[0])
     field_copy.start()
     slope_copy.wait()
-
     for q in range(32):
         base = (q // 16) * HALF
         plain = [jnp.zeros((8, LANE), f32)] * 3
@@ -453,11 +447,11 @@
 
 
 def anywhere(count):
-    return [pl.BlockSpec(memory_space=pl.ANY)] * count
-
-
-def params():
-    return pltpu.CompilerParams(vmem_limit_bytes=VMEM_LIMIT)
+    return [pl.BlockSpec(memory_space=pltpu.HBM)] * count
+
+
+def params(mebibytes):
+    return pltpu.CompilerParams(vmem_limit_bytes=mebibytes * 1024 * 1024)
 
 
 def local(coefficients, col_map, charge_cell, charge_frac, charge, tile_list):
@@ -480,7 +474,7 @@
         in_specs=vmem(2),
         out_specs=vmem(1)[0],
         scratch_shapes=[pltpu.VMEM((4 * LANE, 2 * N), bf16)] * 2,
-        compiler_params=params(),
+        compiler_params=params(12),
         name="columns",
     )(coefficients.reshape(2, slots, N), jnp.asarray(first_table))
     recv = lax.all_to_all(sent, "pw", 0, 0, tiled=True)
@@ -493,7 +487,7 @@
         charges_kernel,
         out_shape=(
             jax.ShapeDtypeStruct((N, N), f32),
-            jax.ShapeDtypeStruct((32, HALF, N), f32),
+            pltpu.HBM((32, HALF, N), f32),
             jax.ShapeDtypeStruct((N, LANE), f32),
             jax.ShapeDtypeStruct((32, N), f32),
             jax.ShapeDtypeStruct((LANE, 8), f32),
@@ -512,7 +506,7 @@
             pltpu.VMEM((32, HALF, N), f32),
             pltpu.SemaphoreType.DMA((32,)),
         ],
-        compiler_params=params(),
+        compiler_params=params(50),
         name="charges",
     )(
         listed,
@@ -533,7 +527,7 @@
             jax.ShapeDtypeStruct((2, N, N), f32),
             jax.ShapeDtypeStruct((1, LANE), f32),
         ),
-        in_specs=smem(2) + vmem(3) + anywhere(3) + vmem(3),
+        in_specs=smem(2) + vmem(5) + anywhere(1) + vmem(3),
         out_specs=tuple(anywhere(1) + vmem(1)),
         scratch_shapes=[
             pltpu.VMEM((4, 8 * LANE, 2 * LANE), f32),
@@ -549,12 +543,10 @@
             pltpu.VMEM((N, N), f32),
             pltpu.VMEM((64, N), f32),
             pltpu.VMEM((2, N, N), f32),
-            pltpu.VMEM((4 * N, N), bf16),
-            pltpu.VMEM((N, N), f32),
             pltpu.VMEM((32, HALF, N), f32),
-            pltpu.SemaphoreType.DMA((4,)),
+            pltpu.SemaphoreType.DMA((2,)),
         ],
-        compiler_params=params(),
+        compiler_params=params(50),
         name="grid",
     )(order, plan, recv, gb, gc, jnp.asarray(second_table), pot, slope, offb, offc, col)
 
@@ -567,7 +559,7 @@
         out_shape=jax.ShapeDtypeStruct((3, charge.shape[0]), f32),
         in_specs=vmem(1),
         out_specs=vmem(1)[0],
-        compiler_params=params(),
+        compiler_params=params(12),
         name="spread",
     )(terms)
     return (field[:, None, None], forces)

time: 79.6 us -> 69.5 us (0.87)
  Pallas kernels: 41.2 us -> 31.6 us
  waiting for transfers between devices: 1.16 us -> 3.01 us
  blocking collectives: 21.1 us -> 19.6 us
    pallas_call x1, Pallas kernels: 24.1 us -> 19.2 us  [local(): pl.pallas_call(grid_kernel, out_shape=(jax.ShapeDtypeStruct((2, N, N), f3...]
    pallas_call x1, Pallas kernels: 11.3 us -> 8.78 us  [local(): pl.pallas_call(charges_kernel, out_shape=(jax.ShapeDtypeStruct((N, N), f3...]
    all_to_all x1, waiting for transfers between devices: 0.01 us -> 1.86 us  [local(): recv = lax.all_to_all(sent, 'pw', 0, 0, tiled=True)]
    unnamed x8 -> x16, local copies, waits for them, and re-layouts: 0.72 us -> 2.35 us
    all_to_all x1, blocking collectives: 21.1 us -> 19.6 us  [local(): lax.all_to_all(jnp.broadcast_to(push[None], (sources, 1, LANE)), 'pw', 0,...]
    pallas_call x1, Pallas kernels: 2.85 us -> 1.44 us  [local(): pl.pallas_call(columns_kernel, out_shape=jax.ShapeDtypeStruct((planes, 8,...]
  transfers between devices with their start and end apart: 3 -> 3, of which waited for: 1 -> 2; matrix products, arithmetic and copies ran while one was open for 3% -> 1% of each run, Pallas kernels for 18% -> 15%
where the time goes in v3:
time: 69.5 us; the launch traced here: 69.6 us
  Pallas kernels  31.6 us (45%)
  blocking collectives  19.6 us (28%)
  starting transfers between devices  11.7 us (17%)
  waiting for transfers between devices  3.01 us (4%)
  local copies, waits for them, and re-layouts  2.79 us (4%)
  between operations  0.8 us (1%)
    all_to_all x1, blocking collectives, local(): lax.all_to_all(jnp.broadcast_to(push[None], (sources, 1, LANE)), 'pw', 0,...  19.6 us
    pallas_call x1, Pallas kernels, local(): pl.pallas_call(grid_kernel, out_shape=(jax.ShapeDtypeStruct((2, N, N), f3...  19.2 us
    all_to_all x1, starting transfers between devices, local(): recv = lax.all_to_all(sent, 'pw', 0, 0, tiled=True)  11.5 us
    pallas_call x1, Pallas kernels, local(): pl.pallas_call(charges_kernel, out_shape=(jax.ShapeDtypeStruct((N, N), f3...  8.78 us
    unnamed x16, local copies, waits for them, and re-layouts  2.35 us
    pallas_call x1, Pallas kernels, local(): pl.pallas_call(spread_kernel, out_shape=jax.ShapeDtypeStruct((3, charge.s...  2.24 us
    all_to_all x1, waiting for transfers between devices, local(): recv = lax.all_to_all(sent, 'pw', 0, 0, tiled=True)  1.86 us
    pallas_call x1, Pallas kernels, local(): pl.pallas_call(columns_kernel, out_shape=jax.ShapeDtypeStruct((planes, 8,...  1.44 us
  transfers between devices with their start and end apart: 3, of which 2 were waited for; matrix products, arithmetic and copies ran while one was open for 1% of the time, Pallas kernels for 15%

profile of v3, /device:TPU:0, one launch (start us, length us, event | category | flops | bytes accessed | tf_op | source)
XLA Modules:
  0.0 69.6 jit_solution(3263277067960130583)
XLA Ops:
  0.6 0.1 collective-permute-start
  0.7 0.0 copy-start
  0.7 1.3 %copy-done = f32[2,1,448,384]{3,2,1,0:T(8,128)S(1)} copy-done((f32[2,1,448,384]{3,2,1,0:T(8,128)S(1)}, f32[2,1,448,384]{3,2,1,0:T(8,128)}, u32[]{:S(2)}) %copy-start) | copy-done | bytes 1376280
  2.1 0.0 copy-start.2
  2.1 1.0 %copy-done.2 = bf16[256,768]{1,0:T(8,128)(2,1)S(1)} copy-done((bf16[256,768]{1,0:T(8,128)(2,1)S(1)}, bf16[256,768]{1,0:T(8,128)(2,1)}, u32[]{:S(2)}) %copy-start.2) | copy-done | bytes 393240
  3.1 0.0 copy-start.6
  3.1 0.0 copy-start.7
  3.1 0.0 copy-start.3
  3.1 0.0 copy-start.4
  3.1 0.0 copy-start.5
  3.1 0.0 copy-start.1
  3.1 1.4 %columns.1 = f32[64,8,128]{2,1,0:T(8,128)} custom-call(f32[2,448,384]{2,1,0:T(8,128)S(1)} %bitcast.14, bf16[256,768]{1,0:T(8,128)(2,1)S(1)} %copy-done.2), custom_call_target="tpu_custom_call" | custom-call | tf_op jit(solution)/shard_map/columns/pallas_call | solution.py:471
  4.5 11.5 %all-to-all-start = ((f32[64,8,128]{2,1,0:T(8,128)}), f32[64,8,128]{2,1,0:T(8,128)S(1)}, u32[]{:S(2)}, u32[]{:S(2)}) async-start(f32[64,8,128]{2,1,0:T(8,128)} %columns.1), calls=%async_computation | async-start | bytes 524288 | tf_op jit(solution)/shard_map/all_to_all | solution.py:480
  16.1 0.0 copy-done.6
  16.1 0.1 reshape.21
  16.2 0.1 slice.3
  16.3 0.1 reshape.27.live_s
  16.4 0.0 collective-permute-done
  16.4 0.0 copy-done.7
  16.5 0.1 pad_add_fusion.list_s
  16.5 0.1 copy.14.list_ref
  16.7 0.0 copy-done.3
  16.7 0.0 copy-done.4
  16.7 0.0 copy-done.5
  16.7 8.8 %charges.1 = (f32[384,384]{1,0:T(8,128)S(1)}, f32[32,192,384]{2,1,0:T(8,128)}, f32[384,128]{1,0:T(8,128)S(1)}, f32[32,384]{1,0:T(8,128)S(1)}, f32[128,8]{1,0:T(8...) custom-call(s32[32]{0:T(128)S(1)} %pad_add_fusion.list_s, ...), custom_call_target="tpu_custom_call" | custom-call | tf_op jit(solution)/shard_map/charges/pallas_call | solution.py:486
  25.5 1.9 %all-to-all-done.recv_ref = f32[64,8,128]{2,1,0:T(8,128)S(1)} async-done(((f32[64,8,128]{2,1,0:T(8,128)}), f32[64,8,128]{2,1,0:T(8,128)S(1)}, u32[]{:S(2)}, u32[]{:S(2)}) %all-to-all-start) | async-done | bytes 262176 | tf_op jit(solution)/shard_map/all_to_all | solution.py:480
  27.3 0.0 copy-done.1
  27.3 19.2 %grid.1 = (f32[2,384,384]{2,1,0:T(8,128)}, f32[1,128]{1,0:T(1,128)S(1)}) custom-call(s32[288]{0:T(512)S(1)} %get-tuple-element.13.order_s, s32[16]{0:T(128)S(1)} %get-tuple-element.14.plan_s, f32[64,8,128]{2,1,0:T(8,128)S(1)} %all-to-all-done.recv_ref, s32[4,72,128]{2,1,0:T(8,128)S(1)} %get-tuple-element.15.gb_ref, ...), custom_call_target="tpu_custom_call" | custom-call | tf_op jit(solution)/shard_map/grid/pallas_call | solution.py:524
  46.5 0.1 collective-permute-start.1
  46.6 1.1 %collective-permute-done.1 = f32[1,128]{1,0:T(1,128)S(1)} collective-permute-done((f32[1,128]{1,0:T(1,128)S(1)}, f32[1,128]{1,0:T(1,128)S(1)}, u32[]{:S(2)}, u32[]{:S(2)}) %collective-permute-start.1) | collective-permute-done | bytes 544 | tf_op jit(solution)/shard_map/ppermute | solution.py:553
  47.8 19.6 %all_to_all.10 = f32[64,1,128]{2,1,0:T(1,128)S(1)} all-to-all(f32[64,1,128]{2,1,0:T(1,128)S(1)} %broadcast_in_dim.25), channel_id=1, replica_groups=mesh['pw'=64,'mm'=2] {'pw'}, dimensions={0} | all-to-all | bytes 65536 | tf_op jit(solution)/shard_map/all_to_all | solution.py:554
  67.4 2.2 %spread.1 = f32[3,512]{1,0:T(4,128)} custom-call(f32[64,128]{1,0:T(8,128)S(1)} %bitcast.15), custom_call_target="tpu_custom_call" | custom-call | tf_op jit(solution)/shard_map/spread/pallas_call | solution.py:557
  (6 shorter events, 0.1 us)
Async XLA Ops:
  0.6 15.8 %collective-permute-start = (s32[16]{0:T(128)}, s32[16]{0:T(128)S(1)}, u32[]{:S(2)}, u32[]{:S(2)}) collective-permute-start(s32[16]{0:T(128)} %bitcast.17), channel_id=1, source_target_pairs={{0,1},{1,0},{2,3},{3,2},{4,5},{5,4},{6,7},{7,6},{8,9},{9,8},{10,11... | collective-permute-start | bytes 200 | tf_op jit(solution)/shard_map/ppermute | solution.py:466
  0.7 1.3 %copy-start = (f32[2,1,448,384]{3,2,1,0:T(8,128)S(1)}, f32[2,1,448,384]{3,2,1,0:T(8,128)}, u32[]{:S(2)}) copy-start(f32[2,1,448,384]{3,2,1,0:T(8,128)} %param.8) | copy-start | bytes 4128772
  2.1 1.0 %copy-start.2 = (bf16[256,768]{1,0:T(8,128)(2,1)S(1)}, bf16[256,768]{1,0:T(8,128)(2,1)}, u32[]{:S(2)}) copy-start(bf16[256,768]{1,0:T(8,128)(2,1)} %constant.19.clone.table_ref) | copy-start | bytes 1179652
  3.1 13.0 %copy-start.6 = (s32[28672]{0:T(1024)S(1)}, s32[28672]{0:T(1024)}, u32[]{:S(2)}) copy-start(s32[28672]{0:T(1024)} %param.9) | copy-start | bytes 344068
  3.1 13.4 %copy-start.7 = (s32[1,16]{1,0:T(1,128)S(1)}, s32[1,16]{1,0:T(1,128)}, u32[]{:S(2)}) copy-start(s32[1,16]{1,0:T(1,128)} %param.13) | copy-start | bytes 196
  3.1 13.6 %copy-start.3 = (s32[3,512]{1,0:T(4,128)S(1)}, s32[3,512]{1,0:T(4,128)}, u32[]{:S(2)}) copy-start(s32[3,512]{1,0:T(4,128)} %cell_ref.1) | copy-start | bytes 18436
  3.1 13.6 %copy-start.4 = (f32[3,512]{1,0:T(4,128)S(1)}, f32[3,512]{1,0:T(4,128)}, u32[]{:S(2)}) copy-start(f32[3,512]{1,0:T(4,128)} %frac_ref.1) | copy-start | bytes 18436
  3.1 13.6 %copy-start.5 = (f32[512]{0:T(512)S(1)}, f32[512]{0:T(512)}, u32[]{:S(2)}) copy-start(f32[512]{0:T(512)} %param.12) | copy-start | bytes 6148
  3.1 24.2 %copy-start.1 = (bf16[1536,384]{1,0:T(8,128)(2,1)S(1)}, bf16[1536,384]{1,0:T(8,128)(2,1)}, u32[]{:S(2)}) copy-start(bf16[1536,384]{1,0:T(8,128)(2,1)} %constant.20.clone.table_ref) | copy-start | bytes 3538948
  4.5 22.8 %all-to-all-start = ((f32[64,8,128]{2,1,0:T(8,128)}), f32[64,8,128]{2,1,0:T(8,128)S(1)}, u32[]{:S(2)}, u32[]{:S(2)}) async-start(f32[64,8,128]{2,1,0:T(8,128)} %columns.1), calls=%async_computation | async-start | bytes 524288 | tf_op jit(solution)/shard_map/all_to_all | solution.py:480
  46.5 1.2 %collective-permute-start.1 = (f32[1,128]{1,0:T(1,128)S(1)}, f32[1,128]{1,0:T(1,128)S(1)}, u32[]{:S(2)}, u32[]{:S(2)}) collective-permute-start(f32[1,128]{1,0:T(1,128)S(1)} %get-tuple-element.23), channel_id=1, source_target_pairs={{0,1},{1,0},{2,3},{3,2},{4,5},{5,4},{6,7},{7,6},{8,9},{9,8},{10,11... | collective-permute-start | bytes 1544 | tf_op jit(solution)/shard_map/ppermute | solution.py:553

commit v4 on v3

--- a/solution.py
+++ b/solution.py
@@ -54,24 +54,63 @@
     return high, low
 
 
-def columns_kernel(coef_ref, table_ref, out_ref, high_ref, low_ref):
+def flip_table(length):
+    row = lax.broadcasted_iota(i32, (length, length), 0)
+    column = lax.broadcasted_iota(i32, (length, length), 1)
+    return jnp.where(row + column == length - 1, 1.0, 0.0).astype(bf16)
+
+
+def columns_kernel(
+    plane_s, coef_in, table_in, out_ref, coef_ref, table_ref, high_ref, low_ref, sems
+):
     slots = coef_ref.shape[1]
-    pad = high_ref.shape[0] - slots
+    half = slots // 2
+    copies = []
+    for part in range(2):
+        for piece in range(2):
+            cut = pl.ds(piece * half, half)
+            copies.append(
+                pltpu.make_async_copy(
+                    coef_in.at[part, cut], coef_ref.at[part, cut], sems.at[2 * part + piece]
+                )
+            )
+    copies.append(pltpu.make_async_copy(table_in, table_ref, sems.at[4]))
+    for copy in copies:
+        copy.start()
+    width = high_ref.shape[0]
     planes = out_ref.shape[0]
+    high_ref[slots:, :] = jnp.zeros((width - slots, 2 * N), bf16)
+    low_ref[slots:, :] = jnp.zeros((width - slots, 2 * N), bf16)
     for part in range(2):
-        high, low = halves(coef_ref[part])
-        high_ref[:slots, part * N : (part + 1) * N] = high
-        low_ref[:slots, part * N : (part + 1) * N] = low
-    high_ref[slots:, :] = jnp.zeros((pad, 2 * N), bf16)
-    low_ref[slots:, :] = jnp.zeros((pad, 2 * N), bf16)
+        for piece in range(2):
+            copies[2 * part + piece].wait()
+            rows = slice(piece * half, (piece + 1) * half)
+            high, low = halves(coef_ref[part, rows])
+            high_ref[rows, part * N : (part + 1) * N] = high
+            low_ref[rows, part * N : (part + 1) * N] = low
+    copies[4].wait()
     rows = 2 * planes
     both = mm(table_ref[...], high_ref[...], NT)
     result = both[:rows] + both[rows:] + mm(table_ref[:rows], low_ref[...], NT)
-    for part in range(2):
-        for piece in range(4):
-            out_ref[:, 4 * part + piece, :] = result[
-                part * planes : (part + 1) * planes, piece * LANE : (piece + 1) * LANE
-            ]
+
+    def put(values):
+        for part in range(2):
+            for piece in range(4):
+                out_ref[:, 4 * part + piece, :] = values[
+                    part * planes : (part + 1) * planes, piece * LANE : (piece + 1) * LANE
+                ]
+
+    reverse = plane_s[0] >= planes // 2
+
+    @pl.when(jnp.logical_not(reverse))
+    def _():
+        put(result)
+
+    @pl.when(reverse)
+    def _():
+        high, low = halves(result)
+        flip = flip_table(width)
+        put(mm(high, flip) + mm(low, flip))
 
 
 def wrap(offset):
@@ -116,7 +155,6 @@
     cell_s,
     frac_s,
     plane_s,
-    live_s,
     list_ref,
     cell_ref,
     frac_ref,
@@ -129,7 +167,7 @@
     col_ref,
     gb_ref,
     gc_ref,
-    order_s,
+    owner_ref,
     plan_s,
     uab_ref,
     eab_ref,
@@ -138,29 +176,29 @@
     slope_ref,
     sems,
 ):
-    chunks = live_s.shape[0]
-
-    def note(i, c):
-        order_s[c] = i
-        return c + live_s[i]
-
-    count = lax.fori_loop(0, chunks, note, jnp.int32(0), unroll=8)
-    for j in range(4 * TILE_CHUNKS):
-        order_s[count + j] = jnp.int32(chunks)
-    plan_s[0] = count
     cells = grid_ref[...]
-    live = cells < EMPTY
-    row = jnp.floor((cells.astype(f32) + 0.5) * (1.0 / N)).astype(i32)
-    gb = jnp.where(live, row, -1000)
-    gc = jnp.where(live, cells - N * row, -1000)
-    blocks = cells.shape[0]
-    for values, out, start in ((gb, gb_ref, 4), (gc, gc_ref, 8)):
+    pairs = cells.shape[0] // 2
+    row = jnp.floor((cells.astype(f32) + 0.5) * (1.0 / N))
+    gb = jnp.where(cells < EMPTY, row, -1000.0)
+    gc = jnp.where(cells < EMPTY, cells.astype(f32) - N * row, -1000.0)
+    high, low = halves(jnp.concatenate([gb[pairs:], gc[pairs:]], axis=0))
+    flip = flip_table(cells.shape[1])
+    turned = mm(high, flip) + mm(low, flip)
+    owned = jnp.where(gb[:pairs] >= 0.0, 1.0, 0.0)
+    for piece in range(4):
+        cut = slice(piece * LANE, (piece + 1) * LANE)
+        owner_ref[:, piece, :] = owned[:, cut]
+        owner_ref[:, 4 + piece, :] = owned[:, cut]
+    for values, other, out, start in (
+        (gb[:pairs], turned[:pairs], gb_ref, 4),
+        (gc[:pairs], turned[pairs:], gc_ref, 8),
+    ):
+        merged = jnp.maximum(values, other)
         for piece in range(4):
-            out[piece, :blocks, :] = values[:, piece * LANE : (piece + 1) * LANE]
-        out[:, blocks:, :] = jnp.full((4, 8, LANE), -1000, i32)
+            out[piece] = merged[:, piece * LANE : (piece + 1) * LANE]
         found = jnp.int32(0)
         for band in range(3):
-            inside = (values >= band * LANE) & (values < (band + 1) * LANE)
+            inside = (merged >= band * LANE) & (merged < (band + 1) * LANE)
             plan_s[start + found] = jnp.int32(band)
             found = found + jnp.max(jnp.where(inside, 1.0, 0.0)).astype(i32)
         for slot in range(4):
@@ -196,29 +234,24 @@
     uab = off_b * off_b + (row_a * row_a + SOFTEN)
     uab_ref[...] = uab
     eab_ref[...] = PEAK * jnp.exp(-uab)
-    pot_ref[...] = jnp.zeros((N, N), f32)
-
-    copies = []
-    for q in range(32):
+
+    def wide(ref, q):
+        return jnp.broadcast_to(ref[q : q + 1, :], (8, N))
+
+    def power(q):
+        return jnp.broadcast_to(strength[q : q + 1, :], (8, N))
+
+    def near(q):
         base = (q // 16) * HALF
-        ucq = jnp.broadcast_to(uc_ref[q : q + 1, :], (8, N))
-        ecq = jnp.broadcast_to(ec_ref[q : q + 1, :], (8, N))
         own = list_s[q]
-        power = jnp.broadcast_to(strength[q : q + 1, :], (8, N))
-        for i in range(HALF // 8):
-            r = slice(base + 8 * i, base + 8 * i + 8)
-            k = lax.rsqrt(uab_ref[r, q : q + 1] + ucq)
-            e = eab_ref[r, q : q + 1] * ecq
-            slope_ref[q, 8 * i : 8 * i + 8, :] = k * k * (e - k)
-            pot_ref[r, :] += power * k
         da = wrap(plane - (cell_s[0, own].astype(f32) + frac_s[0, own]))
-        sb = cell_s[1, own].astype(f32) + frac_s[1, own]
 
         @pl.when(da * da < 16.0)
-        def _(q=q, base=base, ucq=ucq, ecq=ecq, power=power, da=da, sb=sb):
+        def _():
+            sb = cell_s[1, own].astype(f32) + frac_s[1, own]
             first = jnp.floor((sb - 16.0) * 0.125).astype(i32)
 
-            def near(k, _):
+            def fix(k, _):
                 group = first + k
                 group = jnp.where(group < 0, group + N // 8, group)
                 group = jnp.where(group >= N // 8, group - N // 8, group)
@@ -227,27 +260,44 @@
                 @pl.when((i >= 0) & (i < HALF // 8))
                 def _():
                     r = pl.multiple_of(8 * group, 8)
-                    u = uab_ref[pl.ds(r, 8), q : q + 1] + ucq
+                    u = uab_ref[pl.ds(r, 8), q : q + 1] + wide(uc_ref, q)
                     k = lax.rsqrt(u)
-                    e = eab_ref[pl.ds(r, 8), q : q + 1] * ecq
+                    e = eab_ref[pl.ds(r, 8), q : q + 1] * wide(ec_ref, q)
                     full = erf(u * k) * k
                     slope_ref[q, pl.ds(pl.multiple_of(8 * i, 8), 8), :] = k * k * (e - full)
-                    pot_ref[pl.ds(r, 8), :] += power * (full - k)
+                    pot_ref[pl.ds(r, 8), :] += power(q) * (full - k)
 
                 return 0
 
-            lax.fori_loop(0, 6, near, 0)
-
-        copy = pltpu.make_async_copy(slope_ref.at[q], slope_out.at[q], sems.at[q])
-        copy.start()
-        copies.append(copy)
+            lax.fori_loop(0, 6, fix, 0)
+
+    copies = []
+    for a in range(0, 16, 2):
+        for half in range(2):
+            pair = (16 * half + a, 16 * half + a + 1)
+            lanes = [(q, wide(uc_ref, q), wide(ec_ref, q), power(q)) for q in pair]
+            for i in range(HALF // 8):
+                r = slice(half * HALF + 8 * i, half * HALF + 8 * i + 8)
+                total = None
+                for q, ucq, ecq, strong in lanes:
+                    k = lax.rsqrt(uab_ref[r, q : q + 1] + ucq)
+                    e = eab_ref[r, q : q + 1] * ecq
+                    slope_ref[q, 8 * i : 8 * i + 8, :] = k * k * (e - k)
+                    total = strong * k if total is None else total + strong * k
+                pot_ref[r, :] = total if a == 0 else pot_ref[r, :] + total
+        for q in (a, a + 1, 16 + a, 17 + a):
+            near(q)
+            copy = pltpu.make_async_copy(slope_ref.at[q], slope_out.at[q], sems.at[q])
+            copy.start()
+            copies.append(copy)
     for copy in copies:
         copy.wait()
 
+
 def grid_kernel(
-    order_s,
     plan_s,
     recv_ref,
+    owner_ref,
     gb_ref,
     gc_ref,
     table_ref,
@@ -272,28 +322,29 @@
     sum_ref,
     field_ref,
     slope_ref,
+    merged_ref,
     sems,
 ):
     slope_copy = pltpu.make_async_copy(slope_in, slope_ref, sems.at[1])
     slope_copy.start()
-    sources = recv_ref.shape[0]
+    pairs = merged_ref.shape[0]
+    merged_ref[...] = jnp.where(owner_ref[...] > 0.0, recv_ref[:pairs], recv_ref[pairs:])
     iota = lax.broadcasted_iota(i32, (LANE, LANE), 0).astype(f32).astype(bf16)
     one, zero = jnp.ones((LANE, LANE), bf16), jnp.zeros((LANE, LANE), bf16)
 
     def within(cells, band):
-        return iota == (cells - LANE * band).astype(f32).astype(bf16)
+        return iota == (cells - (LANE * band).astype(f32)).astype(bf16)
 
     def build(tile, group_b, group_c, val_ref, hot_ref):
         for j in range(TILE_CHUNKS):
-            index = order_s[tile * TILE_CHUNKS + j]
-            block, piece = index >> 2, index & 3
+            pair = jnp.minimum(tile * (TILE_CHUNKS // 4) + j // 4, pairs - 1)
+            piece = j % 4
             cut = slice(j * LANE, (j + 1) * LANE)
-            gb = gb_ref[piece, pl.ds(block, 1), :]
-            gc = gc_ref[piece, pl.ds(block, 1), :]
-            source = jnp.minimum(block, sources - 1)
+            gb = gb_ref[piece, pl.ds(pair, 1), :]
+            gc = gc_ref[piece, pl.ds(pair, 1), :]
             parts = []
             for part in range(2):
-                value = recv_ref[source, pl.ds(4 * part + piece, 1), :]
+                value = merged_ref[pair, 4 * part + piece : 4 * part + piece + 1, :]
                 high, low = halves(value)
                 parts.append((part, high))
                 parts.append((2 + part, low))
@@ -315,7 +366,7 @@
         build(2 * t + 2, 0, 0, val_a, hot_a)
         return 0
 
-    steps = (plan_s[0] + 2 * TILE_CHUNKS - 1) // (2 * TILE_CHUNKS)
+    steps = 2 * pairs // TILE_CHUNKS
     lax.fori_loop(0, steps, step, 0)
 
     def rest(combo, _):
@@ -460,7 +511,6 @@
     planes = sources
     plane = lax.axis_index("pw").astype(i32)
     first_table, second_table = tables(planes)
-    chunks = 4 * sources
 
     own = tile_list[0]
     other = lax.ppermute(own, "mm", [(0, 1), (1, 0)])
@@ -471,19 +521,24 @@
     sent = pl.pallas_call(
         columns_kernel,
         out_shape=jax.ShapeDtypeStruct((planes, 8, LANE), f32),
-        in_specs=vmem(2),
+        in_specs=smem(1) + anywhere(2),
         out_specs=vmem(1)[0],
-        scratch_shapes=[pltpu.VMEM((4 * LANE, 2 * N), bf16)] * 2,
-        compiler_params=params(12),
+        scratch_shapes=[
+            pltpu.VMEM((2, slots, N), f32),
+            pltpu.VMEM(first_table.shape, bf16),
+            pltpu.VMEM((4 * LANE, 2 * N), bf16),
+            pltpu.VMEM((4 * LANE, 2 * N), bf16),
+            pltpu.SemaphoreType.DMA((5,)),
+        ],
+        compiler_params=params(60),
         name="columns",
-    )(coefficients.reshape(2, slots, N), jnp.asarray(first_table))
+    )(plane[None], coefficients.reshape(2, slots, N), jnp.asarray(first_table))
     recv = lax.all_to_all(sent, "pw", 0, 0, tiled=True)
 
     blocks = col_map.reshape(sources, slots)
     grid = jnp.pad(blocks, ((0, 0), (0, 4 * LANE - slots)), constant_values=EMPTY)
-    live_chunk = (blocks[:, ::LANE] < EMPTY).astype(i32).reshape(chunks)
-
-    pot, slope, offb, offc, col, gb, gc, order, plan = pl.pallas_call(
+
+    pot, slope, offb, offc, col, gb, gc, owner, plan = pl.pallas_call(
         charges_kernel,
         out_shape=(
             jax.ShapeDtypeStruct((N, N), f32),
@@ -491,13 +546,13 @@
             jax.ShapeDtypeStruct((N, LANE), f32),
             jax.ShapeDtypeStruct((32, N), f32),
             jax.ShapeDtypeStruct((LANE, 8), f32),
-            jax.ShapeDtypeStruct((4, sources + 8, LANE), i32),
-            jax.ShapeDtypeStruct((4, sources + 8, LANE), i32),
-            jax.ShapeDtypeStruct((chunks + 4 * TILE_CHUNKS,), i32),
+            jax.ShapeDtypeStruct((4, sources // 2, LANE), f32),
+            jax.ShapeDtypeStruct((4, sources // 2, LANE), f32),
+            jax.ShapeDtypeStruct((sources // 2, 8, LANE), f32),
             jax.ShapeDtypeStruct((16,), i32),
         ),
-        in_specs=smem(5) + vmem(5),
-        out_specs=tuple(vmem(1) + anywhere(1) + vmem(5) + smem(2)),
+        in_specs=smem(4) + vmem(5),
+        out_specs=tuple(vmem(1) + anywhere(1) + vmem(6) + smem(1)),
         scratch_shapes=[
             pltpu.VMEM((N, LANE), f32),
             pltpu.VMEM((N, LANE), f32),
@@ -513,7 +568,6 @@
         charge_cell,
         charge_frac,
         plane[None],
-        live_chunk,
         listed_col,
         charge_cell,
         charge_frac,
@@ -527,7 +581,7 @@
             jax.ShapeDtypeStruct((2, N, N), f32),
             jax.ShapeDtypeStruct((1, LANE), f32),
         ),
-        in_specs=smem(2) + vmem(5) + anywhere(1) + vmem(3),
+        in_specs=smem(1) + vmem(6) + anywhere(1) + vmem(3),
         out_specs=tuple(anywhere(1) + vmem(1)),
         scratch_shapes=[
             pltpu.VMEM((4, 8 * LANE, 2 * LANE), f32),
@@ -544,11 +598,12 @@
             pltpu.VMEM((64, N), f32),
             pltpu.VMEM((2, N, N), f32),
             pltpu.VMEM((32, HALF, N), f32),
+            pltpu.VMEM((sources // 2, 8, LANE), f32),
             pltpu.SemaphoreType.DMA((2,)),
         ],
         compiler_params=params(50),
         name="grid",
-    )(order, plan, recv, gb, gc, jnp.asarray(second_table), pot, slope, offb, offc, col)
+    )(plan, recv, owner, gb, gc, jnp.asarray(second_table), pot, slope, offb, offc, col)
 
     push = push + lax.ppermute(push, "mm", [(0, 1), (1, 0)])
     terms = lax.all_to_all(

time: 69.5 us -> 64.1 us (0.922)
  blocking collectives: 19.6 us -> 16.9 us
  local copies, waits for them, and re-layouts: 2.79 us -> 0.27 us
  Pallas kernels: 31.6 us -> 30.2 us
    all_to_all x1, blocking collectives: 19.6 us -> 16.9 us  [local(): lax.all_to_all(jnp.broadcast_to(push[None], (sources, 1, LANE)), 'pw', 0,...]
    pallas_call x1, Pallas kernels: 19.2 us -> 16.6 us  [local(): pl.pallas_call(grid_kernel, out_shape=(jax.ShapeDtypeStruct((2, N, N), f3...]
    unnamed x16 -> x12, local copies, waits for them, and re-layouts: 2.35 us -> 0.03 us
    pallas_call x1, Pallas kernels: 1.44 us -> 3 us  [local(): pl.pallas_call(columns_kernel, out_shape=jax.ShapeDtypeStruct((planes, 8,...]
  transfers between devices with their start and end apart: 3 -> 3, of which waited for: 2 -> 2; matrix products, arithmetic and copies ran while one was open for 1% -> 0% of each run, Pallas kernels for 15% -> 18%
where the time goes in v4:
time: 64.1 us; the launch traced here: 63.8 us
  Pallas kernels  30.2 us (47%)
  blocking collectives  16.9 us (26%)
  starting transfers between devices  12 us (19%)
  waiting for transfers between devices  3.6 us (6%)
  between operations  0.81 us (1%)
    all_to_all x1, blocking collectives, local(): lax.all_to_all(jnp.broadcast_to(push[None], (sources, 1, LANE)), 'pw', 0,...  16.9 us
    pallas_call x1, Pallas kernels, local(): pl.pallas_call(grid_kernel, out_shape=(jax.ShapeDtypeStruct((2, N, N), f3...  16.6 us
    all_to_all x1, starting transfers between devices, local(): recv = lax.all_to_all(sent, 'pw', 0, 0, tiled=True)  11.8 us
    pallas_call x1, Pallas kernels, local(): pl.pallas_call(charges_kernel, out_shape=(jax.ShapeDtypeStruct((N, N), f3...  8.38 us
    pallas_call x1, Pallas kernels, local(): pl.pallas_call(columns_kernel, out_shape=jax.ShapeDtypeStruct((planes, 8,...  3 us
    all_to_all x1, waiting for transfers between devices, local(): recv = lax.all_to_all(sent, 'pw', 0, 0, tiled=True)  2.45 us
    pallas_call x1, Pallas kernels, local(): pl.pallas_call(spread_kernel, out_shape=jax.ShapeDtypeStruct((3, charge.s...  2.24 us
  transfers between devices with their start and end apart: 3, of which 2 were waited for; matrix products, arithmetic and copies ran while one was open for 0% of the time, Pallas kernels for 18%

profile of v4, /device:TPU:0, one launch (start us, length us, event | category | flops | bytes accessed | tf_op | source)
XLA Modules:
  0.0 63.8 jit_solution(17358009517931754817)
XLA Ops:
  0.6 0.0 copy-start.4
  0.6 0.1 collective-permute-start
  0.7 0.0 copy-start.5
  0.8 0.0 copy-start.1
  0.8 0.0 copy-start.2
  0.8 0.0 copy-start.3
  0.8 0.0 copy-start
  0.8 3.0 %columns.1 = f32[64,8,128]{2,1,0:T(8,128)} custom-call(s32[1]{0:T(128)} %bitcast.1.plane_s, f32[2,448,384]{2,1,0:T(8,128)} %bitcast.16, bf16[256,768]{1,0:T(8,128)(2,1)} %constant.18.clone.table_in), custom_call_target="tpu_custom_call" | custom-call | tf_op jit(solution)/shard_map/columns/pallas_call | solution.py:521
  3.8 11.8 %all-to-all-start = ((f32[64,8,128]{2,1,0:T(8,128)}), f32[64,8,128]{2,1,0:T(8,128)S(1)}, u32[]{:S(2)}, u32[]{:S(2)}) async-start(f32[64,8,128]{2,1,0:T(8,128)} %columns.1), calls=%async_computation | async-start | bytes 524288 | tf_op jit(solution)/shard_map/all_to_all | solution.py:536
  15.6 0.0 copy-done.4
  15.6 0.1 reshape.16
  15.7 0.0 collective-permute-done
  15.7 0.0 copy-done.5
  15.8 0.1 pad_add_fusion.list_s
  15.9 0.1 copy.12.list_ref
  16.0 0.0 copy-done.1
  16.0 0.0 copy-done.2
  16.0 0.0 copy-done.3
  16.0 8.4 %charges.1 = (f32[384,384]{1,0:T(8,128)S(1)}, f32[32,192,384]{2,1,0:T(8,128)}, f32[384,128]{1,0:T(8,128)S(1)}, f32[32,384]{1,0:T(8,128)S(1)}, f32[128,8]{1,0:T(8...) custom-call(s32[32]{0:T(128)S(1)} %pad_add_fusion.list_s, ...), custom_call_target="tpu_custom_call" | custom-call | tf_op jit(solution)/shard_map/charges/pallas_call | solution.py:541
  24.4 2.5 %all-to-all-done.recv_ref = f32[64,8,128]{2,1,0:T(8,128)S(1)} async-done(((f32[64,8,128]{2,1,0:T(8,128)}), f32[64,8,128]{2,1,0:T(8,128)S(1)}, u32[]{:S(2)}, u32[]{:S(2)}) %all-to-all-start) | async-done | bytes 262176 | tf_op jit(solution)/shard_map/all_to_all | solution.py:536
  26.8 0.0 copy-done
  26.8 16.6 %grid.1 = (f32[2,384,384]{2,1,0:T(8,128)}, f32[1,128]{1,0:T(1,128)S(1)}) custom-call(s32[16]{0:T(128)S(1)} %get-tuple-element.13.plan_s, f32[64,8,128]{2,1,0:T(8,128)S(1)} %all-to-all-done.recv_ref, f32[32,8,128]{2,1,0:T(8,128)S(1)} %get-tuple-element.14.owner_ref, f32[4,32,128]{2,1,0:T(8,128)S(1)} %get-tuple-element.15.gb_ref, ...), custom_call_target="tpu_custom_call" | custom-call | tf_op jit(solution)/shard_map/grid/pallas_call | solution.py:578
  43.4 0.1 collective-permute-start.1
  43.5 1.1 %collective-permute-done.1 = f32[1,128]{1,0:T(1,128)S(1)} collective-permute-done((f32[1,128]{1,0:T(1,128)S(1)}, f32[1,128]{1,0:T(1,128)S(1)}, u32[]{:S(2)}, u32[]{:S(2)}) %collective-permute-start.1) | collective-permute-done | bytes 544 | tf_op jit(solution)/shard_map/ppermute | solution.py:608
  44.7 16.9 %all_to_all.10 = f32[64,1,128]{2,1,0:T(1,128)S(1)} all-to-all(f32[64,1,128]{2,1,0:T(1,128)S(1)} %broadcast_in_dim.26), channel_id=1, replica_groups=mesh['pw'=64,'mm'=2] {'pw'}, dimensions={0} | all-to-all | bytes 65536 | tf_op jit(solution)/shard_map/all_to_all | solution.py:609
  61.6 2.2 %spread.1 = f32[3,512]{1,0:T(4,128)} custom-call(f32[64,128]{1,0:T(8,128)S(1)} %bitcast.14), custom_call_target="tpu_custom_call" | custom-call | tf_op jit(solution)/shard_map/spread/pallas_call | solution.py:612
  (5 shorter events, 0.1 us)
Async XLA Ops:
  0.6 15.0 %copy-start.4 = (s32[28672]{0:T(1024)S(1)}, s32[28672]{0:T(1024)}, u32[]{:S(2)}) copy-start(s32[28672]{0:T(1024)} %param.9) | copy-start | bytes 344068
  0.6 15.1 %collective-permute-start = (s32[16]{0:T(128)}, s32[16]{0:T(128)S(1)}, u32[]{:S(2)}, u32[]{:S(2)}) collective-permute-start(s32[16]{0:T(128)} %bitcast.17), channel_id=1, source_target_pairs={{0,1},{1,0},{2,3},{3,2},{4,5},{5,4},{6,7},{7,6},{8,9},{9,8},{10,11... | collective-permute-start | bytes 200 | tf_op jit(solution)/shard_map/ppermute | solution.py:516
  0.7 15.0 %copy-start.5 = (s32[1,16]{1,0:T(1,128)S(1)}, s32[1,16]{1,0:T(1,128)}, u32[]{:S(2)}) copy-start(s32[1,16]{1,0:T(1,128)} %param.13) | copy-start | bytes 196
  0.8 15.2 %copy-start.1 = (s32[3,512]{1,0:T(4,128)S(1)}, s32[3,512]{1,0:T(4,128)}, u32[]{:S(2)}) copy-start(s32[3,512]{1,0:T(4,128)} %cell_ref.1) | copy-start | bytes 18436
  0.8 15.2 %copy-start.2 = (f32[3,512]{1,0:T(4,128)S(1)}, f32[3,512]{1,0:T(4,128)}, u32[]{:S(2)}) copy-start(f32[3,512]{1,0:T(4,128)} %frac_ref.1) | copy-start | bytes 18436
  0.8 15.2 %copy-start.3 = (f32[512]{0:T(512)S(1)}, f32[512]{0:T(512)}, u32[]{:S(2)}) copy-start(f32[512]{0:T(512)} %param.12) | copy-start | bytes 6148
  0.8 26.0 %copy-start = (bf16[1536,384]{1,0:T(8,128)(2,1)S(1)}, bf16[1536,384]{1,0:T(8,128)(2,1)}, u32[]{:S(2)}) copy-start(bf16[1536,384]{1,0:T(8,128)(2,1)} %constant.19.clone.table_ref) | copy-start | bytes 3538948
  3.8 23.0 %all-to-all-start = ((f32[64,8,128]{2,1,0:T(8,128)}), f32[64,8,128]{2,1,0:T(8,128)S(1)}, u32[]{:S(2)}, u32[]{:S(2)}) async-start(f32[64,8,128]{2,1,0:T(8,128)} %columns.1), calls=%async_computation | async-start | bytes 524288 | tf_op jit(solution)/shard_map/all_to_all | solution.py:536
  43.4 1.2 %collective-permute-start.1 = (f32[1,128]{1,0:T(1,128)S(1)}, f32[1,128]{1,0:T(1,128)S(1)}, u32[]{:S(2)}, u32[]{:S(2)}) collective-permute-start(f32[1,128]{1,0:T(1,128)S(1)} %get-tuple-element.23), channel_id=1, source_target_pairs={{0,1},{1,0},{2,3},{3,2},{4,5},{5,4},{6,7},{7,6},{8,9},{9,8},{10,11... | collective-permute-start | bytes 1544 | tf_op jit(solution)/shard_map/ppermute | solution.py:608

commit v5 on v4

--- a/solution.py
+++ b/solution.py
@@ -20,7 +20,10 @@
 PEAK = 2.0 / math.sqrt(math.pi)
 EMPTY = N * N
 TILE_CHUNKS = 8
+WINDOW = 208
+BLOCKS = N // 16
 NT = (((1,), (1,)), ((), ()))
+TN = (((0,), (0,)), ((), ()))
 
 
 def split_table(table):
@@ -154,6 +157,7 @@
     list_s,
     cell_s,
     frac_s,
+    charge_s,
     plane_s,
     list_ref,
     cell_ref,
@@ -189,21 +193,42 @@
         cut = slice(piece * LANE, (piece + 1) * LANE)
         owner_ref[:, piece, :] = owned[:, cut]
         owner_ref[:, 4 + piece, :] = owned[:, cut]
-    for values, other, out, start in (
-        (gb[:pairs], turned[:pairs], gb_ref, 4),
-        (gc[:pairs], turned[pairs:], gc_ref, 8),
-    ):
-        merged = jnp.maximum(values, other)
+    merged_b = jnp.maximum(gb[:pairs], turned[:pairs])
+    merged_c = jnp.maximum(gc[:pairs], turned[pairs:])
+    found = jnp.int32(0)
+    for band in range(3):
+        inside = (merged_c >= band * LANE) & (merged_c < (band + 1) * LANE)
+        plan_s[8 + found] = jnp.int32(band)
+        found = found + jnp.max(jnp.where(inside, 1.0, 0.0)).astype(i32)
+    for slot in range(4):
+        plan_s[8 + slot] = jnp.where(slot < found, plan_s[8 + slot], 3)
+    plan_s[2] = (found + 1) // 2
+    alive = merged_b >= 0.0
+    block = jnp.where(alive, merged_b * (1.0 / 16.0), 0.0).astype(i32)
+    used = jnp.left_shift(jnp.where(alive, 1, 0), block)
+    while used.shape[0] > 8:
+        used = used[: used.shape[0] // 2] | used[used.shape[0] // 2 :]
+    while used.shape[1] > LANE:
+        used = used[:, : used.shape[1] // 2] | used[:, used.shape[1] // 2 :]
+    for axis, width in ((0, 8), (1, LANE)):
+        shift = width // 2
+        while shift:
+            used = used | pltpu.roll(used, shift, axis)
+            shift //= 2
+    occupied = jnp.max(used.astype(f32)).astype(i32)
+    start = jnp.int32(-1)
+    for k in range(BLOCKS):
+        outside = sum(1 << ((k + j) % BLOCKS) for j in range(WINDOW // 16, BLOCKS))
+        start = jnp.where((occupied & outside) == 0, k, start)
+    plan_s[1] = jnp.where(start < 0, 2, 1)
+    start = jnp.maximum(start, 0)
+    plan_s[3] = start
+    shifted = merged_b - (16 * start).astype(f32)
+    shifted = jnp.where(shifted < 0.0, shifted + N, shifted)
+    shifted = jnp.where(alive, shifted, -1000.0)
+    for values, out in ((shifted, gb_ref), (merged_c, gc_ref)):
         for piece in range(4):
-            out[piece] = merged[:, piece * LANE : (piece + 1) * LANE]
-        found = jnp.int32(0)
-        for band in range(3):
-            inside = (merged >= band * LANE) & (merged < (band + 1) * LANE)
-            plan_s[start + found] = jnp.int32(band)
-            found = found + jnp.max(jnp.where(inside, 1.0, 0.0)).astype(i32)
-        for slot in range(4):
-            plan_s[start + slot] = jnp.where(slot < found, plan_s[start + slot], 3)
-        plan_s[start // 4] = (found + 1) // 2
+            out[piece] = values[:, piece * LANE : (piece + 1) * LANE]
 
     listed = list_ref[...]
     mask = lax.broadcasted_iota(i32, (LANE, cell_ref.shape[1]), 1) == listed
@@ -241,35 +266,46 @@
     def power(q):
         return jnp.broadcast_to(strength[q : q + 1, :], (8, N))
 
-    def near(q):
-        base = (q // 16) * HALF
+    close = (row_a * row_a < 16.0).astype(f32)
+    lane = lax.broadcasted_iota(i32, (1, LANE), 1)
+    bits = []
+    for half in range(2):
+        weight = jnp.where((lane >= 16 * half) & (lane < 16 * half + 16), 1, 0)
+        weight = jnp.left_shift(weight, lane & 15).astype(f32)
+        bits.append(jnp.sum(close * weight).astype(i32))
+
+    def fix_charge(q):
+        base = (q >> 4) * (HALF // 8)
         own = list_s[q]
-        da = wrap(plane - (cell_s[0, own].astype(f32) + frac_s[0, own]))
-
-        @pl.when(da * da < 16.0)
-        def _():
-            sb = cell_s[1, own].astype(f32) + frac_s[1, own]
-            first = jnp.floor((sb - 16.0) * 0.125).astype(i32)
-
-            def fix(k, _):
-                group = first + k
-                group = jnp.where(group < 0, group + N // 8, group)
-                group = jnp.where(group >= N // 8, group - N // 8, group)
-                i = group - base // 8
-
-                @pl.when((i >= 0) & (i < HALF // 8))
-                def _():
-                    r = pl.multiple_of(8 * group, 8)
-                    u = uab_ref[pl.ds(r, 8), q : q + 1] + wide(uc_ref, q)
-                    k = lax.rsqrt(u)
-                    e = eab_ref[pl.ds(r, 8), q : q + 1] * wide(ec_ref, q)
-                    full = erf(u * k) * k
-                    slope_ref[q, pl.ds(pl.multiple_of(8 * i, 8), 8), :] = k * k * (e - full)
-                    pot_ref[pl.ds(r, 8), :] += power(q) * (full - k)
-
-                return 0
-
-            lax.fori_loop(0, 6, fix, 0)
+        center = [cell_s[axis, own].astype(f32) + frac_s[axis, own] for axis in range(3)]
+        strong = charge_s[0, own]
+        da = wrap(plane - center[0])
+        rest = da * da + SOFTEN
+        dc = wrap(lax.broadcasted_iota(i32, (8, N), 1).astype(f32) - center[2])
+        rest = rest + dc * dc
+        row = lax.broadcasted_iota(i32, (8, N), 0).astype(f32)
+        first = jnp.floor((center[1] - 16.0) * 0.125).astype(i32)
+
+        def fix(step, _):
+            group = first + step
+            group = jnp.where(group < 0, group + N // 8, group)
+            group = jnp.where(group >= N // 8, group - N // 8, group)
+            i = group - base
+
+            @pl.when((i >= 0) & (i < HALF // 8))
+            def _():
+                r = pl.ds(pl.multiple_of(8 * group, 8), 8)
+                db = wrap(row + ((8 * group).astype(f32) - center[1]))
+                u = db * db + rest
+                k = lax.rsqrt(u)
+                full = erf(u * k) * k
+                slope = k * k * (PEAK * jnp.exp(-u) - full)
+                slope_ref[q, pl.ds(pl.multiple_of(8 * i, 8), 8), :] = slope
+                pot_ref[r, :] += strong * (full - k)
+
+            return 0
+
+        lax.fori_loop(0, 6, fix, 0)
 
     copies = []
     for a in range(0, 16, 2):
@@ -285,8 +321,21 @@
                     slope_ref[q, 8 * i : 8 * i + 8, :] = k * k * (e - k)
                     total = strong * k if total is None else total + strong * k
                 pot_ref[r, :] = total if a == 0 else pot_ref[r, :] + total
+        found = [jnp.right_shift(value, a) & 3 for value in bits]
+        found = found[0] + 4 * found[1]
+
+        @pl.when(found > 0)
+        def _(a=a, found=found):
+            def visit(j, _):
+                @pl.when((jnp.right_shift(found, j) & 1) > 0)
+                def _():
+                    fix_charge(16 * (j >> 1) + a + (j & 1))
+
+                return 0
+
+            lax.fori_loop(0, 4, visit, 0)
+
         for q in (a, a + 1, 16 + a, 17 + a):
-            near(q)
             copy = pltpu.make_async_copy(slope_ref.at[q], slope_out.at[q], sems.at[q])
             copy.start()
             copies.append(copy)
@@ -329,11 +378,12 @@
     slope_copy.start()
     pairs = merged_ref.shape[0]
     merged_ref[...] = jnp.where(owner_ref[...] > 0.0, recv_ref[:pairs], recv_ref[pairs:])
-    iota = lax.broadcasted_iota(i32, (LANE, LANE), 0).astype(f32).astype(bf16)
-    one, zero = jnp.ones((LANE, LANE), bf16), jnp.zeros((LANE, LANE), bf16)
-
-    def within(cells, band):
-        return iota == (cells - (LANE * band).astype(f32)).astype(bf16)
+    def counter(rows):
+        return lax.broadcasted_iota(i32, (rows, LANE), 0).astype(f32).astype(bf16)
+
+    iota_b, iota_c = counter(WINDOW), counter(LANE)
+    zero = jnp.zeros((WINDOW, LANE), bf16)
+    one_c, zero_c = jnp.ones((LANE, LANE), bf16), jnp.zeros((LANE, LANE), bf16)
 
     def build(tile, group_b, group_c, val_ref, hot_ref):
         for j in range(TILE_CHUNKS):
@@ -349,12 +399,12 @@
                 parts.append((part, high))
                 parts.append((2 + part, low))
             for h in range(2):
-                hot = within(gc, plan_s[8 + 2 * group_c + h])
-                hot_ref[h * LANE : (h + 1) * LANE, cut] = jnp.where(hot, one, zero)
-                hit = within(gb, plan_s[4 + 2 * group_b + h])
-                for k, v in parts:
-                    top = (4 * h + k) * LANE
-                    val_ref[top : top + LANE, cut] = jnp.where(hit, v, zero)
+                band = (LANE * plan_s[8 + 2 * group_c + h]).astype(f32)
+                hot = iota_c == (gc - band).astype(bf16)
+                hot_ref[h * LANE : (h + 1) * LANE, cut] = jnp.where(hot, one_c, zero_c)
+            hit = iota_b == (gb - WINDOW * jnp.float32(group_b)).astype(bf16)
+            for k, v in parts:
+                val_ref[k * WINDOW : (k + 1) * WINDOW, cut] = jnp.where(hit, v, zero)
 
     acc_ref[0] = jnp.zeros(acc_ref.shape[1:], f32)
     build(0, 0, 0, val_a, hot_a)
@@ -402,13 +452,12 @@
                     tab_ref[level, bottom, :N] = -sin
                     tab_ref[level, bottom, N:] = cos
             combo = 2 * group_b + group_c
-            for h in range(2):
-                for k in range(4):
-                    top = ((k // 2) * 2 + h) * LANE
-                    flow_ref[top : top + LANE, (k % 2) * 2 * LANE : (k % 2 + 1) * 2 * LANE] = acc_ref[
-                        combo, (4 * h + k) * LANE : (4 * h + k + 1) * LANE, :
-                    ].astype(bf16)
-            half = 2 * LANE
+            for k in range(4):
+                top = (k // 2) * WINDOW
+                flow_ref[top : top + WINDOW, (k % 2) * 2 * LANE : (k % 2 + 1) * 2 * LANE] = acc_ref[
+                    combo, k * WINDOW : (k + 1) * WINDOW, :
+                ].astype(bf16)
+            half = WINDOW
             both = mm(flow_ref[...], tab_ref[0])
             result = both[:half] + both[half:] + mm(flow_ref[:half], tab_ref[1])
             pass_ref[...] = result if first else pass_ref[...] + result
@@ -419,14 +468,15 @@
         def _():
             along(1, False)
 
-        for h in range(2):
-            band = jnp.minimum(plan_s[4 + 2 * group_b + h], 2) * LANE
-            edge_ref[:, h * LANE : (h + 1) * LANE] = table_ref[
-                :, pl.ds(pl.multiple_of(band, LANE), LANE)
-            ]
+        for j in range(WINDOW // 16):
+            block = plan_s[3] + (group_b * WINDOW) // 16 + j
+            block = jnp.where(block >= BLOCKS, block - BLOCKS, block)
+            for k in range(4):
+                row = pl.multiple_of(k * N + 16 * block, 16)
+                edge_ref[16 * j : 16 * j + 16, k * N : (k + 1) * N] = table_ref[pl.ds(row, 16), :]
         high, low = halves(pass_ref[...])
-        result = mm(edge_ref[: 2 * N], high) + (
-            mm(edge_ref[2 * N :], high) + mm(edge_ref[: 2 * N], low)
+        result = mm(edge_ref[:, : 2 * N], high, TN) + (
+            mm(edge_ref[:, 2 * N :], high, TN) + mm(edge_ref[:, : 2 * N], low, TN)
         )
         mid_ref[...] = result if group_b == 0 else mid_ref[...] + result
 
@@ -512,12 +562,6 @@
     plane = lax.axis_index("pw").astype(i32)
     first_table, second_table = tables(planes)
 
-    own = tile_list[0]
-    other = lax.ppermute(own, "mm", [(0, 1), (1, 0)])
-    first = lax.axis_index("mm") == 0
-    listed = jnp.concatenate([jnp.where(first, own, other), jnp.where(first, other, own)])
-    listed_col = jnp.pad(listed, (0, LANE - 32), constant_values=-1)[:, None]
-
     sent = pl.pallas_call(
         columns_kernel,
         out_shape=jax.ShapeDtypeStruct((planes, 8, LANE), f32),
@@ -530,9 +574,15 @@
             pltpu.VMEM((4 * LANE, 2 * N), bf16),
             pltpu.SemaphoreType.DMA((5,)),
         ],
-        compiler_params=params(60),
+        compiler_params=params(54),
         name="columns",
     )(plane[None], coefficients.reshape(2, slots, N), jnp.asarray(first_table))
+    own, sent = lax.optimization_barrier((tile_list[0], sent))
+    other = lax.ppermute(own, "mm", [(0, 1), (1, 0)])
+    first = lax.axis_index("mm") == 0
+    listed = jnp.concatenate([jnp.where(first, own, other), jnp.where(first, other, own)])
+    listed_col = jnp.pad(listed, (0, LANE - 32), constant_values=-1)[:, None]
+
     recv = lax.all_to_all(sent, "pw", 0, 0, tiled=True)
 
     blocks = col_map.reshape(sources, slots)
@@ -551,7 +601,7 @@
             jax.ShapeDtypeStruct((sources // 2, 8, LANE), f32),
             jax.ShapeDtypeStruct((16,), i32),
         ),
-        in_specs=smem(4) + vmem(5),
+        in_specs=smem(5) + vmem(5),
         out_specs=tuple(vmem(1) + anywhere(1) + vmem(6) + smem(1)),
         scratch_shapes=[
             pltpu.VMEM((N, LANE), f32),
@@ -567,6 +617,7 @@
         listed,
         charge_cell,
         charge_frac,
+        charge[None],
         plane[None],
         listed_col,
         charge_cell,
@@ -584,15 +635,15 @@
         in_specs=smem(1) + vmem(6) + anywhere(1) + vmem(3),
         out_specs=tuple(anywhere(1) + vmem(1)),
         scratch_shapes=[
-            pltpu.VMEM((4, 8 * LANE, 2 * LANE), f32),
-            pltpu.VMEM((8 * LANE, TILE_CHUNKS * LANE), bf16),
-            pltpu.VMEM((8 * LANE, TILE_CHUNKS * LANE), bf16),
+            pltpu.VMEM((4, 4 * WINDOW, 2 * LANE), f32),
+            pltpu.VMEM((4 * WINDOW, TILE_CHUNKS * LANE), bf16),
+            pltpu.VMEM((4 * WINDOW, TILE_CHUNKS * LANE), bf16),
             pltpu.VMEM((2 * LANE, TILE_CHUNKS * LANE), bf16),
             pltpu.VMEM((2 * LANE, TILE_CHUNKS * LANE), bf16),
             pltpu.VMEM((2, 4 * LANE, 2 * N), bf16),
-            pltpu.VMEM((4 * LANE, 4 * LANE), bf16),
-            pltpu.VMEM((4 * N, 2 * LANE), bf16),
-            pltpu.VMEM((2 * LANE, 2 * N), f32),
+            pltpu.VMEM((2 * WINDOW, 4 * LANE), bf16),
+            pltpu.VMEM((WINDOW, 4 * N), bf16),
+            pltpu.VMEM((WINDOW, 2 * N), f32),
             pltpu.VMEM((2 * N, 2 * N), f32),
             pltpu.VMEM((N, N), f32),
             pltpu.VMEM((64, N), f32),

time: 64.1 us -> 62.5 us (0.975)
  Pallas kernels: 30.2 us -> 27.8 us
  blocking collectives: 16.9 us -> 18.1 us
    pallas_call x1, Pallas kernels: 16.6 us -> 14.7 us  [local(): pl.pallas_call(grid_kernel, out_shape=(jax.ShapeDtypeStruct((2, N, N), f3...]
    all_to_all x1, waiting for transfers between devices: 2.45 us -> 1.25 us  [local(): recv = lax.all_to_all(sent, 'pw', 0, 0, tiled=True)]
    all_to_all x1, blocking collectives: 16.9 us -> 18.1 us  [local(): lax.all_to_all(jnp.broadcast_to(push[None], (sources, 1, LANE)), 'pw', 0,...]
    ppermute x1, waiting for transfers between devices: 0.01 us -> 1.02 us  [local(): other = lax.ppermute(own, 'mm', [(0, 1), (1, 0)])]
  transfers between devices with their start and end apart: 3 -> 3, of which waited for: 2 -> 3; matrix products, arithmetic and copies ran while one was open for 0% -> 0% of each run, Pallas kernels for 18% -> 13%
where the time goes in v5:
time: 62.5 us; the launch traced here: 62.4 us
  Pallas kernels  27.8 us (44%)
  blocking collectives  18.1 us (29%)
  starting transfers between devices  12 us (19%)
  waiting for transfers between devices  3.42 us (5%)
  between operations  0.79 us (1%)
    all_to_all x1, blocking collectives, local(): lax.all_to_all(jnp.broadcast_to(push[None], (sources, 1, LANE)), 'pw', 0,...  18.1 us
    pallas_call x1, Pallas kernels, local(): pl.pallas_call(grid_kernel, out_shape=(jax.ShapeDtypeStruct((2, N, N), f3...  14.7 us
    all_to_all x1, starting transfers between devices, local(): recv = lax.all_to_all(sent, 'pw', 0, 0, tiled=True)  11.8 us
    pallas_call x1, Pallas kernels, local(): pl.pallas_call(charges_kernel, out_shape=(jax.ShapeDtypeStruct((N, N), f3...  7.86 us
    pallas_call x1, Pallas kernels, local(): pl.pallas_call(columns_kernel, out_shape=jax.ShapeDtypeStruct((planes, 8,...  3 us
    pallas_call x1, Pallas kernels, local(): pl.pallas_call(spread_kernel, out_shape=jax.ShapeDtypeStruct((3, charge.s...  2.24 us
    all_to_all x1, waiting for transfers between devices, local(): recv = lax.all_to_all(sent, 'pw', 0, 0, tiled=True)  1.25 us
  transfers between devices with their start and end apart: 3, of which 3 were waited for; matrix products, arithmetic and copies ran while one was open for 0% of the time, Pallas kernels for 13%

profile of v5, /device:TPU:0, one launch (start us, length us, event | category | flops | bytes accessed | tf_op | source)
XLA Modules:
  0.0 62.4 jit_solution(415976460031149492)
XLA Ops:
  0.6 0.0 copy-start.5
  0.6 0.0 copy-start.4
  0.7 0.0 copy-start.1
  0.7 0.0 copy-start.2
  0.7 0.0 copy-start.3
  0.7 0.0 copy-start
  0.7 3.0 %columns.1 = f32[64,8,128]{2,1,0:T(8,128)} custom-call(s32[1]{0:T(128)} %bitcast.1.plane_s, f32[2,448,384]{2,1,0:T(8,128)} %bitcast.15, bf16[256,768]{1,0:T(8,128)(2,1)} %constant.18.clone.table_in), custom_call_target="tpu_custom_call" | custom-call | tf_op jit(solution)/shard_map/columns/pallas_call | solution.py:565
  3.7 11.8 %all-to-all-start = ((f32[64,8,128]{2,1,0:T(8,128)}), f32[64,8,128]{2,1,0:T(8,128)S(1)}, u32[]{:S(2)}, u32[]{:S(2)}) async-start(f32[64,8,128]{2,1,0:T(8,128)} %columns.1), calls=%async_computation | async-start | bytes 524288 | tf_op jit(solution)/shard_map/all_to_all | solution.py:586
  15.5 0.0 copy-done.5
  15.5 0.1 collective-permute-start
  15.6 0.0 copy-done.4
  15.6 0.1 reshape.17
  15.7 1.0 %collective-permute-done = s32[16]{0:T(128)S(1)} collective-permute-done((s32[16]{0:T(128)S(1)}, s32[16]{0:T(128)S(1)}, u32[]{:S(2)}, u32[]{:S(2)}) %collective-permute-start) | collective-permute-done | bytes 96 | tf_op jit(solution)/shard_map/ppermute | solution.py:581
  16.8 0.1 pad_add_fusion.list_s
  16.9 0.1 copy.12.list_ref
  17.0 0.0 copy-done.1
  17.0 0.0 copy-done.2
  17.0 0.0 copy-done.3
  17.0 7.9 %charges.1 = (f32[384,384]{1,0:T(8,128)S(1)}, f32[32,192,384]{2,1,0:T(8,128)}, f32[384,128]{1,0:T(8,128)S(1)}, f32[32,384]{1,0:T(8,128)S(1)}, f32[128,8]{1,0:T(8...) custom-call(s32[32]{0:T(128)S(1)} %pad_add_fusion.list_s, ...), custom_call_target="tpu_custom_call" | custom-call | tf_op jit(solution)/shard_map/charges/pallas_call | solution.py:591
  24.9 1.3 %all-to-all-done.recv_ref = f32[64,8,128]{2,1,0:T(8,128)S(1)} async-done(((f32[64,8,128]{2,1,0:T(8,128)}), f32[64,8,128]{2,1,0:T(8,128)S(1)}, u32[]{:S(2)}, u32[]{:S(2)}) %all-to-all-start) | async-done | bytes 262176 | tf_op jit(solution)/shard_map/all_to_all | solution.py:586
  26.1 0.0 copy-done
  26.1 14.7 %grid.1 = (f32[2,384,384]{2,1,0:T(8,128)}, f32[1,128]{1,0:T(1,128)S(1)}) custom-call(s32[16]{0:T(128)S(1)} %get-tuple-element.16.plan_s, f32[64,8,128]{2,1,0:T(8,128)S(1)} %all-to-all-done.recv_ref, f32[32,8,128]{2,1,0:T(8,128)S(1)} %get-tuple-element.18.owner_ref, f32[4,32,128]{2,1,0:T(8,128)S(1)} %get-tuple-element.19.gb_ref, ...), custom_call_target="tpu_custom_call" | custom-call | tf_op jit(solution)/shard_map/grid/pallas_call | solution.py:629
  40.8 0.1 collective-permute-start.1
  40.9 1.1 %collective-permute-done.1 = f32[1,128]{1,0:T(1,128)S(1)} collective-permute-done((f32[1,128]{1,0:T(1,128)S(1)}, f32[1,128]{1,0:T(1,128)S(1)}, u32[]{:S(2)}, u32[]{:S(2)}) %collective-permute-start.1) | collective-permute-done | bytes 544 | tf_op jit(solution)/shard_map/ppermute | solution.py:659
  42.1 18.1 %all_to_all.10 = f32[64,1,128]{2,1,0:T(1,128)S(1)} all-to-all(f32[64,1,128]{2,1,0:T(1,128)S(1)} %broadcast_in_dim.27), channel_id=1, replica_groups=mesh['pw'=64,'mm'=2] {'pw'}, dimensions={0} | all-to-all | bytes 65536 | tf_op jit(solution)/shard_map/all_to_all | solution.py:660
  60.2 2.2 %spread.1 = f32[3,512]{1,0:T(4,128)} custom-call(f32[64,128]{1,0:T(8,128)S(1)} %bitcast.12), custom_call_target="tpu_custom_call" | custom-call | tf_op jit(solution)/shard_map/spread/pallas_call | solution.py:663
  (5 shorter events, 0.0 us)
Async XLA Ops:
  0.6 14.9 %copy-start.5 = (s32[1,16]{1,0:T(1,128)S(1)}, s32[1,16]{1,0:T(1,128)}, u32[]{:S(2)}) copy-start(s32[1,16]{1,0:T(1,128)} %param.13) | copy-start | bytes 196
  0.6 15.0 %copy-start.4 = (s32[28672]{0:T(1024)S(1)}, s32[28672]{0:T(1024)}, u32[]{:S(2)}) copy-start(s32[28672]{0:T(1024)} %param.9) | copy-start | bytes 344068
  0.7 16.3 %copy-start.1 = (s32[3,512]{1,0:T(4,128)S(1)}, s32[3,512]{1,0:T(4,128)}, u32[]{:S(2)}) copy-start(s32[3,512]{1,0:T(4,128)} %cell_ref.1) | copy-start | bytes 18436
  0.7 16.3 %copy-start.2 = (f32[3,512]{1,0:T(4,128)S(1)}, f32[3,512]{1,0:T(4,128)}, u32[]{:S(2)}) copy-start(f32[3,512]{1,0:T(4,128)} %frac_ref.1) | copy-start | bytes 18436
  0.7 16.3 %copy-start.3 = (f32[512]{0:T(512)S(1)}, f32[512]{0:T(512)}, u32[]{:S(2)}) copy-start(f32[512]{0:T(512)} %param.12) | copy-start | bytes 6148
  0.7 25.4 %copy-start = (bf16[1536,384]{1,0:T(8,128)(2,1)S(1)}, bf16[1536,384]{1,0:T(8,128)(2,1)}, u32[]{:S(2)}) copy-start(bf16[1536,384]{1,0:T(8,128)(2,1)} %constant.19.clone.table_ref) | copy-start | bytes 3538948
  3.7 22.4 %all-to-all-start = ((f32[64,8,128]{2,1,0:T(8,128)}), f32[64,8,128]{2,1,0:T(8,128)S(1)}, u32[]{:S(2)}, u32[]{:S(2)}) async-start(f32[64,8,128]{2,1,0:T(8,128)} %columns.1), calls=%async_computation | async-start | bytes 524288 | tf_op jit(solution)/shard_map/all_to_all | solution.py:586
  15.5 1.2 %collective-permute-start = (s32[16]{0:T(128)S(1)}, s32[16]{0:T(128)S(1)}, u32[]{:S(2)}, u32[]{:S(2)}) collective-permute-start(s32[16]{0:T(128)S(1)} %bitcast.16), channel_id=1, source_target_pairs={{0,1},{1,0},{2,3},{3,2},{4,5},{5,4},{6,7},{7,6},{8,9},{9,8},{10,11... | collective-permute-start | bytes 200 | tf_op jit(solution)/shard_map/ppermute | solution.py:581
  40.8 1.2 %collective-permute-start.1 = (f32[1,128]{1,0:T(1,128)S(1)}, f32[1,128]{1,0:T(1,128)S(1)}, u32[]{:S(2)}, u32[]{:S(2)}) collective-permute-start(f32[1,128]{1,0:T(1,128)S(1)} %get-tuple-element.27), channel_id=1, source_target_pairs={{0,1},{1,0},{2,3},{3,2},{4,5},{5,4},{6,7},{7,6},{8,9},{9,8},{10,11... | collective-permute-start | bytes 1544 | tf_op jit(solution)/shard_map/ppermute | solution.py:659

commit v6 on v5

--- a/solution.py
+++ b/solution.py
@@ -358,10 +358,6 @@
     field_out,
     push_ref,
     acc_ref,
-    val_a,
-    val_b,
-    hot_a,
-    hot_b,
     tab_ref,
     flow_ref,
     edge_ref,
@@ -385,35 +381,30 @@
     zero = jnp.zeros((WINDOW, LANE), bf16)
     one_c, zero_c = jnp.ones((LANE, LANE), bf16), jnp.zeros((LANE, LANE), bf16)
 
-    def build(tile, group_b, group_c, val_ref, hot_ref):
+    def product(tile, group_b, group_c):
+        columns, weights = [], []
         for j in range(TILE_CHUNKS):
-            pair = jnp.minimum(tile * (TILE_CHUNKS // 4) + j // 4, pairs - 1)
+            pair = tile * (TILE_CHUNKS // 4) + j // 4
             piece = j % 4
-            cut = slice(j * LANE, (j + 1) * LANE)
             gb = gb_ref[piece, pl.ds(pair, 1), :]
             gc = gc_ref[piece, pl.ds(pair, 1), :]
-            parts = []
+            parts = [None] * 4
             for part in range(2):
                 value = merged_ref[pair, 4 * part + piece : 4 * part + piece + 1, :]
-                high, low = halves(value)
-                parts.append((part, high))
-                parts.append((2 + part, low))
+                parts[part], parts[2 + part] = halves(value)
+            hots = []
             for h in range(2):
                 band = (LANE * plan_s[8 + 2 * group_c + h]).astype(f32)
-                hot = iota_c == (gc - band).astype(bf16)
-                hot_ref[h * LANE : (h + 1) * LANE, cut] = jnp.where(hot, one_c, zero_c)
-            hit = iota_b == (gb - WINDOW * jnp.float32(group_b)).astype(bf16)
-            for k, v in parts:
-                val_ref[k * WINDOW : (k + 1) * WINDOW, cut] = jnp.where(hit, v, zero)
+                hots.append(jnp.where(iota_c == (gc - band).astype(bf16), one_c, zero_c))
+            weights.append(jnp.concatenate(hots, axis=0))
+            hit = iota_b == (gb - WINDOW * jnp.asarray(group_b).astype(f32)).astype(bf16)
+            columns.append(jnp.concatenate([jnp.where(hit, v, zero) for v in parts], axis=0))
+        return mm(jnp.concatenate(columns, axis=1), jnp.concatenate(weights, axis=1), NT)
 
     acc_ref[0] = jnp.zeros(acc_ref.shape[1:], f32)
-    build(0, 0, 0, val_a, hot_a)
-
     def step(t, _):
-        acc_ref[0] += mm(val_a[...], hot_a[...], NT)
-        build(2 * t + 1, 0, 0, val_b, hot_b)
-        acc_ref[0] += mm(val_b[...], hot_b[...], NT)
-        build(2 * t + 2, 0, 0, val_a, hot_a)
+        acc_ref[0] += product(2 * t, 0, 0)
+        acc_ref[0] += product(2 * t + 1, 0, 0)
         return 0
 
     steps = 2 * pairs // TILE_CHUNKS
@@ -427,8 +418,7 @@
             acc_ref[combo] = jnp.zeros(acc_ref.shape[1:], f32)
 
             def extra(t, _):
-                build(t, group_b, group_c, val_a, hot_a)
-                acc_ref[combo] += mm(val_a[...], hot_a[...], NT)
+                acc_ref[combo] += product(t, group_b, group_c)
                 return 0
 
             lax.fori_loop(0, 2 * steps, extra, 0)
@@ -636,10 +626,6 @@
         out_specs=tuple(anywhere(1) + vmem(1)),
         scratch_shapes=[
             pltpu.VMEM((4, 4 * WINDOW, 2 * LANE), f32),
-            pltpu.VMEM((4 * WINDOW, TILE_CHUNKS * LANE), bf16),
-            pltpu.VMEM((4 * WINDOW, TILE_CHUNKS * LANE), bf16),
-            pltpu.VMEM((2 * LANE, TILE_CHUNKS * LANE), bf16),
-            pltpu.VMEM((2 * LANE, TILE_CHUNKS * LANE), bf16),
             pltpu.VMEM((2, 4 * LANE, 2 * N), bf16),
             pltpu.VMEM((2 * WINDOW, 4 * LANE), bf16),
             pltpu.VMEM((WINDOW, 4 * N), bf16),

time: 62.5 us -> 61.7 us (0.987)
  Pallas kernels: 27.8 us -> 25.4 us
  waiting for transfers between devices: 3.42 us -> 4.35 us
    pallas_call x1, Pallas kernels: 14.7 us -> 13.2 us  [local(): pl.pallas_call(grid_kernel, out_shape=(jax.ShapeDtypeStruct((2, N, N), f3...]
    all_to_all x1, waiting for transfers between devices: 1.25 us -> 2.18 us  [local(): recv = lax.all_to_all(sent, 'pw', 0, 0, tiled=True)]
    pallas_call x1, Pallas kernels: 7.86 us -> 6.94 us  [local(): pl.pallas_call(charges_kernel, out_shape=(jax.ShapeDtypeStruct((N, N), f3...]
  transfers between devices with their start and end apart: 3 -> 3, of which waited for: 3 -> 3; matrix products, arithmetic and copies ran while one was open for 0% -> 0% of each run, Pallas kernels for 13% -> 11%
where the time goes in v6:
time: 61.7 us; the launch traced here: 61.5 us
  Pallas kernels  25.4 us (41%)
  blocking collectives  18.6 us (30%)
  starting transfers between devices  12 us (19%)
  waiting for transfers between devices  4.35 us (7%)
  between operations  0.79 us (1%)
    all_to_all x1, blocking collectives, local(): lax.all_to_all(jnp.broadcast_to(push[None], (sources, 1, LANE)), 'pw', 0,...  18.6 us
    pallas_call x1, Pallas kernels, local(): pl.pallas_call(grid_kernel, out_shape=(jax.ShapeDtypeStruct((2, N, N), f3...  13.2 us
    all_to_all x1, starting transfers between devices, local(): recv = lax.all_to_all(sent, 'pw', 0, 0, tiled=True)  11.8 us
    pallas_call x1, Pallas kernels, local(): pl.pallas_call(charges_kernel, out_shape=(jax.ShapeDtypeStruct((N, N), f3...  6.94 us
    pallas_call x1, Pallas kernels, local(): pl.pallas_call(columns_kernel, out_shape=jax.ShapeDtypeStruct((planes, 8,...  3 us
    pallas_call x1, Pallas kernels, local(): pl.pallas_call(spread_kernel, out_shape=jax.ShapeDtypeStruct((3, charge.s...  2.24 us
    all_to_all x1, waiting for transfers between devices, local(): recv = lax.all_to_all(sent, 'pw', 0, 0, tiled=True)  2.18 us
  transfers between devices with their start and end apart: 3, of which 3 were waited for; matrix products, arithmetic and copies ran while one was open for 0% of the time, Pallas kernels for 11%

profile of v6, /device:TPU:0, one launch (start us, length us, event | category | flops | bytes accessed | tf_op | source)
XLA Modules:
  0.0 61.5 jit_solution(3399453110704551170)
XLA Ops:
  0.6 0.0 copy-start.5
  0.6 0.0 copy-start.4
  0.7 0.0 copy-start.1
  0.7 0.0 copy-start.2
  0.7 0.0 copy-start.3
  0.7 0.0 copy-start
  0.7 3.0 %columns.1 = f32[64,8,128]{2,1,0:T(8,128)} custom-call(s32[1]{0:T(128)} %bitcast.1.plane_s, f32[2,448,384]{2,1,0:T(8,128)} %bitcast.15, bf16[256,768]{1,0:T(8,128)(2,1)} %constant.18.clone.table_in), custom_call_target="tpu_custom_call" | custom-call | tf_op jit(solution)/shard_map/columns/pallas_call | solution.py:555
  3.7 11.8 %all-to-all-start = ((f32[64,8,128]{2,1,0:T(8,128)}), f32[64,8,128]{2,1,0:T(8,128)S(1)}, u32[]{:S(2)}, u32[]{:S(2)}) async-start(f32[64,8,128]{2,1,0:T(8,128)} %columns.1), calls=%async_computation | async-start | bytes 524288 | tf_op jit(solution)/shard_map/all_to_all | solution.py:576
  15.5 0.0 copy-done.5
  15.5 0.1 collective-permute-start
  15.6 0.0 copy-done.4
  15.6 0.1 reshape.17
  15.7 1.0 %collective-permute-done = s32[16]{0:T(128)S(1)} collective-permute-done((s32[16]{0:T(128)S(1)}, s32[16]{0:T(128)S(1)}, u32[]{:S(2)}, u32[]{:S(2)}) %collective-permute-start) | collective-permute-done | bytes 96 | tf_op jit(solution)/shard_map/ppermute | solution.py:571
  16.8 0.1 pad_add_fusion.list_s
  16.9 0.1 copy.12.list_ref
  17.0 0.0 copy-done.1
  17.0 0.0 copy-done.2
  17.0 0.0 copy-done.3
  17.0 6.9 %charges.1 = (f32[384,384]{1,0:T(8,128)S(1)}, f32[32,192,384]{2,1,0:T(8,128)}, f32[384,128]{1,0:T(8,128)S(1)}, f32[32,384]{1,0:T(8,128)S(1)}, f32[128,8]{1,0:T(8...) custom-call(s32[32]{0:T(128)S(1)} %pad_add_fusion.list_s, ...), custom_call_target="tpu_custom_call" | custom-call | tf_op jit(solution)/shard_map/charges/pallas_call | solution.py:581
  23.9 2.2 %all-to-all-done.recv_ref = f32[64,8,128]{2,1,0:T(8,128)S(1)} async-done(((f32[64,8,128]{2,1,0:T(8,128)}), f32[64,8,128]{2,1,0:T(8,128)S(1)}, u32[]{:S(2)}, u32[]{:S(2)}) %all-to-all-start) | async-done | bytes 262176 | tf_op jit(solution)/shard_map/all_to_all | solution.py:576
  26.1 0.0 copy-done
  26.1 13.2 %grid.1 = (f32[2,384,384]{2,1,0:T(8,128)}, f32[1,128]{1,0:T(1,128)S(1)}) custom-call(s32[16]{0:T(128)S(1)} %get-tuple-element.16.plan_s, f32[64,8,128]{2,1,0:T(8,128)S(1)} %all-to-all-done.recv_ref, f32[32,8,128]{2,1,0:T(8,128)S(1)} %get-tuple-element.18.owner_ref, f32[4,32,128]{2,1,0:T(8,128)S(1)} %get-tuple-element.19.gb_ref, ...), custom_call_target="tpu_custom_call" | custom-call | tf_op jit(solution)/shard_map/grid/pallas_call | solution.py:619
  39.4 0.1 collective-permute-start.1
  39.5 1.1 %collective-permute-done.1 = f32[1,128]{1,0:T(1,128)S(1)} collective-permute-done((f32[1,128]{1,0:T(1,128)S(1)}, f32[1,128]{1,0:T(1,128)S(1)}, u32[]{:S(2)}, u32[]{:S(2)}) %collective-permute-start.1) | collective-permute-done | bytes 544 | tf_op jit(solution)/shard_map/ppermute | solution.py:645
  40.6 18.6 %all_to_all.10 = f32[64,1,128]{2,1,0:T(1,128)S(1)} all-to-all(f32[64,1,128]{2,1,0:T(1,128)S(1)} %broadcast_in_dim.27), channel_id=1, replica_groups=mesh['pw'=64,'mm'=2] {'pw'}, dimensions={0} | all-to-all | bytes 65536 | tf_op jit(solution)/shard_map/all_to_all | solution.py:646
  59.3 2.2 %spread.1 = f32[3,512]{1,0:T(4,128)} custom-call(f32[64,128]{1,0:T(8,128)S(1)} %bitcast.12), custom_call_target="tpu_custom_call" | custom-call | tf_op jit(solution)/shard_map/spread/pallas_call | solution.py:649
  (5 shorter events, 0.0 us)
Async XLA Ops:
  0.6 14.9 %copy-start.5 = (s32[1,16]{1,0:T(1,128)S(1)}, s32[1,16]{1,0:T(1,128)}, u32[]{:S(2)}) copy-start(s32[1,16]{1,0:T(1,128)} %param.13) | copy-start | bytes 196
  0.6 15.0 %copy-start.4 = (s32[28672]{0:T(1024)S(1)}, s32[28672]{0:T(1024)}, u32[]{:S(2)}) copy-start(s32[28672]{0:T(1024)} %param.9) | copy-start | bytes 344068
  0.7 16.3 %copy-start.1 = (s32[3,512]{1,0:T(4,128)S(1)}, s32[3,512]{1,0:T(4,128)}, u32[]{:S(2)}) copy-start(s32[3,512]{1,0:T(4,128)} %cell_ref.1) | copy-start | bytes 18436
  0.7 16.3 %copy-start.2 = (f32[3,512]{1,0:T(4,128)S(1)}, f32[3,512]{1,0:T(4,128)}, u32[]{:S(2)}) copy-start(f32[3,512]{1,0:T(4,128)} %frac_ref.1) | copy-start | bytes 18436
  0.7 16.3 %copy-start.3 = (f32[512]{0:T(512)S(1)}, f32[512]{0:T(512)}, u32[]{:S(2)}) copy-start(f32[512]{0:T(512)} %param.12) | copy-start | bytes 6148
  0.7 25.4 %copy-start = (bf16[1536,384]{1,0:T(8,128)(2,1)S(1)}, bf16[1536,384]{1,0:T(8,128)(2,1)}, u32[]{:S(2)}) copy-start(bf16[1536,384]{1,0:T(8,128)(2,1)} %constant.19.clone.table_ref) | copy-start | bytes 3538948
  3.7 22.4 %all-to-all-start = ((f32[64,8,128]{2,1,0:T(8,128)}), f32[64,8,128]{2,1,0:T(8,128)S(1)}, u32[]{:S(2)}, u32[]{:S(2)}) async-start(f32[64,8,128]{2,1,0:T(8,128)} %columns.1), calls=%async_computation | async-start | bytes 524288 | tf_op jit(solution)/shard_map/all_to_all | solution.py:576
  15.5 1.2 %collective-permute-start = (s32[16]{0:T(128)S(1)}, s32[16]{0:T(128)S(1)}, u32[]{:S(2)}, u32[]{:S(2)}) collective-permute-start(s32[16]{0:T(128)S(1)} %bitcast.16), channel_id=1, source_target_pairs={{0,1},{1,0},{2,3},{3,2},{4,5},{5,4},{6,7},{7,6},{8,9},{9,8},{10,11... | collective-permute-start | bytes 200 | tf_op jit(solution)/shard_map/ppermute | solution.py:571
  39.4 1.2 %collective-permute-start.1 = (f32[1,128]{1,0:T(1,128)S(1)}, f32[1,128]{1,0:T(1,128)S(1)}, u32[]{:S(2)}, u32[]{:S(2)}) collective-permute-start(f32[1,128]{1,0:T(1,128)S(1)} %get-tuple-element.27), channel_id=1, source_target_pairs={{0,1},{1,0},{2,3},{3,2},{4,5},{5,4},{6,7},{7,6},{8,9},{9,8},{10,11... | collective-permute-start | bytes 1544 | tf_op jit(solution)/shard_map/ppermute | solution.py:645

commit v7 on v6

--- a/solution.py
+++ b/solution.py
@@ -19,7 +19,7 @@
 VOLUME = SPACING**3
 PEAK = 2.0 / math.sqrt(math.pi)
 EMPTY = N * N
-TILE_CHUNKS = 8
+TILE_CHUNKS = 32
 WINDOW = 208
 BLOCKS = N // 16
 NT = (((1,), (1,)), ((), ()))
@@ -153,33 +153,7 @@
     return s * num / den
 
 
-def charges_kernel(
-    list_s,
-    cell_s,
-    frac_s,
-    charge_s,
-    plane_s,
-    list_ref,
-    cell_ref,
-    frac_ref,
-    charge_ref,
-    grid_ref,
-    pot_ref,
-    slope_out,
-    offb_ref,
-    offc_ref,
-    col_ref,
-    gb_ref,
-    gc_ref,
-    owner_ref,
-    plan_s,
-    uab_ref,
-    eab_ref,
-    uc_ref,
-    ec_ref,
-    slope_ref,
-    sems,
-):
+def sort_cells(grid_ref, gb_ref, gc_ref, owner_ref, plan_s):
     cells = grid_ref[...]
     pairs = cells.shape[0] // 2
     row = jnp.floor((cells.astype(f32) + 0.5) * (1.0 / N))
@@ -230,6 +204,28 @@
         for piece in range(4):
             out[piece] = values[:, piece * LANE : (piece + 1) * LANE]
 
+
+def charges_kernel(
+    list_s,
+    cell_s,
+    frac_s,
+    charge_s,
+    place_s,
+    list_ref,
+    cell_ref,
+    frac_ref,
+    charge_ref,
+    *refs,
+):
+    refs = list(refs)
+    grid_ref = refs.pop(0) if len(refs) > 11 else None
+    pot_ref, slope_out, offb_ref, offc_ref, col_ref = refs[:5]
+    if grid_ref is not None:
+        sort_cells(grid_ref, *refs[5:9])
+    uab_ref, eab_ref, uc_ref, ec_ref, slope_ref, sems = refs[-6:]
+    plane = place_s[0].astype(f32)
+    tile = place_s[1]
+    start_row = (tile * HALF).astype(f32)
     listed = list_ref[...]
     mask = lax.broadcasted_iota(i32, (LANE, cell_ref.shape[1]), 1) == listed
     center = cell_ref[...].astype(f32) + frac_ref[...]
@@ -239,12 +235,11 @@
 
     ca, cb, cc = (pick(center[i : i + 1]) for i in range(3))
     strength = pick(charge_ref[...])
-    plane = plane_s[0].astype(f32)
     off_a = wrap(plane - ca)
     col_ref[...] = jnp.concatenate(
         [off_a, strength, listed.astype(f32)] + [jnp.zeros((LANE, 5), f32)], axis=1
     )
-    off_c = wrap(lax.broadcasted_iota(i32, (32, N), 1).astype(f32) - cc[:32])
+    off_c = wrap(lax.broadcasted_iota(i32, (16, N), 1).astype(f32) - cc[:16])
     offc_ref[...] = off_c
     sq_c = off_c * off_c
     uc_ref[...] = sq_c
@@ -253,7 +248,8 @@
     def across(column):
         return jnp.transpose(jnp.broadcast_to(column, (LANE, LANE)))[:1]
 
-    off_b = wrap(lax.broadcasted_iota(i32, (N, LANE), 0).astype(f32) - across(cb))
+    row = lax.broadcasted_iota(i32, (HALF, LANE), 0).astype(f32) + start_row
+    off_b = wrap(row - across(cb))
     offb_ref[...] = off_b
     row_a = across(off_a)
     uab = off_b * off_b + (row_a * row_a + SOFTEN)
@@ -268,14 +264,16 @@
 
     close = (row_a * row_a < 16.0).astype(f32)
     lane = lax.broadcasted_iota(i32, (1, LANE), 1)
-    bits = []
-    for half in range(2):
-        weight = jnp.where((lane >= 16 * half) & (lane < 16 * half + 16), 1, 0)
-        weight = jnp.left_shift(weight, lane & 15).astype(f32)
-        bits.append(jnp.sum(close * weight).astype(i32))
+    weight = jnp.left_shift(jnp.where(lane < 16, 1, 0), lane & 15).astype(f32)
+    bits = jnp.sum(close * weight).astype(i32)
+
+    def wide(ref, q):
+        return jnp.broadcast_to(ref[q : q + 1, :], (8, N))
+
+    def power(q):
+        return jnp.broadcast_to(strength[q : q + 1, :], (8, N))
 
     def fix_charge(q):
-        base = (q >> 4) * (HALF // 8)
         own = list_s[q]
         center = [cell_s[axis, own].astype(f32) + frac_s[axis, own] for axis in range(3)]
         strong = charge_s[0, own]
@@ -290,17 +288,17 @@
             group = first + step
             group = jnp.where(group < 0, group + N // 8, group)
             group = jnp.where(group >= N // 8, group - N // 8, group)
-            i = group - base
+            i = group - tile * (HALF // 8)
 
             @pl.when((i >= 0) & (i < HALF // 8))
             def _():
-                r = pl.ds(pl.multiple_of(8 * group, 8), 8)
+                r = pl.ds(pl.multiple_of(8 * i, 8), 8)
                 db = wrap(row + ((8 * group).astype(f32) - center[1]))
                 u = db * db + rest
                 k = lax.rsqrt(u)
                 full = erf(u * k) * k
                 slope = k * k * (PEAK * jnp.exp(-u) - full)
-                slope_ref[q, pl.ds(pl.multiple_of(8 * i, 8), 8), :] = slope
+                slope_ref[q, r, :] = slope
                 pot_ref[r, :] += strong * (full - k)
 
             return 0
@@ -308,34 +306,31 @@
         lax.fori_loop(0, 6, fix, 0)
 
     copies = []
-    for a in range(0, 16, 2):
-        for half in range(2):
-            pair = (16 * half + a, 16 * half + a + 1)
-            lanes = [(q, wide(uc_ref, q), wide(ec_ref, q), power(q)) for q in pair]
-            for i in range(HALF // 8):
-                r = slice(half * HALF + 8 * i, half * HALF + 8 * i + 8)
-                total = None
-                for q, ucq, ecq, strong in lanes:
-                    k = lax.rsqrt(uab_ref[r, q : q + 1] + ucq)
-                    e = eab_ref[r, q : q + 1] * ecq
-                    slope_ref[q, 8 * i : 8 * i + 8, :] = k * k * (e - k)
-                    total = strong * k if total is None else total + strong * k
-                pot_ref[r, :] = total if a == 0 else pot_ref[r, :] + total
-        found = [jnp.right_shift(value, a) & 3 for value in bits]
-        found = found[0] + 4 * found[1]
+    for a in range(0, 16, 4):
+        lanes = [(q, wide(uc_ref, q), wide(ec_ref, q), power(q)) for q in range(a, a + 4)]
+        for i in range(HALF // 8):
+            r = slice(8 * i, 8 * i + 8)
+            total = None if a == 0 else pot_ref[r, :]
+            for q, ucq, ecq, strong in lanes:
+                k = lax.rsqrt(uab_ref[r, q : q + 1] + ucq)
+                e = eab_ref[r, q : q + 1] * ecq
+                slope_ref[q, r, :] = k * k * (e - k)
+                total = strong * k if total is None else total + strong * k
+            pot_ref[r, :] = total
+        found = jnp.right_shift(bits, a) & 15
 
         @pl.when(found > 0)
         def _(a=a, found=found):
             def visit(j, _):
                 @pl.when((jnp.right_shift(found, j) & 1) > 0)
                 def _():
-                    fix_charge(16 * (j >> 1) + a + (j & 1))
+                    fix_charge(a + j)
 
                 return 0
 
             lax.fori_loop(0, 4, visit, 0)
 
-        for q in (a, a + 1, 16 + a, 17 + a):
+        for q in range(a, a + 4):
             copy = pltpu.make_async_copy(slope_ref.at[q], slope_out.at[q], sems.at[q])
             copy.start()
             copies.append(copy)
@@ -345,16 +340,22 @@
 
 def grid_kernel(
     plan_s,
+    place_s,
     recv_ref,
     owner_ref,
     gb_ref,
     gc_ref,
     table_ref,
-    pot_ref,
-    slope_in,
-    offb_ref,
-    offc_ref,
-    col_ref,
+    own_pot_ref,
+    own_slope_in,
+    own_offb_ref,
+    own_offc_ref,
+    own_col_ref,
+    other_pot_ref,
+    other_slope_in,
+    other_offb_ref,
+    other_offc_ref,
+    other_col_ref,
     field_out,
     push_ref,
     acc_ref,
@@ -370,8 +371,14 @@
     merged_ref,
     sems,
 ):
-    slope_copy = pltpu.make_async_copy(slope_in, slope_ref, sems.at[1])
-    slope_copy.start()
+    slope_copies = [
+        pltpu.make_async_copy(source, slope_ref.at[side], sems.at[1 + side])
+        for side, source in enumerate((own_slope_in, other_slope_in))
+    ]
+    for copy in slope_copies:
+        copy.start()
+    tile = place_s[1]
+    bases = [tile * HALF, (1 - tile) * HALF]
     pairs = merged_ref.shape[0]
     merged_ref[...] = jnp.where(owner_ref[...] > 0.0, recv_ref[:pairs], recv_ref[pairs:])
     def counter(rows):
@@ -403,11 +410,10 @@
 
     acc_ref[0] = jnp.zeros(acc_ref.shape[1:], f32)
     def step(t, _):
-        acc_ref[0] += product(2 * t, 0, 0)
-        acc_ref[0] += product(2 * t + 1, 0, 0)
+        acc_ref[0] += product(t, 0, 0)
         return 0
 
-    steps = 2 * pairs // TILE_CHUNKS
+    steps = 4 * pairs // TILE_CHUNKS
     lax.fori_loop(0, steps, step, 0)
 
     def rest(combo, _):
@@ -421,7 +427,7 @@
                 acc_ref[combo] += product(t, group_b, group_c)
                 return 0
 
-            lax.fori_loop(0, 2 * steps, extra, 0)
+            lax.fori_loop(0, steps, extra, 0)
 
         return 0
 
@@ -476,41 +482,53 @@
     def _():
         transform(1)
 
-    def finish(i, _):
-        r = pl.ds(pl.multiple_of(8 * i, 8), 8)
-        s = pl.ds(pl.multiple_of(N + 8 * i, 8), 8)
-        real = mid_ref[r, :N] - mid_ref[s, N:]
-        imag = mid_ref[s, :N] + mid_ref[r, N:]
-        dens_ref[r, :] = real * real + imag * imag
-        pot = pot_ref[r, :]
-        field_ref[0, r, :] = pot * real
-        field_ref[1, r, :] = pot * imag
-        return 0
-
-    lax.fori_loop(0, N // 8, finish, 0, unroll=8)
+    for base, pot_ref in zip(bases, (own_pot_ref, other_pot_ref)):
+
+        def finish(i, _, base=base, pot_ref=pot_ref):
+            r = pl.ds(pl.multiple_of(base + 8 * i, 8), 8)
+            s = pl.ds(pl.multiple_of(N + base + 8 * i, 8), 8)
+            real = mid_ref[r, :N] - mid_ref[s, N:]
+            imag = mid_ref[s, :N] + mid_ref[r, N:]
+            dens_ref[r, :] = real * real + imag * imag
+            pot = pot_ref[pl.ds(pl.multiple_of(8 * i, 8), 8), :]
+            field_ref[0, r, :] = pot * real
+            field_ref[1, r, :] = pot * imag
+            return 0
+
+        lax.fori_loop(0, HALF // 8, finish, 0, unroll=8)
     field_copy = pltpu.make_async_copy(field_ref, field_out, sems.at[0])
     field_copy.start()
-    slope_copy.wait()
-    for q in range(32):
-        base = (q // 16) * HALF
-        plain = [jnp.zeros((8, LANE), f32)] * 3
-        scaled = jnp.zeros((8, LANE), f32)
-        for i in range(HALF // 8):
-            r = slice(base + 8 * i, base + 8 * i + 8)
-            w = dens_ref[r, :] * slope_ref[q, 8 * i : 8 * i + 8, :]
-            w = [w[:, k * LANE : (k + 1) * LANE] for k in range(3)]
-            plain = [p + v for p, v in zip(plain, w)]
-            scaled = scaled + (w[0] + w[1] + w[2]) * offb_ref[r, q : q + 1]
-        for k in range(3):
-            sum_ref[q : q + 1, k * LANE : (k + 1) * LANE] = jnp.sum(plain[k], axis=0, keepdims=True)
-        sum_ref[32 + q : 33 + q, :LANE] = jnp.sum(scaled, axis=0, keepdims=True)
-    plain = sum_ref[:32, :]
-    off_a = col_ref[:32, 0:1]
-    scale = col_ref[:32, 1:2] * VOLUME
-    push_a = off_a * jnp.sum(plain, axis=1, keepdims=True) * scale
-    push_b = jnp.sum(sum_ref[32:, :LANE], axis=1, keepdims=True) * scale
-    push_c = jnp.sum(plain * offc_ref[...], axis=1, keepdims=True) * scale
-    packed = jnp.concatenate([push_a, push_b, push_c, 0.5 * col_ref[:32, 2:3]], axis=0)
+    columns = []
+    for side in range(2):
+        slope_copies[side].wait()
+        offb_ref = (own_offb_ref, other_offb_ref)[side]
+        offc_ref = (own_offc_ref, other_offc_ref)[side]
+        col_ref = (own_col_ref, other_col_ref)[side]
+        for q in range(16):
+            plain = [jnp.zeros((8, LANE), f32)] * 3
+            scaled = jnp.zeros((8, LANE), f32)
+            for i in range(HALF // 8):
+                r = slice(8 * i, 8 * i + 8)
+                rows = pl.ds(pl.multiple_of(bases[side] + 8 * i, 8), 8)
+                w = dens_ref[rows, :] * slope_ref[side, q, r, :]
+                w = [w[:, k * LANE : (k + 1) * LANE] for k in range(3)]
+                plain = [p + v for p, v in zip(plain, w)]
+                scaled = scaled + (w[0] + w[1] + w[2]) * offb_ref[r, q : q + 1]
+            for k in range(3):
+                cut = slice(k * LANE, (k + 1) * LANE)
+                sum_ref[q : q + 1, cut] = jnp.sum(plain[k], axis=0, keepdims=True)
+            sum_ref[16 + q : 17 + q, :LANE] = jnp.sum(scaled, axis=0, keepdims=True)
+        plain = sum_ref[:16, :]
+        scale = col_ref[:16, 1:2] * VOLUME
+        push_a = col_ref[:16, 0:1] * jnp.sum(plain, axis=1, keepdims=True) * scale
+        push_b = jnp.sum(sum_ref[16:, :LANE], axis=1, keepdims=True) * scale
+        push_c = jnp.sum(plain * offc_ref[...], axis=1, keepdims=True) * scale
+        columns.append((push_a, push_b, push_c, 0.5 * col_ref[:16, 2:3]))
+    ordered = []
+    for own, other in zip(*columns):
+        ordered.append(jnp.where(tile == 0, own, other))
+        ordered.append(jnp.where(tile == 0, other, own))
+    packed = jnp.concatenate(ordered, axis=0)
     push_ref[...] = jnp.transpose(jnp.broadcast_to(packed, (LANE, LANE)))[:1]
     field_copy.wait()
 
@@ -567,54 +585,64 @@
         compiler_params=params(54),
         name="columns",
     )(plane[None], coefficients.reshape(2, slots, N), jnp.asarray(first_table))
-    own, sent = lax.optimization_barrier((tile_list[0], sent))
+    own = tile_list[0]
     other = lax.ppermute(own, "mm", [(0, 1), (1, 0)])
-    first = lax.axis_index("mm") == 0
-    listed = jnp.concatenate([jnp.where(first, own, other), jnp.where(first, other, own)])
-    listed_col = jnp.pad(listed, (0, LANE - 32), constant_values=-1)[:, None]
-
+    tile = lax.axis_index("mm").astype(i32)
     recv = lax.all_to_all(sent, "pw", 0, 0, tiled=True)
 
     blocks = col_map.reshape(sources, slots)
     grid = jnp.pad(blocks, ((0, 0), (0, 4 * LANE - slots)), constant_values=EMPTY)
 
-    pot, slope, offb, offc, col, gb, gc, owner, plan = pl.pallas_call(
-        charges_kernel,
-        out_shape=(
-            jax.ShapeDtypeStruct((N, N), f32),
-            pltpu.HBM((32, HALF, N), f32),
-            jax.ShapeDtypeStruct((N, LANE), f32),
-            jax.ShapeDtypeStruct((32, N), f32),
+    def charges(listed, side, extra):
+        shapes = [
+            jax.ShapeDtypeStruct((HALF, N), f32),
+            pltpu.HBM((16, HALF, N), f32),
+            jax.ShapeDtypeStruct((HALF, LANE), f32),
+            jax.ShapeDtypeStruct((16, N), f32),
             jax.ShapeDtypeStruct((LANE, 8), f32),
-            jax.ShapeDtypeStruct((4, sources // 2, LANE), f32),
-            jax.ShapeDtypeStruct((4, sources // 2, LANE), f32),
-            jax.ShapeDtypeStruct((sources // 2, 8, LANE), f32),
-            jax.ShapeDtypeStruct((16,), i32),
-        ),
-        in_specs=smem(5) + vmem(5),
-        out_specs=tuple(vmem(1) + anywhere(1) + vmem(6) + smem(1)),
-        scratch_shapes=[
-            pltpu.VMEM((N, LANE), f32),
-            pltpu.VMEM((N, LANE), f32),
-            pltpu.VMEM((32, N), f32),
-            pltpu.VMEM((32, N), f32),
-            pltpu.VMEM((32, HALF, N), f32),
-            pltpu.SemaphoreType.DMA((32,)),
-        ],
-        compiler_params=params(50),
-        name="charges",
-    )(
-        listed,
-        charge_cell,
-        charge_frac,
-        charge[None],
-        plane[None],
-        listed_col,
-        charge_cell,
-        charge_frac,
-        charge[None],
-        grid,
-    )
+        ]
+        places = vmem(1) + anywhere(1) + vmem(3)
+        if extra:
+            shapes += [
+                jax.ShapeDtypeStruct((4, sources // 2, LANE), f32),
+                jax.ShapeDtypeStruct((4, sources // 2, LANE), f32),
+                jax.ShapeDtypeStruct((sources // 2, 8, LANE), f32),
+                jax.ShapeDtypeStruct((16,), i32),
+            ]
+            places += vmem(3) + smem(1)
+        place = jnp.stack([plane, side])
+        column = jnp.pad(listed, (0, LANE - 16), constant_values=-1)[:, None]
+        return pl.pallas_call(
+            charges_kernel,
+            out_shape=tuple(shapes),
+            in_specs=smem(5) + vmem(4 + len(extra)),
+            out_specs=tuple(places),
+            scratch_shapes=[
+                pltpu.VMEM((HALF, LANE), f32),
+                pltpu.VMEM((HALF, LANE), f32),
+                pltpu.VMEM((16, N), f32),
+                pltpu.VMEM((16, N), f32),
+                pltpu.VMEM((16, HALF, N), f32),
+                pltpu.SemaphoreType.DMA((16,)),
+            ],
+            compiler_params=params(50),
+            name="charges_own" if extra else "charges_other",
+        )(
+            listed,
+            charge_cell,
+            charge_frac,
+            charge[None],
+            place,
+            column,
+            charge_cell,
+            charge_frac,
+            charge[None],
+            *extra,
+        )
+
+    mine = charges(own, tile, [grid])
+    gb, gc, owner, plan = mine[5:]
+    theirs = charges(other, 1 - tile, [])
 
     field, push = pl.pallas_call(
         grid_kernel,
@@ -622,7 +650,7 @@
             jax.ShapeDtypeStruct((2, N, N), f32),
             jax.ShapeDtypeStruct((1, LANE), f32),
         ),
-        in_specs=smem(1) + vmem(6) + anywhere(1) + vmem(3),
+        in_specs=smem(2) + vmem(5) + 2 * (vmem(1) + anywhere(1) + vmem(3)),
         out_specs=tuple(anywhere(1) + vmem(1)),
         scratch_shapes=[
             pltpu.VMEM((4, 4 * WINDOW, 2 * LANE), f32),
@@ -632,15 +660,25 @@
             pltpu.VMEM((WINDOW, 2 * N), f32),
             pltpu.VMEM((2 * N, 2 * N), f32),
             pltpu.VMEM((N, N), f32),
-            pltpu.VMEM((64, N), f32),
+            pltpu.VMEM((32, N), f32),
             pltpu.VMEM((2, N, N), f32),
-            pltpu.VMEM((32, HALF, N), f32),
+            pltpu.VMEM((2, 16, HALF, N), f32),
             pltpu.VMEM((sources // 2, 8, LANE), f32),
-            pltpu.SemaphoreType.DMA((2,)),
+            pltpu.SemaphoreType.DMA((3,)),
         ],
         compiler_params=params(50),
         name="grid",
-    )(plan, recv, owner, gb, gc, jnp.asarray(second_table), pot, slope, offb, offc, col)
+    )(
+        plan,
+        jnp.stack([plane, tile]),
+        recv,
+        owner,
+        gb,
+        gc,
+        jnp.asarray(second_table),
+        *mine[:5],
+        *theirs,
+    )
 
     push = push + lax.ppermute(push, "mm", [(0, 1), (1, 0)])
     terms = lax.all_to_all(

time: 61.7 us -> 62.3 us (level)
  Pallas kernels: 25.4 us -> 27.8 us
  waiting for transfers between devices: 4.35 us -> 2.09 us
    pallas_call x1 -> x2, Pallas kernels: 6.94 us -> 9.78 us  [charges(): pl.pallas_call(charges_kernel, out_shape=tuple(shapes), in_specs=smem(5)...]
    all_to_all x1, waiting for transfers between devices: 2.18 us -> 0.94 us  [local(): recv = lax.all_to_all(sent, 'pw', 0, 0, tiled=True)]
    ppermute x1, waiting for transfers between devices: 1.02 us -> 0.01 us  [local(): other = lax.ppermute(own, 'mm', [(0, 1), (1, 0)])]
  transfers between devices with their start and end apart: 3 -> 3, of which waited for: 3 -> 2; matrix products, arithmetic and copies ran while one was open for 0% -> 1% of each run, Pallas kernels for 11% -> 21%
where the time goes in v7:
time: 62.3 us; the launch traced here: 61.8 us
  Pallas kernels  27.8 us (45%)
  blocking collectives  18.7 us (30%)
  starting transfers between devices  12 us (19%)
  waiting for transfers between devices  2.09 us (3%)
  between operations  0.8 us (1%)
    all_to_all x1, blocking collectives, local(): lax.all_to_all(jnp.broadcast_to(push[None], (sources, 1, LANE)), 'pw', 0,...  18.7 us
    pallas_call x1, Pallas kernels, local(): pl.pallas_call(grid_kernel, out_shape=(jax.ShapeDtypeStruct((2, N, N), f3...  12.8 us
    all_to_all x1, starting transfers between devices, local(): recv = lax.all_to_all(sent, 'pw', 0, 0, tiled=True)  11.8 us
    pallas_call x2, Pallas kernels, charges(): pl.pallas_call(charges_kernel, out_shape=tuple(shapes), in_specs=smem(5)...  9.78 us
    pallas_call x1, Pallas kernels, local(): pl.pallas_call(columns_kernel, out_shape=jax.ShapeDtypeStruct((planes, 8,...  3 us
    pallas_call x1, Pallas kernels, local(): pl.pallas_call(spread_kernel, out_shape=jax.ShapeDtypeStruct((3, charge.s...  2.24 us
  transfers between devices with their start and end apart: 3, of which 2 were waited for; matrix products, arithmetic and copies ran while one was open for 1% of the time, Pallas kernels for 21%

profile of v7, /device:TPU:0, one launch (start us, length us, event | category | flops | bytes accessed | tf_op | source)
XLA Modules:
  0.0 61.8 jit_solution(9633345275242388867)
XLA Ops:
  0.6 0.0 copy-start.4
  0.6 0.0 copy-start.5
  0.7 0.1 collective-permute-start
  0.8 0.0 copy-start.1
  0.8 0.0 copy-start.2
  0.8 0.0 copy-start.3
  0.8 0.0 copy-start
  0.8 3.0 %columns.1 = f32[64,8,128]{2,1,0:T(8,128)} custom-call(s32[1]{0:T(128)} %bitcast.2.plane_s, f32[2,448,384]{2,1,0:T(8,128)} %bitcast.24, bf16[256,768]{1,0:T(8,128)(2,1)} %constant.18.clone.table_in), custom_call_target="tpu_custom_call" | custom-call | tf_op jit(solution)/shard_map/columns/pallas_call | solution.py:573
  3.8 11.8 %all-to-all-start = ((f32[64,8,128]{2,1,0:T(8,128)}), f32[64,8,128]{2,1,0:T(8,128)S(1)}, u32[]{:S(2)}, u32[]{:S(2)}) async-start(f32[64,8,128]{2,1,0:T(8,128)} %columns.1), calls=%async_computation | async-start | bytes 524288 | tf_op jit(solution)/shard_map/all_to_all | solution.py:591
  15.6 0.0 copy-done.4
  15.6 0.1 copy.13.list_ref
  15.7 0.0 copy-done.5
  15.7 0.1 reshape.16
  15.9 0.1 pad_add_fusion
  15.9 0.0 copy-done.1
  15.9 0.0 copy-done.2
  15.9 0.0 copy-done.3
  15.9 5.3 %charges_own.1 = (f32[192,384]{1,0:T(8,128)S(1)}, f32[16,192,384]{2,1,0:T(8,128)}, f32[192,128]{1,0:T(8,128)S(1)}, f32[16,384]{1,0:T(8,128)S(1)}, f32[128,8]{1,0...) custom-call(s32[16]{0:T(128)S(1)} %bitcast.23, ...), custom_call_target="tpu_custom_call" | custom-call | tf_op jit(solution)/shard_map/charges_own/pallas_call | solution.py:615
  21.2 0.0 collective-permute-done.list_s
  21.3 0.1 copy.14.list_ref
  21.4 4.5 %charges_other.1 = (f32[192,384]{1,0:T(8,128)S(1)}, f32[16,192,384]{2,1,0:T(8,128)}, f32[192,128]{1,0:T(8,128)S(1)}, f32[16,384]{1,0:T(8,128)S(1)}, f32[128,8]{1,0:T(8,128)S(1)}) custom-call(s32[16]{0:T(128)S(1)} %collective-permute-done.list_s, s32[3,512]{1,0:T(4,128)S(1)} %copy-done.1, f32[3,512]{1,0:T(4,128)S(1)} %copy-done.2, f32[1,512]{1,0:T(1,128)S(1)} %bitcast.19, ...), custom_call_target="tpu_custom_call" | custom-call | tf_op jit(solution)/shard_map/charges_other/pallas_call | solution.py:615
  25.9 0.9 %all-to-all-done.recv_ref = f32[64,8,128]{2,1,0:T(8,128)S(1)} async-done(((f32[64,8,128]{2,1,0:T(8,128)}), f32[64,8,128]{2,1,0:T(8,128)S(1)}, u32[]{:S(2)}, u32[]{:S(2)}) %all-to-all-start) | async-done | bytes 262176 | tf_op jit(solution)/shard_map/all_to_all | solution.py:591
  26.8 0.0 copy-done
  26.8 12.8 %grid.1 = (f32[2,384,384]{2,1,0:T(8,128)}, f32[1,128]{1,0:T(1,128)S(1)}) custom-call(s32[16]{0:T(128)S(1)} %get-tuple-element.18.plan_s, s32[2]{0:T(128)S(1)} %get-tuple-element.38.place_s, f32[64,8,128]{2,1,0:T(8,128)S(1)} %all-to-all-done.recv_ref, f32[32,8,128]{2,1,0:T(8,128)S(1)} %get-tuple-element.19.owner_ref, ...), custom_call_target="tpu_custom_call" | custom-call | tf_op jit(solution)/shard_map/grid/pallas_call | solution.py:647
  39.6 0.1 collective-permute-start.1
  39.7 1.1 %collective-permute-done.1 = f32[1,128]{1,0:T(1,128)S(1)} collective-permute-done((f32[1,128]{1,0:T(1,128)S(1)}, f32[1,128]{1,0:T(1,128)S(1)}, u32[]{:S(2)}, u32[]{:S(2)}) %collective-permute-start.1) | collective-permute-done | bytes 544 | tf_op jit(solution)/shard_map/ppermute | solution.py:683
  40.9 18.7 %all_to_all.10 = f32[64,1,128]{2,1,0:T(1,128)S(1)} all-to-all(f32[64,1,128]{2,1,0:T(1,128)S(1)} %broadcast_in_dim.29), channel_id=1, replica_groups=mesh['pw'=64,'mm'=2] {'pw'}, dimensions={0} | all-to-all | bytes 65536 | tf_op jit(solution)/shard_map/all_to_all | solution.py:684
  59.5 2.2 %spread.1 = f32[3,512]{1,0:T(4,128)} custom-call(f32[64,128]{1,0:T(8,128)S(1)} %bitcast.16), custom_call_target="tpu_custom_call" | custom-call | tf_op jit(solution)/shard_map/spread/pallas_call | solution.py:687
  (5 shorter events, 0.0 us)
Async XLA Ops:
  0.6 15.0 %copy-start.4 = (s32[1,16]{1,0:T(1,128)S(1)}, s32[1,16]{1,0:T(1,128)}, u32[]{:S(2)}) copy-start(s32[1,16]{1,0:T(1,128)} %param.13) | copy-start | bytes 196
  0.6 15.1 %copy-start.5 = (s32[28672]{0:T(1024)S(1)}, s32[28672]{0:T(1024)}, u32[]{:S(2)}) copy-start(s32[28672]{0:T(1024)} %param.9) | copy-start | bytes 344068
  0.7 20.6 %collective-permute-start = (s32[16]{0:T(128)}, s32[16]{0:T(128)S(1)}, u32[]{:S(2)}, u32[]{:S(2)}) collective-permute-start(s32[16]{0:T(128)} %bitcast.21), channel_id=1, source_target_pairs={{0,1},{1,0},{2,3},{3,2},{4,5},{5,4},{6,7},{7,6},{8,9},{9,8},{10,11... | collective-permute-start | bytes 200 | tf_op jit(solution)/shard_map/ppermute | solution.py:589
  0.8 15.2 %copy-start.1 = (s32[3,512]{1,0:T(4,128)S(1)}, s32[3,512]{1,0:T(4,128)}, u32[]{:S(2)}) copy-start(s32[3,512]{1,0:T(4,128)} %cell_ref.3) | copy-start | bytes 18436
  0.8 15.2 %copy-start.2 = (f32[3,512]{1,0:T(4,128)S(1)}, f32[3,512]{1,0:T(4,128)}, u32[]{:S(2)}) copy-start(f32[3,512]{1,0:T(4,128)} %frac_ref.3) | copy-start | bytes 18436
  0.8 15.2 %copy-start.3 = (f32[512]{0:T(512)S(1)}, f32[512]{0:T(512)}, u32[]{:S(2)}) copy-start(f32[512]{0:T(512)} %param.12) | copy-start | bytes 6148
  0.8 26.0 %copy-start = (bf16[1536,384]{1,0:T(8,128)(2,1)S(1)}, bf16[1536,384]{1,0:T(8,128)(2,1)}, u32[]{:S(2)}) copy-start(bf16[1536,384]{1,0:T(8,128)(2,1)} %constant.19.clone.table_ref) | copy-start | bytes 3538948
  3.8 23.0 %all-to-all-start = ((f32[64,8,128]{2,1,0:T(8,128)}), f32[64,8,128]{2,1,0:T(8,128)S(1)}, u32[]{:S(2)}, u32[]{:S(2)}) async-start(f32[64,8,128]{2,1,0:T(8,128)} %columns.1), calls=%async_computation | async-start | bytes 524288 | tf_op jit(solution)/shard_map/all_to_all | solution.py:591
  39.6 1.2 %collective-permute-start.1 = (f32[1,128]{1,0:T(1,128)S(1)}, f32[1,128]{1,0:T(1,128)S(1)}, u32[]{:S(2)}, u32[]{:S(2)}) collective-permute-start(f32[1,128]{1,0:T(1,128)S(1)} %get-tuple-element.33), channel_id=1, source_target_pairs={{0,1},{1,0},{2,3},{3,2},{4,5},{5,4},{6,7},{7,6},{8,9},{9,8},{10,11... | collective-permute-start | bytes 1544 | tf_op jit(solution)/shard_map/ppermute | solution.py:683

commit v8 on v7

--- a/solution.py
+++ b/solution.py
@@ -103,7 +103,7 @@
                     part * planes : (part + 1) * planes, piece * LANE : (piece + 1) * LANE
                 ]
 
-    reverse = plane_s[0] >= planes // 2
+    reverse = plane_s[0] < planes // 2
 
     @pl.when(jnp.logical_not(reverse))
     def _():
@@ -159,16 +159,16 @@
     row = jnp.floor((cells.astype(f32) + 0.5) * (1.0 / N))
     gb = jnp.where(cells < EMPTY, row, -1000.0)
     gc = jnp.where(cells < EMPTY, cells.astype(f32) - N * row, -1000.0)
-    high, low = halves(jnp.concatenate([gb[pairs:], gc[pairs:]], axis=0))
+    high, low = halves(jnp.concatenate([gb[:pairs], gc[:pairs]], axis=0))
     flip = flip_table(cells.shape[1])
     turned = mm(high, flip) + mm(low, flip)
-    owned = jnp.where(gb[:pairs] >= 0.0, 1.0, 0.0)
+    owned = jnp.where(turned[:pairs] >= 0.0, 1.0, 0.0)
     for piece in range(4):
         cut = slice(piece * LANE, (piece + 1) * LANE)
         owner_ref[:, piece, :] = owned[:, cut]
         owner_ref[:, 4 + piece, :] = owned[:, cut]
-    merged_b = jnp.maximum(gb[:pairs], turned[:pairs])
-    merged_c = jnp.maximum(gc[:pairs], turned[pairs:])
+    merged_b = jnp.maximum(gb[pairs:], turned[:pairs])
+    merged_c = jnp.maximum(gc[pairs:], turned[pairs:])
     found = jnp.int32(0)
     for band in range(3):
         inside = (merged_c >= band * LANE) & (merged_c < (band + 1) * LANE)
@@ -220,14 +220,12 @@
     refs = list(refs)
     grid_ref = refs.pop(0) if len(refs) > 11 else None
     pot_ref, slope_out, offb_ref, offc_ref, col_ref = refs[:5]
-    if grid_ref is not None:
-        sort_cells(grid_ref, *refs[5:9])
     uab_ref, eab_ref, uc_ref, ec_ref, slope_ref, sems = refs[-6:]
     plane = place_s[0].astype(f32)
     tile = place_s[1]
     start_row = (tile * HALF).astype(f32)
     listed = list_ref[...]
-    mask = lax.broadcasted_iota(i32, (LANE, cell_ref.shape[1]), 1) == listed
+    mask = lax.broadcasted_iota(i32, (16, cell_ref.shape[1]), 1) == listed
     center = cell_ref[...].astype(f32) + frac_ref[...]
 
     def pick(row):
@@ -237,16 +235,17 @@
     strength = pick(charge_ref[...])
     off_a = wrap(plane - ca)
     col_ref[...] = jnp.concatenate(
-        [off_a, strength, listed.astype(f32)] + [jnp.zeros((LANE, 5), f32)], axis=1
+        [off_a, strength, listed.astype(f32)] + [jnp.zeros((16, 5), f32)], axis=1
     )
-    off_c = wrap(lax.broadcasted_iota(i32, (16, N), 1).astype(f32) - cc[:16])
+    off_c = wrap(lax.broadcasted_iota(i32, (16, N), 1).astype(f32) - cc)
     offc_ref[...] = off_c
     sq_c = off_c * off_c
     uc_ref[...] = sq_c
     ec_ref[...] = jnp.exp(-sq_c)
 
     def across(column):
-        return jnp.transpose(jnp.broadcast_to(column, (LANE, LANE)))[:1]
+        tall = jnp.concatenate([column, jnp.zeros((LANE - 16, 1), f32)], axis=0)
+        return jnp.transpose(jnp.broadcast_to(tall, (LANE, LANE)))[:1]
 
     row = lax.broadcasted_iota(i32, (HALF, LANE), 0).astype(f32) + start_row
     off_b = wrap(row - across(cb))
@@ -334,6 +333,8 @@
             copy = pltpu.make_async_copy(slope_ref.at[q], slope_out.at[q], sems.at[q])
             copy.start()
             copies.append(copy)
+    if grid_ref is not None:
+        sort_cells(grid_ref, *refs[5:9])
     for copy in copies:
         copy.wait()
 
@@ -534,15 +535,17 @@
 
 
 def spread_kernel(terms_ref, out_ref):
-    terms = terms_ref[...]
     charges = out_ref.shape[1]
-    lane = lax.broadcasted_iota(i32, (terms.shape[0], charges), 1).astype(f32)
-    totals = [jnp.zeros((terms.shape[0], charges), f32)] * 3
-    for q in range(32):
-        hot = terms[:, 96 + q : 97 + q] == lane
-        for axis in range(3):
-            value = terms[:, 32 * axis + q : 32 * axis + q + 1]
-            totals[axis] = totals[axis] + jnp.where(hot, value, 0.0)
+    rows = 32
+    lane = lax.broadcasted_iota(i32, (rows, charges), 1).astype(f32)
+    totals = [jnp.zeros((rows, charges), f32)] * 3
+    for group in range(terms_ref.shape[0] // rows):
+        terms = terms_ref[rows * group : rows * (group + 1), :]
+        for q in range(32):
+            hot = terms[:, 96 + q : 97 + q] == lane
+            for axis in range(3):
+                value = terms[:, 32 * axis + q : 32 * axis + q + 1]
+                totals[axis] = totals[axis] + jnp.where(hot, value, 0.0)
     for axis in range(3):
         out_ref[axis : axis + 1, :] = jnp.sum(totals[axis], axis=0, keepdims=True)
 
@@ -599,7 +602,7 @@
             pltpu.HBM((16, HALF, N), f32),
             jax.ShapeDtypeStruct((HALF, LANE), f32),
             jax.ShapeDtypeStruct((16, N), f32),
-            jax.ShapeDtypeStruct((LANE, 8), f32),
+            jax.ShapeDtypeStruct((16, 8), f32),
         ]
         places = vmem(1) + anywhere(1) + vmem(3)
         if extra:
@@ -611,7 +614,7 @@
             ]
             places += vmem(3) + smem(1)
         place = jnp.stack([plane, side])
-        column = jnp.pad(listed, (0, LANE - 16), constant_values=-1)[:, None]
+        column = listed[:, None]
         return pl.pallas_call(
             charges_kernel,
             out_shape=tuple(shapes),

time: 62.3 us -> 62.6 us (level)
  waiting for transfers between devices: 2.09 us -> 0.82 us
  blocking collectives: 18.7 us -> 19.7 us
  Pallas kernels: 27.8 us -> 28.6 us
    all_to_all x1, blocking collectives: 18.7 us -> 19.7 us  [local(): lax.all_to_all(jnp.broadcast_to(push[None], (sources, 1, LANE)), 'pw', 0,...]
    all_to_all x1, waiting for transfers between devices: 0.94 us -> 0.01 us  [local(): recv = lax.all_to_all(sent, 'pw', 0, 0, tiled=True)]
  transfers between devices with their start and end apart: 3 -> 3, of which waited for: 2 -> 1; matrix products, arithmetic and copies ran while one was open for 1% -> 1% of each run, Pallas kernels for 21% -> 16%
where the time goes in v8:
time: 62.6 us; the launch traced here: 62.3 us
  Pallas kernels  28.6 us (46%)
  blocking collectives  19.7 us (31%)
  starting transfers between devices  11.9 us (19%)
  waiting for transfers between devices  0.82 us (1%)
  between operations  0.79 us (1%)
    all_to_all x1, blocking collectives, local(): lax.all_to_all(jnp.broadcast_to(push[None], (sources, 1, LANE)), 'pw', 0,...  19.7 us
    pallas_call x1, Pallas kernels, local(): pl.pallas_call(grid_kernel, out_shape=(jax.ShapeDtypeStruct((2, N, N), f3...  12.8 us
    all_to_all x1, starting transfers between devices, local(): recv = lax.all_to_all(sent, 'pw', 0, 0, tiled=True)  11.3 us
    pallas_call x2, Pallas kernels, charges(): pl.pallas_call(charges_kernel, out_shape=tuple(shapes), in_specs=smem(5)...  10.2 us
    pallas_call x1, Pallas kernels, local(): pl.pallas_call(columns_kernel, out_shape=jax.ShapeDtypeStruct((planes, 8,...  3.26 us
    pallas_call x1, Pallas kernels, local(): pl.pallas_call(spread_kernel, out_shape=jax.ShapeDtypeStruct((3, charge.s...  2.32 us
  transfers between devices with their start and end apart: 3, of which 1 were waited for; matrix products, arithmetic and copies ran while one was open for 1% of the time, Pallas kernels for 16%

profile of v8, /device:TPU:0, one launch (start us, length us, event | category | flops | bytes accessed | tf_op | source)
XLA Modules:
  0.0 62.3 jit_solution(6864965110870798124)
XLA Ops:
  0.6 0.0 copy-start.4
  0.6 0.0 copy-start.5
  0.7 0.0 copy-start.1
  0.7 0.0 copy-start.2
  0.7 0.0 copy-start.3
  0.7 0.0 copy-start
  0.7 3.3 %columns.1 = f32[64,8,128]{2,1,0:T(8,128)} custom-call(s32[1]{0:T(128)} %bitcast.2.plane_s, f32[2,448,384]{2,1,0:T(8,128)} %bitcast.23, bf16[256,768]{1,0:T(8,128)(2,1)} %constant.16.clone.table_in), custom_call_target="tpu_custom_call" | custom-call | tf_op jit(solution)/shard_map/columns/pallas_call | solution.py:576
  4.0 11.3 %all-to-all-start = ((f32[64,8,128]{2,1,0:T(8,128)}), f32[64,8,128]{2,1,0:T(8,128)S(1)}, u32[]{:S(2)}, u32[]{:S(2)}) async-start(f32[64,8,128]{2,1,0:T(8,128)} %columns.1), calls=%async_computation | async-start | bytes 524288 | tf_op jit(solution)/shard_map/all_to_all | solution.py:594
  15.3 0.0 copy-done.4
  15.3 0.1 collective-permute-start
  15.4 0.1 copy.13.list_ref
  15.4 0.0 copy-done.5
  15.4 0.1 reshape.16
  15.6 0.1 pad_add_fusion
  15.6 0.0 copy-done.1
  15.6 0.0 copy-done.2
  15.6 0.0 copy-done.3
  15.7 5.8 %charges_own.1 = (f32[192,384]{1,0:T(8,128)S(1)}, f32[16,192,384]{2,1,0:T(8,128)}, f32[192,128]{1,0:T(8,128)S(1)}, f32[16,384]{1,0:T(8,128)S(1)}, f32[16,8]{1,0:...) custom-call(s32[16]{0:T(128)S(1)} %bitcast.21, ...), custom_call_target="tpu_custom_call" | custom-call | tf_op jit(solution)/shard_map/charges_own/pallas_call | solution.py:618
  21.5 0.0 collective-permute-done.list_s
  21.5 0.1 copy.14.list_ref
  21.6 4.4 %charges_other.1 = (f32[192,384]{1,0:T(8,128)S(1)}, f32[16,192,384]{2,1,0:T(8,128)}, f32[192,128]{1,0:T(8,128)S(1)}, f32[16,384]{1,0:T(8,128)S(1)}, f32[16,8]{1,0:T(8,128)S(1)}) custom-call(s32[16]{0:T(128)S(1)} %collective-permute-done.list_s, s32[3,512]{1,0:T(4,128)S(1)} %copy-done.1, f32[3,512]{1,0:T(4,128)S(1)} %copy-done.2, f32[1,512]{1,0:T(1,128)S(1)} %bitcast.17, ...), custom_call_target="tpu_custom_call" | custom-call | tf_op jit(solution)/shard_map/charges_other/pallas_call | solution.py:618
  26.0 0.0 all-to-all-done.recv_ref
  26.0 0.0 copy-done
  26.0 12.8 %grid.1 = (f32[2,384,384]{2,1,0:T(8,128)}, f32[1,128]{1,0:T(1,128)S(1)}) custom-call(s32[16]{0:T(128)S(1)} %get-tuple-element.18.plan_s, s32[2]{0:T(128)S(1)} %get-tuple-element.38.place_s, f32[64,8,128]{2,1,0:T(8,128)S(1)} %all-to-all-done.recv_ref, f32[32,8,128]{2,1,0:T(8,128)S(1)} %get-tuple-element.19.owner_ref, ...), custom_call_target="tpu_custom_call" | custom-call | tf_op jit(solution)/shard_map/grid/pallas_call | solution.py:650
  38.8 0.6 collective-permute-start.1
  39.4 0.8 %collective-permute-done.1 = f32[1,128]{1,0:T(1,128)S(1)} collective-permute-done((f32[1,128]{1,0:T(1,128)S(1)}, f32[1,128]{1,0:T(1,128)S(1)}, u32[]{:S(2)}, u32[]{:S(2)}) %collective-permute-start.1) | collective-permute-done | bytes 544 | tf_op jit(solution)/shard_map/ppermute | solution.py:686
  40.2 19.7 %all_to_all.10 = f32[64,1,128]{2,1,0:T(1,128)S(1)} all-to-all(f32[64,1,128]{2,1,0:T(1,128)S(1)} %broadcast_in_dim.25), channel_id=1, replica_groups=mesh['pw'=64,'mm'=2] {'pw'}, dimensions={0} | all-to-all | bytes 65536 | tf_op jit(solution)/shard_map/all_to_all | solution.py:687
  60.0 2.3 %spread.1 = f32[3,512]{1,0:T(4,128)} custom-call(f32[64,128]{1,0:T(8,128)S(1)} %bitcast.14), custom_call_target="tpu_custom_call" | custom-call | tf_op jit(solution)/shard_map/spread/pallas_call | solution.py:690
  (3 shorter events, 0.0 us)
Async XLA Ops:
  0.6 14.6 %copy-start.4 = (s32[1,16]{1,0:T(1,128)S(1)}, s32[1,16]{1,0:T(1,128)}, u32[]{:S(2)}) copy-start(s32[1,16]{1,0:T(1,128)} %param.13) | copy-start | bytes 196
  0.6 14.8 %copy-start.5 = (s32[28672]{0:T(1024)S(1)}, s32[28672]{0:T(1024)}, u32[]{:S(2)}) copy-start(s32[28672]{0:T(1024)} %param.9) | copy-start | bytes 344068
  0.7 15.0 %copy-start.1 = (s32[3,512]{1,0:T(4,128)S(1)}, s32[3,512]{1,0:T(4,128)}, u32[]{:S(2)}) copy-start(s32[3,512]{1,0:T(4,128)} %cell_ref.3) | copy-start | bytes 18436
  0.7 15.0 %copy-start.2 = (f32[3,512]{1,0:T(4,128)S(1)}, f32[3,512]{1,0:T(4,128)}, u32[]{:S(2)}) copy-start(f32[3,512]{1,0:T(4,128)} %frac_ref.3) | copy-start | bytes 18436
  0.7 15.0 %copy-start.3 = (f32[512]{0:T(512)S(1)}, f32[512]{0:T(512)}, u32[]{:S(2)}) copy-start(f32[512]{0:T(512)} %param.12) | copy-start | bytes 6148
  0.7 25.3 %copy-start = (bf16[1536,384]{1,0:T(8,128)(2,1)S(1)}, bf16[1536,384]{1,0:T(8,128)(2,1)}, u32[]{:S(2)}) copy-start(bf16[1536,384]{1,0:T(8,128)(2,1)} %constant.17.clone.table_ref) | copy-start | bytes 3538948
  4.0 22.0 %all-to-all-start = ((f32[64,8,128]{2,1,0:T(8,128)}), f32[64,8,128]{2,1,0:T(8,128)S(1)}, u32[]{:S(2)}, u32[]{:S(2)}) async-start(f32[64,8,128]{2,1,0:T(8,128)} %columns.1), calls=%async_computation | async-start | bytes 524288 | tf_op jit(solution)/shard_map/all_to_all | solution.py:594
  15.3 6.2 %collective-permute-start = (s32[16]{0:T(128)S(1)}, s32[16]{0:T(128)S(1)}, u32[]{:S(2)}, u32[]{:S(2)}) collective-permute-start(s32[16]{0:T(128)S(1)} %bitcast.19), channel_id=1, source_target_pairs={{0,1},{1,0},{2,3},{3,2},{4,5},{5,4},{6,7},{7,6},{8,9},{9,8},{10,11... | collective-permute-start | bytes 200 | tf_op jit(solution)/shard_map/ppermute | solution.py:592
  38.8 1.4 %collective-permute-start.1 = (f32[1,128]{1,0:T(1,128)S(1)}, f32[1,128]{1,0:T(1,128)S(1)}, u32[]{:S(2)}, u32[]{:S(2)}) collective-permute-start(f32[1,128]{1,0:T(1,128)S(1)} %get-tuple-element.33), channel_id=1, source_target_pairs={{0,1},{1,0},{2,3},{3,2},{4,5},{5,4},{6,7},{7,6},{8,9},{9,8},{10,11... | collective-permute-start | bytes 1544 | tf_op jit(solution)/shard_map/ppermute | solution.py:686

commit v9 on v6

--- a/solution.py
+++ b/solution.py
@@ -19,7 +19,7 @@
 VOLUME = SPACING**3
 PEAK = 2.0 / math.sqrt(math.pi)
 EMPTY = N * N
-TILE_CHUNKS = 8
+TILE_CHUNKS = 32
 WINDOW = 208
 BLOCKS = N // 16
 NT = (((1,), (1,)), ((), ()))
@@ -64,7 +64,7 @@
 
 
 def columns_kernel(
-    plane_s, coef_in, table_in, out_ref, coef_ref, table_ref, high_ref, low_ref, sems
+    coef_in, table_in, out_ref, coef_ref, table_ref, high_ref, low_ref, sems
 ):
     slots = coef_ref.shape[1]
     half = slots // 2
@@ -103,7 +103,7 @@
                     part * planes : (part + 1) * planes, piece * LANE : (piece + 1) * LANE
                 ]
 
-    reverse = plane_s[0] >= planes // 2
+    reverse = lax.axis_index("pw") < planes // 2
 
     @pl.when(jnp.logical_not(reverse))
     def _():
@@ -154,11 +154,6 @@
 
 
 def charges_kernel(
-    list_s,
-    cell_s,
-    frac_s,
-    charge_s,
-    plane_s,
     list_ref,
     cell_ref,
     frac_ref,
@@ -185,16 +180,16 @@
     row = jnp.floor((cells.astype(f32) + 0.5) * (1.0 / N))
     gb = jnp.where(cells < EMPTY, row, -1000.0)
     gc = jnp.where(cells < EMPTY, cells.astype(f32) - N * row, -1000.0)
-    high, low = halves(jnp.concatenate([gb[pairs:], gc[pairs:]], axis=0))
+    high, low = halves(jnp.concatenate([gb[:pairs], gc[:pairs]], axis=0))
     flip = flip_table(cells.shape[1])
     turned = mm(high, flip) + mm(low, flip)
-    owned = jnp.where(gb[:pairs] >= 0.0, 1.0, 0.0)
+    owned = jnp.where(turned[:pairs] >= 0.0, 1.0, 0.0)
     for piece in range(4):
         cut = slice(piece * LANE, (piece + 1) * LANE)
         owner_ref[:, piece, :] = owned[:, cut]
         owner_ref[:, 4 + piece, :] = owned[:, cut]
-    merged_b = jnp.maximum(gb[:pairs], turned[:pairs])
-    merged_c = jnp.maximum(gc[:pairs], turned[pairs:])
+    merged_b = jnp.maximum(gb[pairs:], turned[:pairs])
+    merged_c = jnp.maximum(gc[pairs:], turned[pairs:])
     found = jnp.int32(0)
     for band in range(3):
         inside = (merged_c >= band * LANE) & (merged_c < (band + 1) * LANE)
@@ -231,7 +226,7 @@
             out[piece] = values[:, piece * LANE : (piece + 1) * LANE]
 
     listed = list_ref[...]
-    mask = lax.broadcasted_iota(i32, (LANE, cell_ref.shape[1]), 1) == listed
+    mask = lax.broadcasted_iota(i32, (32, cell_ref.shape[1]), 1) == listed
     center = cell_ref[...].astype(f32) + frac_ref[...]
 
     def pick(row):
@@ -239,21 +234,23 @@
 
     ca, cb, cc = (pick(center[i : i + 1]) for i in range(3))
     strength = pick(charge_ref[...])
-    plane = plane_s[0].astype(f32)
+    plane = lax.axis_index("pw").astype(f32)
     off_a = wrap(plane - ca)
     col_ref[...] = jnp.concatenate(
-        [off_a, strength, listed.astype(f32)] + [jnp.zeros((LANE, 5), f32)], axis=1
+        [off_a, strength, listed.astype(f32)] + [jnp.zeros((32, 5), f32)], axis=1
     )
-    off_c = wrap(lax.broadcasted_iota(i32, (32, N), 1).astype(f32) - cc[:32])
+    off_c = wrap(lax.broadcasted_iota(i32, (32, N), 1).astype(f32) - cc)
     offc_ref[...] = off_c
     sq_c = off_c * off_c
     uc_ref[...] = sq_c
     ec_ref[...] = jnp.exp(-sq_c)
 
     def across(column):
-        return jnp.transpose(jnp.broadcast_to(column, (LANE, LANE)))[:1]
-
-    off_b = wrap(lax.broadcasted_iota(i32, (N, LANE), 0).astype(f32) - across(cb))
+        tall = jnp.concatenate([column, jnp.zeros((LANE - 32, 1), f32)], axis=0)
+        return jnp.transpose(jnp.broadcast_to(tall, (LANE, LANE)))[:1]
+
+    row_b, row_c, row_s = across(cb), across(cc), across(strength)
+    off_b = wrap(lax.broadcasted_iota(i32, (N, LANE), 0).astype(f32) - row_b)
     offb_ref[...] = off_b
     row_a = across(off_a)
     uab = off_b * off_b + (row_a * row_a + SOFTEN)
@@ -276,15 +273,15 @@
 
     def fix_charge(q):
         base = (q >> 4) * (HALF // 8)
-        own = list_s[q]
-        center = [cell_s[axis, own].astype(f32) + frac_s[axis, own] for axis in range(3)]
-        strong = charge_s[0, own]
-        da = wrap(plane - center[0])
-        rest = da * da + SOFTEN
-        dc = wrap(lax.broadcasted_iota(i32, (8, N), 1).astype(f32) - center[2])
-        rest = rest + dc * dc
+
+        def one(row):
+            return jnp.sum(jnp.where(lane == q, row, 0.0), axis=1, keepdims=True)
+
+        da, cb_one, cc_one, strong = one(row_a), one(row_b), one(row_c), one(row_s)
+        dc = wrap(lax.broadcasted_iota(i32, (8, N), 1).astype(f32) - cc_one)
+        rest = dc * dc + (da * da + SOFTEN)
         row = lax.broadcasted_iota(i32, (8, N), 0).astype(f32)
-        first = jnp.floor((center[1] - 16.0) * 0.125).astype(i32)
+        first = jnp.floor((jnp.sum(cb_one) - 16.0) * 0.125).astype(i32)
 
         def fix(step, _):
             group = first + step
@@ -295,7 +292,7 @@
             @pl.when((i >= 0) & (i < HALF // 8))
             def _():
                 r = pl.ds(pl.multiple_of(8 * group, 8), 8)
-                db = wrap(row + ((8 * group).astype(f32) - center[1]))
+                db = wrap(row + ((8 * group).astype(f32) - cb_one))
                 u = db * db + rest
                 k = lax.rsqrt(u)
                 full = erf(u * k) * k
@@ -403,11 +400,10 @@
 
     acc_ref[0] = jnp.zeros(acc_ref.shape[1:], f32)
     def step(t, _):
-        acc_ref[0] += product(2 * t, 0, 0)
-        acc_ref[0] += product(2 * t + 1, 0, 0)
+        acc_ref[0] += product(t, 0, 0)
         return 0
 
-    steps = 2 * pairs // TILE_CHUNKS
+    steps = 4 * pairs // TILE_CHUNKS
     lax.fori_loop(0, steps, step, 0)
 
     def rest(combo, _):
@@ -421,7 +417,7 @@
                 acc_ref[combo] += product(t, group_b, group_c)
                 return 0
 
-            lax.fori_loop(0, 2 * steps, extra, 0)
+            lax.fori_loop(0, steps, extra, 0)
 
         return 0
 
@@ -549,13 +545,12 @@
     slots = coefficients.shape[2]
     sources = lax.axis_size("pw")
     planes = sources
-    plane = lax.axis_index("pw").astype(i32)
     first_table, second_table = tables(planes)
 
     sent = pl.pallas_call(
         columns_kernel,
         out_shape=jax.ShapeDtypeStruct((planes, 8, LANE), f32),
-        in_specs=smem(1) + anywhere(2),
+        in_specs=anywhere(2),
         out_specs=vmem(1)[0],
         scratch_shapes=[
             pltpu.VMEM((2, slots, N), f32),
@@ -566,12 +561,11 @@
         ],
         compiler_params=params(54),
         name="columns",
-    )(plane[None], coefficients.reshape(2, slots, N), jnp.asarray(first_table))
-    own, sent = lax.optimization_barrier((tile_list[0], sent))
+    )(coefficients.reshape(2, slots, N), jnp.asarray(first_table))
+    own = tile_list[0]
     other = lax.ppermute(own, "mm", [(0, 1), (1, 0)])
     first = lax.axis_index("mm") == 0
     listed = jnp.concatenate([jnp.where(first, own, other), jnp.where(first, other, own)])
-    listed_col = jnp.pad(listed, (0, LANE - 32), constant_values=-1)[:, None]
 
     recv = lax.all_to_all(sent, "pw", 0, 0, tiled=True)
 
@@ -585,13 +579,13 @@
             pltpu.HBM((32, HALF, N), f32),
             jax.ShapeDtypeStruct((N, LANE), f32),
             jax.ShapeDtypeStruct((32, N), f32),
-            jax.ShapeDtypeStruct((LANE, 8), f32),
+            jax.ShapeDtypeStruct((32, 8), f32),
             jax.ShapeDtypeStruct((4, sources // 2, LANE), f32),
             jax.ShapeDtypeStruct((4, sources // 2, LANE), f32),
             jax.ShapeDtypeStruct((sources // 2, 8, LANE), f32),
             jax.ShapeDtypeStruct((16,), i32),
         ),
-        in_specs=smem(5) + vmem(5),
+        in_specs=vmem(5),
         out_specs=tuple(vmem(1) + anywhere(1) + vmem(6) + smem(1)),
         scratch_shapes=[
             pltpu.VMEM((N, LANE), f32),
@@ -604,12 +598,7 @@
         compiler_params=params(50),
         name="charges",
     )(
-        listed,
-        charge_cell,
-        charge_frac,
-        charge[None],
-        plane[None],
-        listed_col,
+        listed[:, None],
         charge_cell,
         charge_frac,
         charge[None],

time: 61.7 us -> 58.8 us (0.953)
  blocking collectives: 18.6 us -> 16 us
  waiting for transfers between devices: 4.35 us -> 5.15 us
    all_to_all x1, blocking collectives: 18.6 us -> 16 us  [local(): lax.all_to_all(jnp.broadcast_to(push[None], (sources, 1, LANE)), 'pw', 0,...]
    all_to_all x1, waiting for transfers between devices: 2.18 us -> 4 us  [local(): recv = lax.all_to_all(sent, 'pw', 0, 0, tiled=True)]
    ppermute x1, waiting for transfers between devices: 1.02 us -> 0.01 us  [local(): other = lax.ppermute(own, 'mm', [(0, 1), (1, 0)])]
    pallas_call x1, Pallas kernels: 13.2 us -> 12.4 us  [local(): pl.pallas_call(grid_kernel, out_shape=(jax.ShapeDtypeStruct((2, N, N), f3...]
  transfers between devices with their start and end apart: 3 -> 3, of which waited for: 3 -> 2; matrix products, arithmetic and copies ran while one was open for 0% -> 0% of each run, Pallas kernels for 11% -> 17%
where the time goes in v9:
time: 58.8 us; the launch traced here: 58.5 us
  Pallas kernels  24.8 us (42%)
  blocking collectives  16 us (27%)
  starting transfers between devices  11.5 us (20%)
  waiting for transfers between devices  5.15 us (9%)
  between operations  0.79 us (1%)
    all_to_all x1, blocking collectives, local(): lax.all_to_all(jnp.broadcast_to(push[None], (sources, 1, LANE)), 'pw', 0,...  16 us
    pallas_call x1, Pallas kernels, local(): pl.pallas_call(grid_kernel, out_shape=(jax.ShapeDtypeStruct((2, N, N), f3...  12.4 us
    all_to_all x1, starting transfers between devices, local(): recv = lax.all_to_all(sent, 'pw', 0, 0, tiled=True)  11.3 us
    pallas_call x1, Pallas kernels, local(): pl.pallas_call(charges_kernel, out_shape=(jax.ShapeDtypeStruct((N, N), f3...  6.88 us
    all_to_all x1, waiting for transfers between devices, local(): recv = lax.all_to_all(sent, 'pw', 0, 0, tiled=True)  4 us
    pallas_call x1, Pallas kernels, local(): pl.pallas_call(columns_kernel, out_shape=jax.ShapeDtypeStruct((planes, 8,...  3.26 us
    pallas_call x1, Pallas kernels, local(): pl.pallas_call(spread_kernel, out_shape=jax.ShapeDtypeStruct((3, charge.s...  2.24 us
  transfers between devices with their start and end apart: 3, of which 2 were waited for; matrix products, arithmetic and copies ran while one was open for 0% of the time, Pallas kernels for 17%

profile of v9, /device:TPU:0, one launch (start us, length us, event | category | flops | bytes accessed | tf_op | source)
XLA Modules:
  0.0 58.5 jit_solution(12014635936579027497)
XLA Ops:
  0.6 0.0 copy-start.4
  0.6 0.1 collective-permute-start
  0.7 0.0 copy-start.5
  0.7 0.0 copy-start.1
  0.8 0.0 copy-start.2
  0.8 0.0 copy-start.3
  0.8 0.0 copy-start
  0.8 3.3 %columns.1 = f32[64,8,128]{2,1,0:T(8,128)} custom-call(f32[2,448,384]{2,1,0:T(8,128)} %bitcast.15, bf16[256,768]{1,0:T(8,128)(2,1)} %constant.12.clone.table_in), custom_call_target="tpu_custom_call" | custom-call | tf_op jit(solution)/shard_map/columns/pallas_call | solution.py:550
  4.0 11.3 %all-to-all-start = ((f32[64,8,128]{2,1,0:T(8,128)}), f32[64,8,128]{2,1,0:T(8,128)S(1)}, u32[]{:S(2)}, u32[]{:S(2)}) async-start(f32[64,8,128]{2,1,0:T(8,128)} %columns.1), calls=%async_computation | async-start | bytes 524288 | tf_op jit(solution)/shard_map/all_to_all | solution.py:570
  15.3 0.0 copy-done.4
  15.4 0.1 reshape.16
  15.5 0.0 collective-permute-done
  15.5 0.0 copy-done.5
  15.5 0.1 add_bitcast_fusion
  15.6 0.1 copy.12.list_ref
  15.7 0.0 copy-done.1
  15.7 0.0 copy-done.2
  15.7 0.0 copy-done.3
  15.7 6.9 %charges.1 = (f32[384,384]{1,0:T(8,128)S(1)}, f32[32,192,384]{2,1,0:T(8,128)}, f32[384,128]{1,0:T(8,128)S(1)}, f32[32,384]{1,0:T(8,128)S(1)}, f32[32,8]{1,0:T(8,...) custom-call(s32[32,1]{1,0:T(8,128)S(1)} %copy.12.list_ref, ...), custom_call_target="tpu_custom_call" | custom-call | tf_op jit(solution)/shard_map/charges/pallas_call | solution.py:575
  22.6 4.0 %all-to-all-done.recv_ref = f32[64,8,128]{2,1,0:T(8,128)S(1)} async-done(((f32[64,8,128]{2,1,0:T(8,128)}), f32[64,8,128]{2,1,0:T(8,128)S(1)}, u32[]{:S(2)}, u32[]{:S(2)}) %all-to-all-start) | async-done | bytes 262176 | tf_op jit(solution)/shard_map/all_to_all | solution.py:570
  26.6 0.0 copy-done
  26.6 12.4 %grid.1 = (f32[2,384,384]{2,1,0:T(8,128)}, f32[1,128]{1,0:T(1,128)S(1)}) custom-call(s32[16]{0:T(128)S(1)} %get-tuple-element.13.plan_s, f32[64,8,128]{2,1,0:T(8,128)S(1)} %all-to-all-done.recv_ref, f32[32,8,128]{2,1,0:T(8,128)S(1)} %get-tuple-element.14.owner_ref, f32[4,32,128]{2,1,0:T(8,128)S(1)} %get-tuple-element.15.gb_ref, ...), custom_call_target="tpu_custom_call" | custom-call | tf_op jit(solution)/shard_map/grid/pallas_call | solution.py:608
  39.0 0.1 collective-permute-start.1
  39.1 1.1 %collective-permute-done.1 = f32[1,128]{1,0:T(1,128)S(1)} collective-permute-done((f32[1,128]{1,0:T(1,128)S(1)}, f32[1,128]{1,0:T(1,128)S(1)}, u32[]{:S(2)}, u32[]{:S(2)}) %collective-permute-start.1) | collective-permute-done | bytes 544 | tf_op jit(solution)/shard_map/ppermute | solution.py:634
  40.2 16.0 %all_to_all.10 = f32[64,1,128]{2,1,0:T(1,128)S(1)} all-to-all(f32[64,1,128]{2,1,0:T(1,128)S(1)} %broadcast_in_dim.21), channel_id=1, replica_groups=mesh['pw'=64,'mm'=2] {'pw'}, dimensions={0} | all-to-all | bytes 65536 | tf_op jit(solution)/shard_map/all_to_all | solution.py:635
  56.3 2.2 %spread.1 = f32[3,512]{1,0:T(4,128)} custom-call(f32[64,128]{1,0:T(8,128)S(1)} %bitcast.13), custom_call_target="tpu_custom_call" | custom-call | tf_op jit(solution)/shard_map/spread/pallas_call | solution.py:638
  (4 shorter events, 0.0 us)
Async XLA Ops:
  0.6 14.7 %copy-start.4 = (s32[28672]{0:T(1024)S(1)}, s32[28672]{0:T(1024)}, u32[]{:S(2)}) copy-start(s32[28672]{0:T(1024)} %param.9) | copy-start | bytes 344068
  0.6 14.8 %collective-permute-start = (s32[16]{0:T(128)}, s32[16]{0:T(128)S(1)}, u32[]{:S(2)}, u32[]{:S(2)}) collective-permute-start(s32[16]{0:T(128)} %bitcast.16), channel_id=1, source_target_pairs={{0,1},{1,0},{2,3},{3,2},{4,5},{5,4},{6,7},{7,6},{8,9},{9,8},{10,11... | collective-permute-start | bytes 200 | tf_op jit(solution)/shard_map/ppermute | solution.py:566
  0.7 14.7 %copy-start.5 = (s32[1,16]{1,0:T(1,128)S(1)}, s32[1,16]{1,0:T(1,128)}, u32[]{:S(2)}) copy-start(s32[1,16]{1,0:T(1,128)} %param.13) | copy-start | bytes 196
  0.7 14.9 %copy-start.1 = (s32[3,512]{1,0:T(4,128)S(1)}, s32[3,512]{1,0:T(4,128)}, u32[]{:S(2)}) copy-start(s32[3,512]{1,0:T(4,128)} %cell_ref.1) | copy-start | bytes 18436
  0.8 14.9 %copy-start.2 = (f32[3,512]{1,0:T(4,128)S(1)}, f32[3,512]{1,0:T(4,128)}, u32[]{:S(2)}) copy-start(f32[3,512]{1,0:T(4,128)} %frac_ref.1) | copy-start | bytes 18436
  0.8 14.9 %copy-start.3 = (f32[512]{0:T(512)S(1)}, f32[512]{0:T(512)}, u32[]{:S(2)}) copy-start(f32[512]{0:T(512)} %param.12) | copy-start | bytes 6148
  0.8 25.8 %copy-start = (bf16[1536,384]{1,0:T(8,128)(2,1)S(1)}, bf16[1536,384]{1,0:T(8,128)(2,1)}, u32[]{:S(2)}) copy-start(bf16[1536,384]{1,0:T(8,128)(2,1)} %constant.13.clone.table_ref) | copy-start | bytes 3538948
  4.0 22.5 %all-to-all-start = ((f32[64,8,128]{2,1,0:T(8,128)}), f32[64,8,128]{2,1,0:T(8,128)S(1)}, u32[]{:S(2)}, u32[]{:S(2)}) async-start(f32[64,8,128]{2,1,0:T(8,128)} %columns.1), calls=%async_computation | async-start | bytes 524288 | tf_op jit(solution)/shard_map/all_to_all | solution.py:570
  39.0 1.2 %collective-permute-start.1 = (f32[1,128]{1,0:T(1,128)S(1)}, f32[1,128]{1,0:T(1,128)S(1)}, u32[]{:S(2)}, u32[]{:S(2)}) collective-permute-start(f32[1,128]{1,0:T(1,128)S(1)} %get-tuple-element.23), channel_id=1, source_target_pairs={{0,1},{1,0},{2,3},{3,2},{4,5},{5,4},{6,7},{7,6},{8,9},{9,8},{10,11... | collective-permute-start | bytes 1544 | tf_op jit(solution)/shard_map/ppermute | solution.py:634

commit v10 on v9

--- a/solution.py
+++ b/solution.py
@@ -513,16 +513,31 @@
 
 def spread_kernel(terms_ref, out_ref):
     terms = terms_ref[...]
-    charges = out_ref.shape[1]
-    lane = lax.broadcasted_iota(i32, (terms.shape[0], charges), 1).astype(f32)
-    totals = [jnp.zeros((terms.shape[0], charges), f32)] * 3
+    sources = terms.shape[0]
+    width = out_ref.shape[1] // 2
+    turned = jnp.transpose(jnp.concatenate([terms, pltpu.roll(terms, LANE - 1, 1)], axis=0))
+    rows = []
+    for axis in range(3):
+        picked = [32 * axis + 2 * k for k in range(16)]
+        rows.append(jnp.concatenate([turned[r : r + 1, :] for r in picked], axis=1))
+    value = jnp.concatenate(rows, axis=0)
+    first = value.astype(bf16).astype(f32)
+    second = (value - first).astype(bf16).astype(f32)
+    third = value - first - second
+    zeros = jnp.zeros((7, value.shape[1]), f32)
+    parts = jnp.concatenate([first, second, third, zeros], axis=0).astype(bf16)
+    iota = lax.broadcasted_iota(i32, (sources, width), 1).astype(f32).astype(bf16)
+    one, zero = jnp.ones((sources, width), bf16), jnp.zeros((sources, width), bf16)
+    hots = []
     for q in range(32):
-        hot = terms[:, 96 + q : 97 + q] == lane
-        for axis in range(3):
-            value = terms[:, 32 * axis + q : 32 * axis + q + 1]
-            totals[axis] = totals[axis] + jnp.where(hot, value, 0.0)
-    for axis in range(3):
-        out_ref[axis : axis + 1, :] = jnp.sum(totals[axis], axis=0, keepdims=True)
+        number = terms[:, 96 + q : 97 + q]
+        hot = []
+        for half in range(2):
+            wide = jnp.broadcast_to(number - half * width, (sources, width)).astype(bf16)
+            hot.append(jnp.where(iota == wide, one, zero))
+        hots.append(jnp.concatenate(hot, axis=1))
+    result = mm(parts, jnp.concatenate(hots, axis=0))
+    out_ref[...] = result[0:3] + result[3:6] + result[6:9]
 
 
 def vmem(count):

time: 58.8 us -> 57.6 us (0.980)
  Pallas kernels: 24.8 us -> 23.5 us
    pallas_call x1, Pallas kernels: 2.24 us -> 1.15 us  [local(): pl.pallas_call(spread_kernel, out_shape=jax.ShapeDtypeStruct((3, charge.s...]
where the time goes in v10:
time: 57.6 us
  Pallas kernels  23.5 us (41%)
  blocking collectives  16.2 us (28%)
  starting transfers between devices  11.5 us (20%)
  waiting for transfers between devices  5.32 us (9%)
  between operations  0.79 us (1%)
    all_to_all x1, blocking collectives, local(): lax.all_to_all(jnp.broadcast_to(push[None], (sources, 1, LANE)), 'pw', 0,...  16.2 us
    pallas_call x1, Pallas kernels, local(): pl.pallas_call(grid_kernel, out_shape=(jax.ShapeDtypeStruct((2, N, N), f3...  12.4 us
    all_to_all x1, starting transfers between devices, local(): recv = lax.all_to_all(sent, 'pw', 0, 0, tiled=True)  11.3 us
    pallas_call x1, Pallas kernels, local(): pl.pallas_call(charges_kernel, out_shape=(jax.ShapeDtypeStruct((N, N), f3...  6.71 us
    all_to_all x1, waiting for transfers between devices, local(): recv = lax.all_to_all(sent, 'pw', 0, 0, tiled=True)  4.17 us
    pallas_call x1, Pallas kernels, local(): pl.pallas_call(columns_kernel, out_shape=jax.ShapeDtypeStruct((planes, 8,...  3.26 us
  transfers between devices with their start and end apart: 3, of which 2 were waited for; matrix products, arithmetic and copies ran while one was open for 0% of the time, Pallas kernels for 17%

profile of v10, /device:TPU:0, one launch (start us, length us, event | category | flops | bytes accessed | tf_op | source)
XLA Modules:
  0.0 57.6 jit_solution(8354367212586735207)
XLA Ops:
  0.6 0.0 copy-start.4
  0.6 0.1 collective-permute-start
  0.7 0.0 copy-start.5
  0.7 0.0 copy-start.1
  0.8 0.0 copy-start.2
  0.8 0.0 copy-start.3
  0.8 0.0 copy-start
  0.8 3.3 %columns.1 = f32[64,8,128]{2,1,0:T(8,128)} custom-call(f32[2,448,384]{2,1,0:T(8,128)} %bitcast.15, bf16[256,768]{1,0:T(8,128)(2,1)} %constant.12.clone.table_in), custom_call_target="tpu_custom_call" | custom-call | tf_op jit(solution)/shard_map/columns/pallas_call | solution.py:565
  4.0 11.3 %all-to-all-start = ((f32[64,8,128]{2,1,0:T(8,128)}), f32[64,8,128]{2,1,0:T(8,128)S(1)}, u32[]{:S(2)}, u32[]{:S(2)}) async-start(f32[64,8,128]{2,1,0:T(8,128)} %columns.1), calls=%async_computation | async-start | bytes 524288 | tf_op jit(solution)/shard_map/all_to_all | solution.py:585
  15.3 0.0 copy-done.4
  15.4 0.1 reshape.16
  15.5 0.0 collective-permute-done
  15.5 0.0 copy-done.5
  15.5 0.1 add_bitcast_fusion
  15.6 0.1 copy.12.list_ref
  15.7 0.0 copy-done.1
  15.7 0.0 copy-done.2
  15.7 0.0 copy-done.3
  15.7 6.7 %charges.1 = (f32[384,384]{1,0:T(8,128)S(1)}, f32[32,192,384]{2,1,0:T(8,128)}, f32[384,128]{1,0:T(8,128)S(1)}, f32[32,384]{1,0:T(8,128)S(1)}, f32[32,8]{1,0:T(8,...) custom-call(s32[32,1]{1,0:T(8,128)S(1)} %copy.12.list_ref, ...), custom_call_target="tpu_custom_call" | custom-call | tf_op jit(solution)/shard_map/charges/pallas_call | solution.py:590
  22.4 4.2 %all-to-all-done.recv_ref = f32[64,8,128]{2,1,0:T(8,128)S(1)} async-done(((f32[64,8,128]{2,1,0:T(8,128)}), f32[64,8,128]{2,1,0:T(8,128)S(1)}, u32[]{:S(2)}, u32[]{:S(2)}) %all-to-all-start) | async-done | bytes 262176 | tf_op jit(solution)/shard_map/all_to_all | solution.py:585
  26.6 0.0 copy-done
  26.6 12.4 %grid.1 = (f32[2,384,384]{2,1,0:T(8,128)}, f32[1,128]{1,0:T(1,128)S(1)}) custom-call(s32[16]{0:T(128)S(1)} %get-tuple-element.13.plan_s, f32[64,8,128]{2,1,0:T(8,128)S(1)} %all-to-all-done.recv_ref, f32[32,8,128]{2,1,0:T(8,128)S(1)} %get-tuple-element.14.owner_ref, f32[4,32,128]{2,1,0:T(8,128)S(1)} %get-tuple-element.15.gb_ref, ...), custom_call_target="tpu_custom_call" | custom-call | tf_op jit(solution)/shard_map/grid/pallas_call | solution.py:623
  39.0 0.1 collective-permute-start.1
  39.1 1.1 %collective-permute-done.1 = f32[1,128]{1,0:T(1,128)S(1)} collective-permute-done((f32[1,128]{1,0:T(1,128)S(1)}, f32[1,128]{1,0:T(1,128)S(1)}, u32[]{:S(2)}, u32[]{:S(2)}) %collective-permute-start.1) | collective-permute-done | bytes 544 | tf_op jit(solution)/shard_map/ppermute | solution.py:649
  40.2 16.2 %all_to_all.10 = f32[64,1,128]{2,1,0:T(1,128)S(1)} all-to-all(f32[64,1,128]{2,1,0:T(1,128)S(1)} %broadcast_in_dim.21), channel_id=1, replica_groups=mesh['pw'=64,'mm'=2] {'pw'}, dimensions={0} | all-to-all | bytes 65536 | tf_op jit(solution)/shard_map/all_to_all | solution.py:650
  56.5 1.1 %spread.1 = f32[3,512]{1,0:T(4,128)} custom-call(f32[64,128]{1,0:T(8,128)S(1)} %bitcast.13), custom_call_target="tpu_custom_call" | custom-call | tf_op jit(solution)/shard_map/spread/pallas_call | solution.py:653
  (4 shorter events, 0.0 us)
Async XLA Ops:
  0.6 14.7 %copy-start.4 = (s32[28672]{0:T(1024)S(1)}, s32[28672]{0:T(1024)}, u32[]{:S(2)}) copy-start(s32[28672]{0:T(1024)} %param.9) | copy-start | bytes 344068
  0.6 14.8 %collective-permute-start = (s32[16]{0:T(128)}, s32[16]{0:T(128)S(1)}, u32[]{:S(2)}, u32[]{:S(2)}) collective-permute-start(s32[16]{0:T(128)} %bitcast.16), channel_id=1, source_target_pairs={{0,1},{1,0},{2,3},{3,2},{4,5},{5,4},{6,7},{7,6},{8,9},{9,8},{10,11... | collective-permute-start | bytes 200 | tf_op jit(solution)/shard_map/ppermute | solution.py:581
  0.7 14.7 %copy-start.5 = (s32[1,16]{1,0:T(1,128)S(1)}, s32[1,16]{1,0:T(1,128)}, u32[]{:S(2)}) copy-start(s32[1,16]{1,0:T(1,128)} %param.13) | copy-start | bytes 196
  0.7 14.9 %copy-start.1 = (s32[3,512]{1,0:T(4,128)S(1)}, s32[3,512]{1,0:T(4,128)}, u32[]{:S(2)}) copy-start(s32[3,512]{1,0:T(4,128)} %cell_ref.1) | copy-start | bytes 18436
  0.8 14.9 %copy-start.2 = (f32[3,512]{1,0:T(4,128)S(1)}, f32[3,512]{1,0:T(4,128)}, u32[]{:S(2)}) copy-start(f32[3,512]{1,0:T(4,128)} %frac_ref.1) | copy-start | bytes 18436
  0.8 14.9 %copy-start.3 = (f32[512]{0:T(512)S(1)}, f32[512]{0:T(512)}, u32[]{:S(2)}) copy-start(f32[512]{0:T(512)} %param.12) | copy-start | bytes 6148
  0.8 25.8 %copy-start = (bf16[1536,384]{1,0:T(8,128)(2,1)S(1)}, bf16[1536,384]{1,0:T(8,128)(2,1)}, u32[]{:S(2)}) copy-start(bf16[1536,384]{1,0:T(8,128)(2,1)} %constant.13.clone.table_ref) | copy-start | bytes 3538948
  4.0 22.5 %all-to-all-start = ((f32[64,8,128]{2,1,0:T(8,128)}), f32[64,8,128]{2,1,0:T(8,128)S(1)}, u32[]{:S(2)}, u32[]{:S(2)}) async-start(f32[64,8,128]{2,1,0:T(8,128)} %columns.1), calls=%async_computation | async-start | bytes 524288 | tf_op jit(solution)/shard_map/all_to_all | solution.py:585
  39.0 1.2 %collective-permute-start.1 = (f32[1,128]{1,0:T(1,128)S(1)}, f32[1,128]{1,0:T(1,128)S(1)}, u32[]{:S(2)}, u32[]{:S(2)}) collective-permute-start(f32[1,128]{1,0:T(1,128)S(1)} %get-tuple-element.23), channel_id=1, source_target_pairs={{0,1},{1,0},{2,3},{3,2},{4,5},{5,4},{6,7},{7,6},{8,9},{9,8},{10,11... | collective-permute-start | bytes 1544 | tf_op jit(solution)/shard_map/ppermute | solution.py:649

commit v11 on v10

--- a/solution.py
+++ b/solution.py
@@ -19,7 +19,7 @@
 VOLUME = SPACING**3
 PEAK = 2.0 / math.sqrt(math.pi)
 EMPTY = N * N
-TILE_CHUNKS = 32
+TILE_CHUNKS = 64
 WINDOW = 208
 BLOCKS = N // 16
 NT = (((1,), (1,)), ((), ()))
@@ -280,29 +280,21 @@
         da, cb_one, cc_one, strong = one(row_a), one(row_b), one(row_c), one(row_s)
         dc = wrap(lax.broadcasted_iota(i32, (8, N), 1).astype(f32) - cc_one)
         rest = dc * dc + (da * da + SOFTEN)
-        row = lax.broadcasted_iota(i32, (8, N), 0).astype(f32)
-        first = jnp.floor((jnp.sum(cb_one) - 16.0) * 0.125).astype(i32)
-
-        def fix(step, _):
-            group = first + step
-            group = jnp.where(group < 0, group + N // 8, group)
-            group = jnp.where(group >= N // 8, group - N // 8, group)
-            i = group - base
-
-            @pl.when((i >= 0) & (i < HALF // 8))
-            def _():
-                r = pl.ds(pl.multiple_of(8 * group, 8), 8)
-                db = wrap(row + ((8 * group).astype(f32) - cb_one))
-                u = db * db + rest
-                k = lax.rsqrt(u)
-                full = erf(u * k) * k
-                slope = k * k * (PEAK * jnp.exp(-u) - full)
-                slope_ref[q, pl.ds(pl.multiple_of(8 * i, 8), 8), :] = slope
-                pot_ref[r, :] += strong * (full - k)
-
-            return 0
-
-        lax.fori_loop(0, 6, fix, 0)
+        local = jnp.floor((jnp.sum(cb_one) - 16.0) * 0.125).astype(i32) - base
+        local = jnp.where(local < -5, local + N // 8, local)
+        local = jnp.where(local >= N // 8 - 5, local - N // 8, local)
+
+        @pl.when(local < HALF // 8)
+        def _():
+            i = jnp.clip(local, 0, HALF // 8 - 6)
+            row = lax.broadcasted_iota(i32, (48, N), 0).astype(f32)
+            db = wrap(row + ((8 * (base + i)).astype(f32) - cb_one))
+            u = db * db + rest[:1]
+            k = lax.rsqrt(u)
+            full = erf(u * k) * k
+            rows = pl.ds(pl.multiple_of(8 * i, 8), 48)
+            slope_ref[q, rows, :] = k * k * (PEAK * jnp.exp(-u) - full)
+            pot_ref[pl.ds(pl.multiple_of(8 * (base + i), 8), 48), :] += strong * (full - k)
 
     copies = []
     for a in range(0, 16, 2):

time: 57.6 us -> 57.1 us (level)
    pallas_call x1, Pallas kernels: 12.4 us -> 11.8 us  [local(): pl.pallas_call(grid_kernel, out_shape=(jax.ShapeDtypeStruct((2, N, N), f3...]
  transfers between devices with their start and end apart: 3 -> 3, of which waited for: 2 -> 2; matrix products, arithmetic and copies ran while one was open for 0% -> 0% of each run, Pallas kernels for 17% -> 18%
where the time goes in v11:
time: 57.1 us; the launch traced here: 56.7 us
  Pallas kernels  23.2 us (41%)
  blocking collectives  16 us (28%)
  starting transfers between devices  11.5 us (20%)
  waiting for transfers between devices  5.05 us (9%)
  between operations  0.79 us (1%)
    all_to_all x1, blocking collectives, local(): lax.all_to_all(jnp.broadcast_to(push[None], (sources, 1, LANE)), 'pw', 0,...  16 us
    pallas_call x1, Pallas kernels, local(): pl.pallas_call(grid_kernel, out_shape=(jax.ShapeDtypeStruct((2, N, N), f3...  11.8 us
    all_to_all x1, starting transfers between devices, local(): recv = lax.all_to_all(sent, 'pw', 0, 0, tiled=True)  11.3 us
    pallas_call x1, Pallas kernels, local(): pl.pallas_call(charges_kernel, out_shape=(jax.ShapeDtypeStruct((N, N), f3...  6.98 us
    all_to_all x1, waiting for transfers between devices, local(): recv = lax.all_to_all(sent, 'pw', 0, 0, tiled=True)  3.9 us
    pallas_call x1, Pallas kernels, local(): pl.pallas_call(columns_kernel, out_shape=jax.ShapeDtypeStruct((planes, 8,...  3.26 us
    ppermute x1, waiting for transfers between devices, local(): push = push + lax.ppermute(push, 'mm', [(0, 1), (1, 0)])  1.15 us
    pallas_call x1, Pallas kernels, local(): pl.pallas_call(spread_kernel, out_shape=jax.ShapeDtypeStruct((3, charge.s...  1.15 us
  transfers between devices with their start and end apart: 3, of which 2 were waited for; matrix products, arithmetic and copies ran while one was open for 0% of the time, Pallas kernels for 18%

profile of v11, /device:TPU:0, one launch (start us, length us, event | category | flops | bytes accessed | tf_op | source)
XLA Modules:
  0.0 56.7 jit_solution(6495488516314592950)
XLA Ops:
  0.6 0.0 copy-start.4
  0.6 0.1 collective-permute-start
  0.7 0.0 copy-start.5
  0.7 0.0 copy-start.1
  0.8 0.0 copy-start.2
  0.8 0.0 copy-start.3
  0.8 0.0 copy-start
  0.8 3.3 %columns.1 = f32[64,8,128]{2,1,0:T(8,128)} custom-call(f32[2,448,384]{2,1,0:T(8,128)} %bitcast.15, bf16[256,768]{1,0:T(8,128)(2,1)} %constant.12.clone.table_in), custom_call_target="tpu_custom_call" | custom-call | tf_op jit(solution)/shard_map/columns/pallas_call | solution.py:557
  4.0 11.3 %all-to-all-start = ((f32[64,8,128]{2,1,0:T(8,128)}), f32[64,8,128]{2,1,0:T(8,128)S(1)}, u32[]{:S(2)}, u32[]{:S(2)}) async-start(f32[64,8,128]{2,1,0:T(8,128)} %columns.1), calls=%async_computation | async-start | bytes 524288 | tf_op jit(solution)/shard_map/all_to_all | solution.py:577
  15.3 0.0 copy-done.4
  15.4 0.1 reshape.16
  15.5 0.0 collective-permute-done
  15.5 0.0 copy-done.5
  15.5 0.1 add_bitcast_fusion
  15.6 0.1 copy.12.list_ref
  15.7 0.0 copy-done.1
  15.7 0.0 copy-done.2
  15.7 0.0 copy-done.3
  15.7 7.0 %charges.1 = (f32[384,384]{1,0:T(8,128)S(1)}, f32[32,192,384]{2,1,0:T(8,128)}, f32[384,128]{1,0:T(8,128)S(1)}, f32[32,384]{1,0:T(8,128)S(1)}, f32[32,8]{1,0:T(8,...) custom-call(s32[32,1]{1,0:T(8,128)S(1)} %copy.12.list_ref, ...), custom_call_target="tpu_custom_call" | custom-call | tf_op jit(solution)/shard_map/charges/pallas_call | solution.py:582
  22.7 3.9 %all-to-all-done.recv_ref = f32[64,8,128]{2,1,0:T(8,128)S(1)} async-done(((f32[64,8,128]{2,1,0:T(8,128)}), f32[64,8,128]{2,1,0:T(8,128)S(1)}, u32[]{:S(2)}, u32[]{:S(2)}) %all-to-all-start) | async-done | bytes 262176 | tf_op jit(solution)/shard_map/all_to_all | solution.py:577
  26.6 0.0 copy-done
  26.6 11.8 %grid.1 = (f32[2,384,384]{2,1,0:T(8,128)}, f32[1,128]{1,0:T(1,128)S(1)}) custom-call(s32[16]{0:T(128)S(1)} %get-tuple-element.13.plan_s, f32[64,8,128]{2,1,0:T(8,128)S(1)} %all-to-all-done.recv_ref, f32[32,8,128]{2,1,0:T(8,128)S(1)} %get-tuple-element.14.owner_ref, f32[4,32,128]{2,1,0:T(8,128)S(1)} %get-tuple-element.15.gb_ref, ...), custom_call_target="tpu_custom_call" | custom-call | tf_op jit(solution)/shard_map/grid/pallas_call | solution.py:615
  38.4 0.1 collective-permute-start.1
  38.5 1.1 %collective-permute-done.1 = f32[1,128]{1,0:T(1,128)S(1)} collective-permute-done((f32[1,128]{1,0:T(1,128)S(1)}, f32[1,128]{1,0:T(1,128)S(1)}, u32[]{:S(2)}, u32[]{:S(2)}) %collective-permute-start.1) | collective-permute-done | bytes 544 | tf_op jit(solution)/shard_map/ppermute | solution.py:641
  39.6 16.0 %all_to_all.10 = f32[64,1,128]{2,1,0:T(1,128)S(1)} all-to-all(f32[64,1,128]{2,1,0:T(1,128)S(1)} %broadcast_in_dim.21), channel_id=1, replica_groups=mesh['pw'=64,'mm'=2] {'pw'}, dimensions={0} | all-to-all | bytes 65536 | tf_op jit(solution)/shard_map/all_to_all | solution.py:642
  55.6 1.1 %spread.1 = f32[3,512]{1,0:T(4,128)} custom-call(f32[64,128]{1,0:T(8,128)S(1)} %bitcast.13), custom_call_target="tpu_custom_call" | custom-call | tf_op jit(solution)/shard_map/spread/pallas_call | solution.py:645
  (4 shorter events, 0.0 us)
Async XLA Ops:
  0.6 14.7 %copy-start.4 = (s32[28672]{0:T(1024)S(1)}, s32[28672]{0:T(1024)}, u32[]{:S(2)}) copy-start(s32[28672]{0:T(1024)} %param.9) | copy-start | bytes 344068
  0.6 14.8 %collective-permute-start = (s32[16]{0:T(128)}, s32[16]{0:T(128)S(1)}, u32[]{:S(2)}, u32[]{:S(2)}) collective-permute-start(s32[16]{0:T(128)} %bitcast.16), channel_id=1, source_target_pairs={{0,1},{1,0},{2,3},{3,2},{4,5},{5,4},{6,7},{7,6},{8,9},{9,8},{10,11... | collective-permute-start | bytes 200 | tf_op jit(solution)/shard_map/ppermute | solution.py:573
  0.7 14.7 %copy-start.5 = (s32[1,16]{1,0:T(1,128)S(1)}, s32[1,16]{1,0:T(1,128)}, u32[]{:S(2)}) copy-start(s32[1,16]{1,0:T(1,128)} %param.13) | copy-start | bytes 196
  0.7 14.9 %copy-start.1 = (s32[3,512]{1,0:T(4,128)S(1)}, s32[3,512]{1,0:T(4,128)}, u32[]{:S(2)}) copy-start(s32[3,512]{1,0:T(4,128)} %cell_ref.1) | copy-start | bytes 18436
  0.8 14.9 %copy-start.2 = (f32[3,512]{1,0:T(4,128)S(1)}, f32[3,512]{1,0:T(4,128)}, u32[]{:S(2)}) copy-start(f32[3,512]{1,0:T(4,128)} %frac_ref.1) | copy-start | bytes 18436
  0.8 14.9 %copy-start.3 = (f32[512]{0:T(512)S(1)}, f32[512]{0:T(512)}, u32[]{:S(2)}) copy-start(f32[512]{0:T(512)} %param.12) | copy-start | bytes 6148
  0.8 25.8 %copy-start = (bf16[1536,384]{1,0:T(8,128)(2,1)S(1)}, bf16[1536,384]{1,0:T(8,128)(2,1)}, u32[]{:S(2)}) copy-start(bf16[1536,384]{1,0:T(8,128)(2,1)} %constant.13.clone.table_ref) | copy-start | bytes 3538948
  4.0 22.5 %all-to-all-start = ((f32[64,8,128]{2,1,0:T(8,128)}), f32[64,8,128]{2,1,0:T(8,128)S(1)}, u32[]{:S(2)}, u32[]{:S(2)}) async-start(f32[64,8,128]{2,1,0:T(8,128)} %columns.1), calls=%async_computation | async-start | bytes 524288 | tf_op jit(solution)/shard_map/all_to_all | solution.py:577
  38.4 1.2 %collective-permute-start.1 = (f32[1,128]{1,0:T(1,128)S(1)}, f32[1,128]{1,0:T(1,128)S(1)}, u32[]{:S(2)}, u32[]{:S(2)}) collective-permute-start(f32[1,128]{1,0:T(1,128)S(1)} %get-tuple-element.23), channel_id=1, source_target_pairs={{0,1},{1,0},{2,3},{3,2},{4,5},{5,4},{6,7},{7,6},{8,9},{9,8},{10,11... | collective-permute-start | bytes 1544 | tf_op jit(solution)/shard_map/ppermute | solution.py:641

commit v12 on v11

--- a/solution.py
+++ b/solution.py
@@ -22,6 +22,8 @@
 TILE_CHUNKS = 64
 WINDOW = 208
 BLOCKS = N // 16
+LAST = (14, 15)
+STORED = 30
 NT = (((1,), (1,)), ((), ()))
 TN = (((0,), (0,)), ((), ()))
 
@@ -153,6 +155,10 @@
     return s * num / den
 
 
+def place(last_ref, slope_ref, q):
+    return (last_ref, q - LAST[0]) if q in LAST else (slope_ref, q - 2 * (q // 16))
+
+
 def charges_kernel(
     list_ref,
     cell_ref,
@@ -160,6 +166,7 @@
     charge_ref,
     grid_ref,
     pot_ref,
+    last_ref,
     slope_out,
     offb_ref,
     offc_ref,
@@ -271,7 +278,7 @@
         weight = jnp.left_shift(weight, lane & 15).astype(f32)
         bits.append(jnp.sum(close * weight).astype(i32))
 
-    def fix_charge(q):
+    def fix_charge(q, target_ref, slot):
         base = (q >> 4) * (HALF // 8)
 
         def one(row):
@@ -293,12 +300,13 @@
             k = lax.rsqrt(u)
             full = erf(u * k) * k
             rows = pl.ds(pl.multiple_of(8 * i, 8), 48)
-            slope_ref[q, rows, :] = k * k * (PEAK * jnp.exp(-u) - full)
+            target_ref[slot, rows, :] = k * k * (PEAK * jnp.exp(-u) - full)
             pot_ref[pl.ds(pl.multiple_of(8 * (base + i), 8), 48), :] += strong * (full - k)
 
     copies = []
-    for a in range(0, 16, 2):
-        for half in range(2):
+    rounds = [(a, (0, 1)) for a in range(0, LAST[0], 2)] + [(LAST[0], (1,)), (LAST[0], (0,))]
+    for a, sides in rounds:
+        for half in sides:
             pair = (16 * half + a, 16 * half + a + 1)
             lanes = [(q, wide(uc_ref, q), wide(ec_ref, q), power(q)) for q in pair]
             for i in range(HALF // 8):
@@ -307,27 +315,38 @@
                 for q, ucq, ecq, strong in lanes:
                     k = lax.rsqrt(uab_ref[r, q : q + 1] + ucq)
                     e = eab_ref[r, q : q + 1] * ecq
-                    slope_ref[q, 8 * i : 8 * i + 8, :] = k * k * (e - k)
+                    target_ref, slot = place(last_ref, slope_ref, q)
+                    target_ref[slot, 8 * i : 8 * i + 8, :] = k * k * (e - k)
                     total = strong * k if total is None else total + strong * k
                 pot_ref[r, :] = total if a == 0 else pot_ref[r, :] + total
         found = [jnp.right_shift(value, a) & 3 for value in bits]
-        found = found[0] + 4 * found[1]
+        found = found[0] + 4 * found[1] if len(sides) == 2 else found[sides[0]]
 
         @pl.when(found > 0)
-        def _(a=a, found=found):
+        def _(a=a, sides=sides, found=found):
             def visit(j, _):
                 @pl.when((jnp.right_shift(found, j) & 1) > 0)
                 def _():
-                    fix_charge(16 * (j >> 1) + a + (j & 1))
+                    half = (j >> 1) + sides[0]
+                    q = 16 * half + a + (j & 1)
+                    if sides == (0,) and a == LAST[0]:
+                        fix_charge(q, last_ref, q - LAST[0])
+                    else:
+                        fix_charge(q, slope_ref, q - 2 * half)
 
                 return 0
 
-            lax.fori_loop(0, 4, visit, 0)
-
-        for q in (a, a + 1, 16 + a, 17 + a):
-            copy = pltpu.make_async_copy(slope_ref.at[q], slope_out.at[q], sems.at[q])
-            copy.start()
-            copies.append(copy)
+            lax.fori_loop(0, 2 * len(sides), visit, 0)
+
+        for half in sides:
+            for q in (16 * half + a, 16 * half + a + 1):
+                if q not in LAST:
+                    slot = q - 2 * half
+                    copy = pltpu.make_async_copy(
+                        slope_ref.at[slot], slope_out.at[slot], sems.at[slot]
+                    )
+                    copy.start()
+                    copies.append(copy)
     for copy in copies:
         copy.wait()
 
@@ -340,6 +359,7 @@
     gc_ref,
     table_ref,
     pot_ref,
+    last_ref,
     slope_in,
     offb_ref,
     offc_ref,
@@ -485,7 +505,8 @@
         scaled = jnp.zeros((8, LANE), f32)
         for i in range(HALF // 8):
             r = slice(base + 8 * i, base + 8 * i + 8)
-            w = dens_ref[r, :] * slope_ref[q, 8 * i : 8 * i + 8, :]
+            source_ref, slot = place(last_ref, slope_ref, q)
+            w = dens_ref[r, :] * source_ref[slot, 8 * i : 8 * i + 8, :]
             w = [w[:, k * LANE : (k + 1) * LANE] for k in range(3)]
             plain = [p + v for p, v in zip(plain, w)]
             scaled = scaled + (w[0] + w[1] + w[2]) * offb_ref[r, q : q + 1]
@@ -579,11 +600,12 @@
     blocks = col_map.reshape(sources, slots)
     grid = jnp.pad(blocks, ((0, 0), (0, 4 * LANE - slots)), constant_values=EMPTY)
 
-    pot, slope, offb, offc, col, gb, gc, owner, plan = pl.pallas_call(
+    pot, last, slope, offb, offc, col, gb, gc, owner, plan = pl.pallas_call(
         charges_kernel,
         out_shape=(
             jax.ShapeDtypeStruct((N, N), f32),
-            pltpu.HBM((32, HALF, N), f32),
+            jax.ShapeDtypeStruct((2, HALF, N), f32),
+            pltpu.HBM((STORED, HALF, N), f32),
             jax.ShapeDtypeStruct((N, LANE), f32),
             jax.ShapeDtypeStruct((32, N), f32),
             jax.ShapeDtypeStruct((32, 8), f32),
@@ -593,14 +615,14 @@
             jax.ShapeDtypeStruct((16,), i32),
         ),
         in_specs=vmem(5),
-        out_specs=tuple(vmem(1) + anywhere(1) + vmem(6) + smem(1)),
+        out_specs=tuple(vmem(2) + anywhere(1) + vmem(6) + smem(1)),
         scratch_shapes=[
             pltpu.VMEM((N, LANE), f32),
             pltpu.VMEM((N, LANE), f32),
             pltpu.VMEM((32, N), f32),
             pltpu.VMEM((32, N), f32),
-            pltpu.VMEM((32, HALF, N), f32),
-            pltpu.SemaphoreType.DMA((32,)),
+            pltpu.VMEM((STORED, HALF, N), f32),
+            pltpu.SemaphoreType.DMA((STORED,)),
         ],
         compiler_params=params(50),
         name="charges",
@@ -618,7 +640,7 @@
             jax.ShapeDtypeStruct((2, N, N), f32),
             jax.ShapeDtypeStruct((1, LANE), f32),
         ),
-        in_specs=smem(1) + vmem(6) + anywhere(1) + vmem(3),
+        in_specs=smem(1) + vmem(7) + anywhere(1) + vmem(3),
         out_specs=tuple(anywhere(1) + vmem(1)),
         scratch_shapes=[
             pltpu.VMEM((4, 4 * WINDOW, 2 * LANE), f32),
@@ -630,13 +652,13 @@
             pltpu.VMEM((N, N), f32),
             pltpu.VMEM((64, N), f32),
             pltpu.VMEM((2, N, N), f32),
-            pltpu.VMEM((32, HALF, N), f32),
+            pltpu.VMEM((STORED, HALF, N), f32),
             pltpu.VMEM((sources // 2, 8, LANE), f32),
             pltpu.SemaphoreType.DMA((2,)),
         ],
         compiler_params=params(50),
         name="grid",
-    )(plan, recv, owner, gb, gc, jnp.asarray(second_table), pot, slope, offb, offc, col)
+    )(plan, recv, owner, gb, gc, jnp.asarray(second_table), pot, last, slope, offb, offc, col)
 
     push = push + lax.ppermute(push, "mm", [(0, 1), (1, 0)])
     terms = lax.all_to_all(

time: 57.1 us -> 56.4 us (0.988)
  Pallas kernels: 23.2 us -> 22 us
  waiting for transfers between devices: 5.05 us -> 6.23 us
    pallas_call x1, Pallas kernels: 6.98 us -> 5.8 us  [local(): pl.pallas_call(charges_kernel, out_shape=(jax.ShapeDtypeStruct((N, N), f3...]
    all_to_all x1, waiting for transfers between devices: 3.9 us -> 5.08 us  [local(): recv = lax.all_to_all(sent, 'pw', 0, 0, tiled=True)]
  transfers between devices with their start and end apart: 3 -> 3, of which waited for: 2 -> 2; matrix products, arithmetic and copies ran while one was open for 0% -> 0% of each run, Pallas kernels for 18% -> 16%
where the time goes in v12:
time: 56.4 us; the launch traced here: 56.3 us
  Pallas kernels  22 us (39%)
  blocking collectives  15.5 us (27%)
  starting transfers between devices  11.5 us (20%)
  waiting for transfers between devices  6.23 us (11%)
  between operations  0.79 us (1%)
    all_to_all x1, blocking collectives, local(): lax.all_to_all(jnp.broadcast_to(push[None], (sources, 1, LANE)), 'pw', 0,...  15.5 us
    pallas_call x1, Pallas kernels, local(): pl.pallas_call(grid_kernel, out_shape=(jax.ShapeDtypeStruct((2, N, N), f3...  11.8 us
    all_to_all x1, starting transfers between devices, local(): recv = lax.all_to_all(sent, 'pw', 0, 0, tiled=True)  11.3 us
    pallas_call x1, Pallas kernels, local(): pl.pallas_call(charges_kernel, out_shape=(jax.ShapeDtypeStruct((N, N), f3...  5.8 us
    all_to_all x1, waiting for transfers between devices, local(): recv = lax.all_to_all(sent, 'pw', 0, 0, tiled=True)  5.08 us
    pallas_call x1, Pallas kernels, local(): pl.pallas_call(columns_kernel, out_shape=jax.ShapeDtypeStruct((planes, 8,...  3.26 us
    ppermute x1, waiting for transfers between devices, local(): push = push + lax.ppermute(push, 'mm', [(0, 1), (1, 0)])  1.15 us
    pallas_call x1, Pallas kernels, local(): pl.pallas_call(spread_kernel, out_shape=jax.ShapeDtypeStruct((3, charge.s...  1.15 us
  transfers between devices with their start and end apart: 3, of which 2 were waited for; matrix products, arithmetic and copies ran while one was open for 0% of the time, Pallas kernels for 16%

profile of v12, /device:TPU:0, one launch (start us, length us, event | category | flops | bytes accessed | tf_op | source)
XLA Modules:
  0.0 56.3 jit_solution(18379630030425877052)
XLA Ops:
  0.6 0.0 copy-start.4
  0.6 0.1 collective-permute-start
  0.7 0.0 copy-start.5
  0.7 0.0 copy-start.1
  0.8 0.0 copy-start.2
  0.8 0.0 copy-start.3
  0.8 0.0 copy-start
  0.8 3.3 %columns.1 = f32[64,8,128]{2,1,0:T(8,128)} custom-call(f32[2,448,384]{2,1,0:T(8,128)} %bitcast.15, bf16[256,768]{1,0:T(8,128)(2,1)} %constant.12.clone.table_in), custom_call_target="tpu_custom_call" | custom-call | tf_op jit(solution)/shard_map/columns/pallas_call | solution.py:578
  4.0 11.3 %all-to-all-start = ((f32[64,8,128]{2,1,0:T(8,128)}), f32[64,8,128]{2,1,0:T(8,128)S(1)}, u32[]{:S(2)}, u32[]{:S(2)}) async-start(f32[64,8,128]{2,1,0:T(8,128)} %columns.1), calls=%async_computation | async-start | bytes 524288 | tf_op jit(solution)/shard_map/all_to_all | solution.py:598
  15.3 0.0 copy-done.4
  15.4 0.1 reshape.16
  15.5 0.0 collective-permute-done
  15.5 0.0 copy-done.5
  15.5 0.1 add_bitcast_fusion
  15.6 0.1 copy.12.list_ref
  15.7 0.0 copy-done.1
  15.7 0.0 copy-done.2
  15.7 0.0 copy-done.3
  15.7 5.8 %charges.1 = (f32[384,384]{1,0:T(8,128)S(1)}, f32[2,192,384]{2,1,0:T(8,128)S(1)}, f32[30,192,384]{2,1,0:T(8,128)}, f32[384,128]{1,0:T(8,128)S(1)}, f32[32,384]{1...) custom-call(s32[32,1]{1,0:T(8,128)S(1)} %copy.12.list_ref, ...), custom_call_target="tpu_custom_call" | custom-call | tf_op jit(solution)/shard_map/charges/pallas_call | solution.py:603
  21.5 5.1 %all-to-all-done.recv_ref = f32[64,8,128]{2,1,0:T(8,128)S(1)} async-done(((f32[64,8,128]{2,1,0:T(8,128)}), f32[64,8,128]{2,1,0:T(8,128)S(1)}, u32[]{:S(2)}, u32[]{:S(2)}) %all-to-all-start) | async-done | bytes 262176 | tf_op jit(solution)/shard_map/all_to_all | solution.py:598
  26.6 0.0 copy-done
  26.6 11.8 %grid.1 = (f32[2,384,384]{2,1,0:T(8,128)}, f32[1,128]{1,0:T(1,128)S(1)}) custom-call(s32[16]{0:T(128)S(1)} %get-tuple-element.14.plan_s, f32[64,8,128]{2,1,0:T(8,128)S(1)} %all-to-all-done.recv_ref, f32[32,8,128]{2,1,0:T(8,128)S(1)} %get-tuple-element.15.owner_ref, f32[4,32,128]{2,1,0:T(8,128)S(1)} %get-tuple-element.16.gb_ref, ...), custom_call_target="tpu_custom_call" | custom-call | tf_op jit(solution)/shard_map/grid/pallas_call | solution.py:637
  38.4 0.1 collective-permute-start.1
  38.5 1.1 %collective-permute-done.1 = f32[1,128]{1,0:T(1,128)S(1)} collective-permute-done((f32[1,128]{1,0:T(1,128)S(1)}, f32[1,128]{1,0:T(1,128)S(1)}, u32[]{:S(2)}, u32[]{:S(2)}) %collective-permute-start.1) | collective-permute-done | bytes 544 | tf_op jit(solution)/shard_map/ppermute | solution.py:663
  39.7 15.5 %all_to_all.10 = f32[64,1,128]{2,1,0:T(1,128)S(1)} all-to-all(f32[64,1,128]{2,1,0:T(1,128)S(1)} %broadcast_in_dim.21), channel_id=1, replica_groups=mesh['pw'=64,'mm'=2] {'pw'}, dimensions={0} | all-to-all | bytes 65536 | tf_op jit(solution)/shard_map/all_to_all | solution.py:664
  55.1 1.1 %spread.1 = f32[3,512]{1,0:T(4,128)} custom-call(f32[64,128]{1,0:T(8,128)S(1)} %bitcast.13), custom_call_target="tpu_custom_call" | custom-call | tf_op jit(solution)/shard_map/spread/pallas_call | solution.py:667
  (4 shorter events, 0.0 us)
Async XLA Ops:
  0.6 14.7 %copy-start.4 = (s32[28672]{0:T(1024)S(1)}, s32[28672]{0:T(1024)}, u32[]{:S(2)}) copy-start(s32[28672]{0:T(1024)} %param.9) | copy-start | bytes 344068
  0.6 14.8 %collective-permute-start = (s32[16]{0:T(128)}, s32[16]{0:T(128)S(1)}, u32[]{:S(2)}, u32[]{:S(2)}) collective-permute-start(s32[16]{0:T(128)} %bitcast.16), channel_id=1, source_target_pairs={{0,1},{1,0},{2,3},{3,2},{4,5},{5,4},{6,7},{7,6},{8,9},{9,8},{10,11... | collective-permute-start | bytes 200 | tf_op jit(solution)/shard_map/ppermute | solution.py:594
  0.7 14.7 %copy-start.5 = (s32[1,16]{1,0:T(1,128)S(1)}, s32[1,16]{1,0:T(1,128)}, u32[]{:S(2)}) copy-start(s32[1,16]{1,0:T(1,128)} %param.13) | copy-start | bytes 196
  0.7 14.9 %copy-start.1 = (s32[3,512]{1,0:T(4,128)S(1)}, s32[3,512]{1,0:T(4,128)}, u32[]{:S(2)}) copy-start(s32[3,512]{1,0:T(4,128)} %cell_ref.1) | copy-start | bytes 18436
  0.8 14.9 %copy-start.2 = (f32[3,512]{1,0:T(4,128)S(1)}, f32[3,512]{1,0:T(4,128)}, u32[]{:S(2)}) copy-start(f32[3,512]{1,0:T(4,128)} %frac_ref.1) | copy-start | bytes 18436
  0.8 14.9 %copy-start.3 = (f32[512]{0:T(512)S(1)}, f32[512]{0:T(512)}, u32[]{:S(2)}) copy-start(f32[512]{0:T(512)} %param.12) | copy-start | bytes 6148
  0.8 25.8 %copy-start = (bf16[1536,384]{1,0:T(8,128)(2,1)S(1)}, bf16[1536,384]{1,0:T(8,128)(2,1)}, u32[]{:S(2)}) copy-start(bf16[1536,384]{1,0:T(8,128)(2,1)} %constant.13.clone.table_ref) | copy-start | bytes 3538948
  4.0 22.5 %all-to-all-start = ((f32[64,8,128]{2,1,0:T(8,128)}), f32[64,8,128]{2,1,0:T(8,128)S(1)}, u32[]{:S(2)}, u32[]{:S(2)}) async-start(f32[64,8,128]{2,1,0:T(8,128)} %columns.1), calls=%async_computation | async-start | bytes 524288 | tf_op jit(solution)/shard_map/all_to_all | solution.py:598
  38.4 1.2 %collective-permute-start.1 = (f32[1,128]{1,0:T(1,128)S(1)}, f32[1,128]{1,0:T(1,128)S(1)}, u32[]{:S(2)}, u32[]{:S(2)}) collective-permute-start(f32[1,128]{1,0:T(1,128)S(1)} %get-tuple-element.25), channel_id=1, source_target_pairs={{0,1},{1,0},{2,3},{3,2},{4,5},{5,4},{6,7},{7,6},{8,9},{9,8},{10,11... | collective-permute-start | bytes 1544 | tf_op jit(solution)/shard_map/ppermute | solution.py:663

commit v13 on v12

--- a/solution.py
+++ b/solution.py
@@ -155,33 +155,7 @@
     return s * num / den
 
 
-def place(last_ref, slope_ref, q):
-    return (last_ref, q - LAST[0]) if q in LAST else (slope_ref, q - 2 * (q // 16))
-
-
-def charges_kernel(
-    list_ref,
-    cell_ref,
-    frac_ref,
-    charge_ref,
-    grid_ref,
-    pot_ref,
-    last_ref,
-    slope_out,
-    offb_ref,
-    offc_ref,
-    col_ref,
-    gb_ref,
-    gc_ref,
-    owner_ref,
-    plan_s,
-    uab_ref,
-    eab_ref,
-    uc_ref,
-    ec_ref,
-    slope_ref,
-    sems,
-):
+def sort_cells(grid_ref, gb_ref, gc_ref, owner_ref, plan_s):
     cells = grid_ref[...]
     pairs = cells.shape[0] // 2
     row = jnp.floor((cells.astype(f32) + 0.5) * (1.0 / N))
@@ -232,6 +206,34 @@
         for piece in range(4):
             out[piece] = values[:, piece * LANE : (piece + 1) * LANE]
 
+
+def place(last_ref, slope_ref, q):
+    return (last_ref, q - LAST[0]) if q in LAST else (slope_ref, q - 2 * (q // 16))
+
+
+def charges_kernel(
+    list_ref,
+    cell_ref,
+    frac_ref,
+    charge_ref,
+    grid_ref,
+    pot_ref,
+    last_ref,
+    slope_out,
+    offb_ref,
+    offc_ref,
+    col_ref,
+    gb_ref,
+    gc_ref,
+    owner_ref,
+    plan_s,
+    uab_ref,
+    eab_ref,
+    uc_ref,
+    ec_ref,
+    slope_ref,
+    sems,
+):
     listed = list_ref[...]
     mask = lax.broadcasted_iota(i32, (32, cell_ref.shape[1]), 1) == listed
     center = cell_ref[...].astype(f32) + frac_ref[...]
@@ -347,6 +349,8 @@
                     )
                     copy.start()
                     copies.append(copy)
+        if a == 0:
+            sort_cells(grid_ref, gb_ref, gc_ref, owner_ref, plan_s)
     for copy in copies:
         copy.wait()
 

time: 56.4 us -> 56.6 us (level)
  Pallas kernels: 22 us -> 22.8 us
  waiting for transfers between devices: 6.23 us -> 5.47 us
    all_to_all x1, waiting for transfers between devices: 5.08 us -> 4.31 us  [local(): recv = lax.all_to_all(sent, 'pw', 0, 0, tiled=True)]
    pallas_call x1, Pallas kernels: 5.8 us -> 6.57 us  [local(): pl.pallas_call(charges_kernel, out_shape=(jax.ShapeDtypeStruct((N, N), f3...]
  transfers between devices with their start and end apart: 3 -> 3, of which waited for: 2 -> 2; matrix products, arithmetic and copies ran while one was open for 0% -> 0% of each run, Pallas kernels for 16% -> 17%
where the time goes in v13:
time: 56.6 us; the launch traced here: 56.4 us
  Pallas kernels  22.8 us (40%)
  blocking collectives  15.6 us (28%)
  starting transfers between devices  11.5 us (20%)
  waiting for transfers between devices  5.47 us (10%)
  between operations  0.79 us (1%)
    all_to_all x1, blocking collectives, local(): lax.all_to_all(jnp.broadcast_to(push[None], (sources, 1, LANE)), 'pw', 0,...  15.6 us
    pallas_call x1, Pallas kernels, local(): pl.pallas_call(grid_kernel, out_shape=(jax.ShapeDtypeStruct((2, N, N), f3...  11.8 us
    all_to_all x1, starting transfers between devices, local(): recv = lax.all_to_all(sent, 'pw', 0, 0, tiled=True)  11.3 us
    pallas_call x1, Pallas kernels, local(): pl.pallas_call(charges_kernel, out_shape=(jax.ShapeDtypeStruct((N, N), f3...  6.57 us
    all_to_all x1, waiting for transfers between devices, local(): recv = lax.all_to_all(sent, 'pw', 0, 0, tiled=True)  4.31 us
    pallas_call x1, Pallas kernels, local(): pl.pallas_call(columns_kernel, out_shape=jax.ShapeDtypeStruct((planes, 8,...  3.26 us
    ppermute x1, waiting for transfers between devices, local(): push = push + lax.ppermute(push, 'mm', [(0, 1), (1, 0)])  1.15 us
    pallas_call x1, Pallas kernels, local(): pl.pallas_call(spread_kernel, out_shape=jax.ShapeDtypeStruct((3, charge.s...  1.15 us
  transfers between devices with their start and end apart: 3, of which 2 were waited for; matrix products, arithmetic and copies ran while one was open for 0% of the time, Pallas kernels for 17%

profile of v13, /device:TPU:0, one launch (start us, length us, event | category | flops | bytes accessed | tf_op | source)
XLA Modules:
  0.0 56.4 jit_solution(1153204372282210060)
XLA Ops:
  0.6 0.0 copy-start.4
  0.6 0.1 collective-permute-start
  0.7 0.0 copy-start.5
  0.7 0.0 copy-start.1
  0.8 0.0 copy-start.2
  0.8 0.0 copy-start.3
  0.8 0.0 copy-start
  0.8 3.3 %columns.1 = f32[64,8,128]{2,1,0:T(8,128)} custom-call(f32[2,448,384]{2,1,0:T(8,128)} %bitcast.15, bf16[256,768]{1,0:T(8,128)(2,1)} %constant.12.clone.table_in), custom_call_target="tpu_custom_call" | custom-call | tf_op jit(solution)/shard_map/columns/pallas_call | solution.py:582
  4.0 11.3 %all-to-all-start = ((f32[64,8,128]{2,1,0:T(8,128)}), f32[64,8,128]{2,1,0:T(8,128)S(1)}, u32[]{:S(2)}, u32[]{:S(2)}) async-start(f32[64,8,128]{2,1,0:T(8,128)} %columns.1), calls=%async_computation | async-start | bytes 524288 | tf_op jit(solution)/shard_map/all_to_all | solution.py:602
  15.3 0.0 copy-done.4
  15.4 0.1 reshape.16
  15.5 0.0 collective-permute-done
  15.5 0.0 copy-done.5
  15.5 0.1 add_bitcast_fusion
  15.6 0.1 copy.12.list_ref
  15.7 0.0 copy-done.1
  15.7 0.0 copy-done.2
  15.7 0.0 copy-done.3
  15.7 6.6 %charges.1 = (f32[384,384]{1,0:T(8,128)S(1)}, f32[2,192,384]{2,1,0:T(8,128)S(1)}, f32[30,192,384]{2,1,0:T(8,128)}, f32[384,128]{1,0:T(8,128)S(1)}, f32[32,384]{1...) custom-call(s32[32,1]{1,0:T(8,128)S(1)} %copy.12.list_ref, ...), custom_call_target="tpu_custom_call" | custom-call | tf_op jit(solution)/shard_map/charges/pallas_call | solution.py:607
  22.3 4.3 %all-to-all-done.recv_ref = f32[64,8,128]{2,1,0:T(8,128)S(1)} async-done(((f32[64,8,128]{2,1,0:T(8,128)}), f32[64,8,128]{2,1,0:T(8,128)S(1)}, u32[]{:S(2)}, u32[]{:S(2)}) %all-to-all-start) | async-done | bytes 262176 | tf_op jit(solution)/shard_map/all_to_all | solution.py:602
  26.6 0.0 copy-done
  26.6 11.8 %grid.1 = (f32[2,384,384]{2,1,0:T(8,128)}, f32[1,128]{1,0:T(1,128)S(1)}) custom-call(s32[16]{0:T(128)S(1)} %get-tuple-element.14.plan_s, f32[64,8,128]{2,1,0:T(8,128)S(1)} %all-to-all-done.recv_ref, f32[32,8,128]{2,1,0:T(8,128)S(1)} %get-tuple-element.15.owner_ref, f32[4,32,128]{2,1,0:T(8,128)S(1)} %get-tuple-element.16.gb_ref, ...), custom_call_target="tpu_custom_call" | custom-call | tf_op jit(solution)/shard_map/grid/pallas_call | solution.py:641
  38.4 0.1 collective-permute-start.1
  38.5 1.1 %collective-permute-done.1 = f32[1,128]{1,0:T(1,128)S(1)} collective-permute-done((f32[1,128]{1,0:T(1,128)S(1)}, f32[1,128]{1,0:T(1,128)S(1)}, u32[]{:S(2)}, u32[]{:S(2)}) %collective-permute-start.1) | collective-permute-done | bytes 544 | tf_op jit(solution)/shard_map/ppermute | solution.py:667
  39.7 15.6 %all_to_all.10 = f32[64,1,128]{2,1,0:T(1,128)S(1)} all-to-all(f32[64,1,128]{2,1,0:T(1,128)S(1)} %broadcast_in_dim.21), channel_id=1, replica_groups=mesh['pw'=64,'mm'=2] {'pw'}, dimensions={0} | all-to-all | bytes 65536 | tf_op jit(solution)/shard_map/all_to_all | solution.py:668
  55.3 1.1 %spread.1 = f32[3,512]{1,0:T(4,128)} custom-call(f32[64,128]{1,0:T(8,128)S(1)} %bitcast.13), custom_call_target="tpu_custom_call" | custom-call | tf_op jit(solution)/shard_map/spread/pallas_call | solution.py:671
  (4 shorter events, 0.0 us)
Async XLA Ops:
  0.6 14.7 %copy-start.4 = (s32[28672]{0:T(1024)S(1)}, s32[28672]{0:T(1024)}, u32[]{:S(2)}) copy-start(s32[28672]{0:T(1024)} %param.9) | copy-start | bytes 344068
  0.6 14.8 %collective-permute-start = (s32[16]{0:T(128)}, s32[16]{0:T(128)S(1)}, u32[]{:S(2)}, u32[]{:S(2)}) collective-permute-start(s32[16]{0:T(128)} %bitcast.16), channel_id=1, source_target_pairs={{0,1},{1,0},{2,3},{3,2},{4,5},{5,4},{6,7},{7,6},{8,9},{9,8},{10,11... | collective-permute-start | bytes 200 | tf_op jit(solution)/shard_map/ppermute | solution.py:598
  0.7 14.7 %copy-start.5 = (s32[1,16]{1,0:T(1,128)S(1)}, s32[1,16]{1,0:T(1,128)}, u32[]{:S(2)}) copy-start(s32[1,16]{1,0:T(1,128)} %param.13) | copy-start | bytes 196
  0.7 14.9 %copy-start.1 = (s32[3,512]{1,0:T(4,128)S(1)}, s32[3,512]{1,0:T(4,128)}, u32[]{:S(2)}) copy-start(s32[3,512]{1,0:T(4,128)} %cell_ref.1) | copy-start | bytes 18436
  0.8 14.9 %copy-start.2 = (f32[3,512]{1,0:T(4,128)S(1)}, f32[3,512]{1,0:T(4,128)}, u32[]{:S(2)}) copy-start(f32[3,512]{1,0:T(4,128)} %frac_ref.1) | copy-start | bytes 18436
  0.8 14.9 %copy-start.3 = (f32[512]{0:T(512)S(1)}, f32[512]{0:T(512)}, u32[]{:S(2)}) copy-start(f32[512]{0:T(512)} %param.12) | copy-start | bytes 6148
  0.8 25.8 %copy-start = (bf16[1536,384]{1,0:T(8,128)(2,1)S(1)}, bf16[1536,384]{1,0:T(8,128)(2,1)}, u32[]{:S(2)}) copy-start(bf16[1536,384]{1,0:T(8,128)(2,1)} %constant.13.clone.table_ref) | copy-start | bytes 3538948
  4.0 22.5 %all-to-all-start = ((f32[64,8,128]{2,1,0:T(8,128)}), f32[64,8,128]{2,1,0:T(8,128)S(1)}, u32[]{:S(2)}, u32[]{:S(2)}) async-start(f32[64,8,128]{2,1,0:T(8,128)} %columns.1), calls=%async_computation | async-start | bytes 524288 | tf_op jit(solution)/shard_map/all_to_all | solution.py:602
  38.4 1.2 %collective-permute-start.1 = (f32[1,128]{1,0:T(1,128)S(1)}, f32[1,128]{1,0:T(1,128)S(1)}, u32[]{:S(2)}, u32[]{:S(2)}) collective-permute-start(f32[1,128]{1,0:T(1,128)S(1)} %get-tuple-element.25), channel_id=1, source_target_pairs={{0,1},{1,0},{2,3},{3,2},{4,5},{5,4},{6,7},{7,6},{8,9},{9,8},{10,11... | collective-permute-start | bytes 1544 | tf_op jit(solution)/shard_map/ppermute | solution.py:667
